TPU v7x, 32 devices: a whole 2x2x4 slice. The times are simulated.
32 devices in a mesh: dp: 8 (over z, y), fsdp: 4 (over x, core).
Axes of the slice: x: 2, y: 2, z: 4, core: 2. Of those that a mesh axis runs over, the one named last changes fastest.
Arguments:
- tokens: bfloat16 [8192, 1024], P(('dp', 'fsdp')), may hold values from -6 to 6
- lengths: int32 [8, 6], P('dp'), may hold values from 0 to 1024, as said below
- visibility_mask: int32 [8192], P(('dp', 'fsdp')), may hold values from 0 to 1, as said below
- visible_counts: int32 [8, 4], P('dp', 'fsdp'), may hold values from 0 to 256, as said below
- ln1_gain: float32 [1024], P(('dp', 'fsdp')), may hold values from 0.5 to 1.5
- ln1_bias: float32 [1024], P(('dp', 'fsdp')), may hold values from -1.25 to 1.25
- qkv_weight: float32 [1024, 3072], P(('dp', 'fsdp')), may hold values from -0.1875 to 0.1875
- qkv_bias: float32 [3072], P(('dp', 'fsdp')), may hold values from -1.25 to 1.25
- out_weight: float32 [1024, 1024], P(('dp', 'fsdp')), may hold values from -1.5 to 1.5
- out_bias: float32 [1024], P(('dp', 'fsdp')), may hold values from -1.25 to 1.25
- ln2_gain: float32 [1024], P(('dp', 'fsdp')), may hold values from 0.5 to 1.5
- ln2_bias: float32 [1024], P(('dp', 'fsdp')), may hold values from -1.25 to 1.25
- fc1_weight: float32 [1024, 4096], P(('dp', 'fsdp')), may hold values from -0.1875 to 0.1875
- fc1_bias: float32 [4096], P(('dp', 'fsdp')), may hold values from -1.25 to 1.25
- fc2_weight: float32 [4096, 1024], P(('dp', 'fsdp')), may hold values from -0.09375 to 0.09375
- fc2_bias: float32 [1024], P(('dp', 'fsdp')), may hold values from -1.25 to 1.25
- context_cot: bfloat16 [8192, 1024], P(('dp', 'fsdp')), may hold values from -12 to 12
Outputs:
- target_out: bfloat16 [8192, 1024], P(('dp', 'fsdp'))
- context_out: bfloat16 [8192, 1024], P(('dp', 'fsdp'))
- tokens_grad: bfloat16 [8192, 1024], P(('dp', 'fsdp'))
- ln1_gain_grad: float32 [1024], P(('dp', 'fsdp'))
- ln1_bias_grad: float32 [1024], P(('dp', 'fsdp'))
- qkv_weight_grad: float32 [1024, 3072], P(('dp', 'fsdp'))
- qkv_bias_grad: float32 [3072], P(('dp', 'fsdp'))
- out_weight_grad: float32 [1024, 1024], P(('dp', 'fsdp'))
- out_bias_grad: float32 [1024], P(('dp', 'fsdp'))
- ln2_gain_grad: float32 [1024], P(('dp', 'fsdp'))
- ln2_bias_grad: float32 [1024], P(('dp', 'fsdp'))
- fc1_weight_grad: float32 [1024, 4096], P(('dp', 'fsdp'))
- fc1_bias_grad: float32 [4096], P(('dp', 'fsdp'))
- fc2_weight_grad: float32 [4096, 1024], P(('dp', 'fsdp'))
- fc2_bias_grad: float32 [1024], P(('dp', 'fsdp'))
Inputs may be any that keep to these rules, and one draw needn't show every extreme that they name: Each pack's lengths sum to 1024: either images of 196 tokens, or one video of 1024 tokens followed by images of 196 tokens; in both, the last image is shorter if the rest is no multiple of 196. At least one pack holds a video. `visibility_mask`: each pack holds exactly 256 ones. `visible_counts`: each entry is the number of ones of visibility_mask among the 256 tokens of that device.
All inputs are finite; a program needn't handle non-finite values.
Results may differ from a plain program's by a relative error of at most 0.014.
Values may be sent and summed in bfloat16 or wider, within the bound.
A program may use at most 256 MiB of HBM per device.

v0:
```python
import math

import jax
import jax.numpy as jnp
from jax import lax
from jax.sharding import PartitionSpec as P

HEADS = 16
HDIM = 64
GRID = 14
VIS_DEV = 64


norm_eps = 1e-06
masked_fill = -1e30


def layer_norm(inputs, scale_vec, shift_vec):
    center = inputs - jnp.mean(inputs, axis=-1, keepdims=True)
    spread = jnp.mean(center * center, axis=-1, keepdims=True)
    return center * lax.rsqrt(spread + norm_eps) * scale_vec + shift_vec


def gelu_erf(values):
    return jax.nn.gelu(values, approximate=False)


def pack_layout(seq_lens, pack_len):
    seq_ends = jnp.cumsum(seq_lens)
    places = jnp.arange(pack_len, dtype=jnp.int32)
    passed = places[:, None] >= seq_ends[None, :]
    segment = jnp.sum(passed.astype(jnp.int32), axis=1)
    before = jnp.sum(jnp.where(passed, seq_lens[None, :], 0), axis=1)
    return (segment, places - before)


def rope_tables(places):
    frame_index = (places // (GRID * GRID)).astype(jnp.float32)
    grid_row = (places // GRID % GRID).astype(jnp.float32)
    grid_col = (places % GRID).astype(jnp.float32)
    pair_index = jnp.arange(HDIM // 2, dtype=jnp.int32)
    axis_pick = jnp.minimum(pair_index // 11, 2)
    pair_order = (pair_index - 11 * axis_pick).astype(jnp.float32)
    frequency = jnp.exp(pair_order * (-math.log(10000.0) / 11.0))
    angles = (
        frame_index[:, None] * (axis_pick == 0).astype(jnp.float32)[None, :]
        + grid_row[:, None] * (axis_pick == 1).astype(jnp.float32)[None, :]
        + grid_col[:, None] * (axis_pick == 2).astype(jnp.float32)[None, :]
    ) * frequency[None, :]
    return (jnp.cos(angles), jnp.sin(angles))


def rotate(heads, cosine_table, sine_table):
    half_size = heads.shape[-1] // 2
    first_half = heads[..., :half_size]
    second_half = heads[..., half_size:]
    cosine_cols = cosine_table[:, None, :]
    sine_cols = sine_table[:, None, :]
    return jnp.concatenate(
        [
            first_half * cosine_cols - second_half * sine_cols,
            second_half * cosine_cols + first_half * sine_cols,
        ],
        axis=-1,
    )


def rotate_back(grads, cosine_table, sine_table):
    half_size = grads.shape[-1] // 2
    first_half = grads[..., :half_size]
    second_half = grads[..., half_size:]
    cosine_cols = cosine_table[:, None, :]
    sine_cols = sine_table[:, None, :]
    return jnp.concatenate(
        [
            first_half * cosine_cols + second_half * sine_cols,
            second_half * cosine_cols - first_half * sine_cols,
        ],
        axis=-1,
    )


def project(token_rows, weights, cosine_table, sine_table):
    inputs = token_rows.astype(jnp.float32)
    row_count = inputs.shape[0]
    model_width = inputs.shape[1]
    normed = layer_norm(
        inputs, weights[0].astype(jnp.float32), weights[1].astype(jnp.float32)
    ).astype(jnp.bfloat16)
    joined = jnp.dot(normed, weights[2], preferred_element_type=jnp.float32) + weights[3].astype(
        jnp.float32
    )
    query_heads = rotate(
        joined[:, :model_width].reshape(row_count, HEADS, HDIM), cosine_table, sine_table
    ).astype(jnp.bfloat16)
    key_flat = (
        rotate(
            joined[:, model_width : 2 * model_width].reshape(row_count, HEADS, HDIM),
            cosine_table,
            sine_table,
        )
        .astype(jnp.bfloat16)
        .reshape(row_count, model_width)
    )
    value_flat = joined[:, 2 * model_width :].astype(jnp.bfloat16)
    return (inputs, normed, query_heads, key_flat, value_flat)


def attend(query_heads, key_flat, value_flat, seg_query, seg_key):
    key_heads = key_flat.reshape(key_flat.shape[0], HEADS, HDIM)
    value_heads = value_flat.reshape(value_flat.shape[0], HEADS, HDIM)
    scores = jnp.einsum(
        "qhd,khd->hqk", query_heads, key_heads, preferred_element_type=jnp.float32
    ) * HDIM ** (-0.5)
    allowed = seg_query[:, None] == seg_key[None, :]
    masked = jnp.where(allowed[None], scores, masked_fill)
    row_max = jnp.max(masked, axis=-1, keepdims=True)
    raised = jnp.exp(masked - row_max)
    totals = jnp.sum(raised, axis=-1, keepdims=True)
    attn_probs = (raised / totals).astype(jnp.bfloat16)
    attended = jnp.einsum(
        "hqk,khd->qhd", attn_probs, value_heads, preferred_element_type=jnp.float32
    )
    return (
        attended.reshape(query_heads.shape[0], -1).astype(jnp.bfloat16),
        row_max + jnp.log(totals),
    )


def attend_back(query_heads, key_flat, value_flat, seg_query, seg_key, log_total, grad_att):
    key_heads = key_flat.reshape(key_flat.shape[0], HEADS, HDIM)
    value_heads = value_flat.reshape(value_flat.shape[0], HEADS, HDIM)
    scale_factor = HDIM ** (-0.5)
    scores = (
        jnp.einsum("qhd,khd->hqk", query_heads, key_heads, preferred_element_type=jnp.float32)
        * scale_factor
    )
    allowed = seg_query[:, None] == seg_key[None, :]
    masked = jnp.where(allowed[None], scores, masked_fill)
    attn_probs = jnp.exp(masked - log_total)
    grad_heads = grad_att.reshape(grad_att.shape[0], HEADS, HDIM)
    grad_probs = jnp.einsum(
        "qhd,khd->hqk", grad_heads, value_heads, preferred_element_type=jnp.float32
    )
    row_delta = jnp.sum(attn_probs * grad_probs, axis=-1, keepdims=True)
    grad_scores = (attn_probs * (grad_probs - row_delta)).astype(jnp.bfloat16)
    grad_query = (
        jnp.einsum("hqk,khd->qhd", grad_scores, key_heads, preferred_element_type=jnp.float32)
        * scale_factor
    )
    grad_key = (
        jnp.einsum("hqk,qhd->khd", grad_scores, query_heads, preferred_element_type=jnp.float32)
        * scale_factor
    )
    grad_value = jnp.einsum(
        "hqk,qhd->khd",
        attn_probs.astype(jnp.bfloat16),
        grad_heads,
        preferred_element_type=jnp.float32,
    )
    return (
        grad_query,
        grad_key.reshape(key_flat.shape[0], -1),
        grad_value.reshape(value_flat.shape[0], -1),
    )


def finish(inputs, attended, weights):
    middle = inputs + (
        jnp.dot(attended, weights[4], preferred_element_type=jnp.float32)
        + weights[5].astype(jnp.float32)
    )
    second = layer_norm(
        middle, weights[6].astype(jnp.float32), weights[7].astype(jnp.float32)
    ).astype(jnp.bfloat16)
    hidden = jnp.dot(second, weights[8], preferred_element_type=jnp.float32) + weights[9].astype(
        jnp.float32
    )
    activated = gelu_erf(hidden).astype(jnp.bfloat16)
    result = middle + (
        jnp.dot(activated, weights[10], preferred_element_type=jnp.float32)
        + weights[11].astype(jnp.float32)
    )
    return (result, middle, second, hidden, activated)


def on_device(
    tokens,
    lengths,
    visibility_mask,
    visible_counts,
    ln1_gain,
    ln1_bias,
    qkv_weight,
    qkv_bias,
    out_weight,
    out_bias,
    ln2_gain,
    ln2_bias,
    fc1_weight,
    fc1_bias,
    fc2_weight,
    fc2_bias,
    context_cot,
):
    tok_rows = tokens.shape[0]
    model_width = tokens.shape[1]
    groups = lax.axis_size("fsdp")
    member = lax.axis_index("fsdp")
    pack_len = tok_rows * groups
    vis_rows = VIS_DEV
    vis_pack = vis_rows * groups
    zero_low = jnp.zeros((), jnp.bfloat16)
    shards = [
        weight.astype(jnp.bfloat16)
        for weight in (
            ln1_gain,
            ln1_bias,
            qkv_weight,
            qkv_bias,
            out_weight,
            out_bias,
            ln2_gain,
            ln2_bias,
            fc1_weight,
            fc1_bias,
            fc2_weight,
            fc2_bias,
        )
    ]
    weights = (
        lax.all_gather(shards[0], ("dp", "fsdp"), axis=0, tiled=True),
        lax.all_gather(shards[1], ("dp", "fsdp"), axis=0, tiled=True),
        lax.all_gather(shards[2], ("dp", "fsdp"), axis=0, tiled=True),
        lax.all_gather(shards[3], ("dp", "fsdp"), axis=0, tiled=True),
        lax.all_gather(shards[4], ("dp", "fsdp"), axis=0, tiled=True),
        lax.all_gather(shards[5], ("dp", "fsdp"), axis=0, tiled=True),
        lax.all_gather(shards[6], ("dp", "fsdp"), axis=0, tiled=True),
        lax.all_gather(shards[7], ("dp", "fsdp"), axis=0, tiled=True),
        lax.all_gather(shards[8], ("dp", "fsdp"), axis=0, tiled=True),
        lax.all_gather(shards[9], ("dp", "fsdp"), axis=0, tiled=True),
        lax.all_gather(shards[10], ("dp", "fsdp"), axis=0, tiled=True),
        lax.all_gather(shards[11], ("dp", "fsdp"), axis=0, tiled=True),
    )
    segment, places = pack_layout(lengths[0], pack_len)
    home_rows = member * tok_rows + jnp.arange(tok_rows, dtype=jnp.int32)
    seg_home = jnp.take(segment, home_rows)
    cos_home, sin_home = rope_tables(jnp.take(places, home_rows))
    inputs, normed, query_heads, key_flat, value_flat = project(tokens, weights, cos_home, sin_home)
    key_pack, value_pack = (
        lax.all_gather(key_flat, "fsdp", axis=0, tiled=True),
        lax.all_gather(value_flat, "fsdp", axis=0, tiled=True),
    )
    attended = attend(query_heads, key_pack, value_pack, seg_home, segment)[0]
    target_out = finish(inputs, attended, weights)[0].astype(jnp.bfloat16)
    running = jnp.cumsum(visibility_mask)
    visible_here = visibility_mask * (running <= visible_counts[0, 0]).astype(jnp.int32)
    visible_all = lax.all_gather(visible_here, "fsdp", axis=0, tiled=True)
    inclusive = jnp.cumsum(visible_all)
    rank_index = jnp.arange(vis_pack, dtype=jnp.int32)
    row_of = jnp.sum((inclusive[None, :] <= rank_index[:, None]).astype(jnp.int32), axis=1)
    owner_dev = row_of // tok_rows
    local_row = row_of % tok_rows
    mine_here = (owner_dev == member)[:, None]
    send_tokens = jnp.where(mine_here, jnp.take(tokens, local_row, axis=0), zero_low)
    send_cot = jnp.where(mine_here, jnp.take(context_cot, local_row, axis=0), zero_low)
    recv_tokens, recv_cot = (
        lax.all_to_all(send_tokens, "fsdp", split_axis=0, concat_axis=0, tiled=True),
        lax.all_to_all(send_cot, "fsdp", split_axis=0, concat_axis=0, tiled=True),
    )
    slot_index = jnp.arange(vis_rows, dtype=jnp.int32)
    my_ranks = member * vis_rows + slot_index
    my_owner = jnp.take(owner_dev, my_ranks)
    my_row = jnp.take(row_of, my_ranks)
    picked = my_owner * vis_rows + slot_index
    bal_tokens = jnp.take(recv_tokens, picked, axis=0)
    bal_cot = jnp.take(recv_cot, picked, axis=0)
    seg_bal = jnp.take(segment, my_row)
    seg_keys = jnp.take(segment, row_of)
    cos_bal, sin_bal = rope_tables(jnp.take(places, my_row))
    inputs_bal, normed_bal, query_bal, key_bal, value_bal = project(
        bal_tokens, weights, cos_bal, sin_bal
    )
    key_vis, value_vis = (
        lax.all_gather(key_bal, "fsdp", axis=0, tiled=True),
        lax.all_gather(value_bal, "fsdp", axis=0, tiled=True),
    )
    attended_bal, log_total = attend(query_bal, key_vis, value_vis, seg_bal, seg_keys)
    result_bal, middle_bal, second_bal, hidden_bal, activated_bal = finish(
        inputs_bal, attended_bal, weights
    )
    grad_result = bal_cot.astype(jnp.float32)
    result_low = grad_result.astype(jnp.bfloat16)
    grad_fc2 = jnp.einsum(
        "nf,nd->fd", activated_bal, result_low, preferred_element_type=jnp.float32
    )
    grad_bfc2 = jnp.sum(result_low.astype(jnp.float32), axis=0)
    grad_activated = jnp.einsum(
        "nd,fd->nf", result_low, weights[10], preferred_element_type=jnp.float32
    )
    gelu_pull = jax.vjp(gelu_erf, hidden_bal)[1]
    hidden_low = gelu_pull(grad_activated)[0].astype(jnp.bfloat16)
    grad_fc1 = jnp.einsum("nd,nf->df", second_bal, hidden_low, preferred_element_type=jnp.float32)
    grad_bfc1 = jnp.sum(hidden_low.astype(jnp.float32), axis=0)
    grad_second = jnp.einsum(
        "nf,df->nd", hidden_low, weights[8], preferred_element_type=jnp.float32
    )
    norm_two_pull = jax.vjp(
        layer_norm, middle_bal, weights[6].astype(jnp.float32), weights[7].astype(jnp.float32)
    )[1]
    grad_mid_norm, grad_gain_two, grad_shift_two = norm_two_pull(grad_second)
    grad_middle = grad_result + grad_mid_norm
    middle_low = grad_middle.astype(jnp.bfloat16)
    grad_wout = jnp.einsum(
        "nd,ne->de", attended_bal, middle_low, preferred_element_type=jnp.float32
    )
    grad_bout = jnp.sum(middle_low.astype(jnp.float32), axis=0)
    grad_att = jnp.einsum(
        "ne,de->nd", middle_low, weights[4], preferred_element_type=jnp.float32
    ).astype(jnp.bfloat16)
    grad_query, grad_key_all, grad_value_all = attend_back(
        query_bal, key_vis, value_vis, seg_bal, seg_keys, log_total, grad_att
    )
    grad_key_own, grad_value_own = (
        lax.psum_scatter(
            grad_key_all.astype(jnp.bfloat16), "fsdp", scatter_dimension=0, tiled=True
        ).astype(jnp.float32),
        lax.psum_scatter(
            grad_value_all.astype(jnp.bfloat16), "fsdp", scatter_dimension=0, tiled=True
        ).astype(jnp.float32),
    )
    grad_query_pre = rotate_back(grad_query, cos_bal, sin_bal).reshape(vis_rows, model_width)
    grad_key_pre = rotate_back(
        grad_key_own.reshape(vis_rows, HEADS, HDIM), cos_bal, sin_bal
    ).reshape(vis_rows, model_width)
    joined_low = jnp.concatenate([grad_query_pre, grad_key_pre, grad_value_own], axis=1).astype(
        jnp.bfloat16
    )
    grad_wqkv = jnp.einsum("nd,ne->de", normed_bal, joined_low, preferred_element_type=jnp.float32)
    grad_bqkv = jnp.sum(joined_low.astype(jnp.float32), axis=0)
    grad_normed = jnp.einsum(
        "ne,de->nd", joined_low, weights[2], preferred_element_type=jnp.float32
    )
    norm_one_pull = jax.vjp(
        layer_norm, inputs_bal, weights[0].astype(jnp.float32), weights[1].astype(jnp.float32)
    )[1]
    grad_in_norm, grad_gain_one, grad_shift_one = norm_one_pull(grad_normed)
    grad_inputs = grad_middle + grad_in_norm
    destinations = jnp.arange(groups, dtype=jnp.int32)
    route_mask = (my_owner[None, :] == destinations[:, None])[:, :, None]
    send_out = jnp.where(route_mask, result_bal.astype(jnp.bfloat16)[None], zero_low).reshape(
        vis_pack, model_width
    )
    send_grad = jnp.where(route_mask, grad_inputs.astype(jnp.bfloat16)[None], zero_low).reshape(
        vis_pack, model_width
    )
    back_out, back_grad = (
        lax.all_to_all(send_out, "fsdp", split_axis=0, concat_axis=0, tiled=True),
        lax.all_to_all(send_grad, "fsdp", split_axis=0, concat_axis=0, tiled=True),
    )
    rank_home = jnp.maximum(jnp.take(inclusive, home_rows) - 1, 0)
    is_visible = (visible_here > 0)[:, None]
    context_out = jnp.where(is_visible, jnp.take(back_out, rank_home, axis=0), zero_low)
    tokens_grad = jnp.where(is_visible, jnp.take(back_grad, rank_home, axis=0), zero_low)
    grad_list = [
        grad_gain_one,
        grad_shift_one,
        grad_wqkv,
        grad_bqkv,
        grad_wout,
        grad_bout,
        grad_gain_two,
        grad_shift_two,
        grad_fc1,
        grad_bfc1,
        grad_fc2,
        grad_bfc2,
    ]
    reduced = (
        lax.psum_scatter(grad_list[0], ("dp", "fsdp"), scatter_dimension=0, tiled=True),
        lax.psum_scatter(grad_list[1], ("dp", "fsdp"), scatter_dimension=0, tiled=True),
        lax.psum_scatter(grad_list[2], ("dp", "fsdp"), scatter_dimension=0, tiled=True),
        lax.psum_scatter(grad_list[3], ("dp", "fsdp"), scatter_dimension=0, tiled=True),
        lax.psum_scatter(grad_list[4], ("dp", "fsdp"), scatter_dimension=0, tiled=True),
        lax.psum_scatter(grad_list[5], ("dp", "fsdp"), scatter_dimension=0, tiled=True),
        lax.psum_scatter(grad_list[6], ("dp", "fsdp"), scatter_dimension=0, tiled=True),
        lax.psum_scatter(grad_list[7], ("dp", "fsdp"), scatter_dimension=0, tiled=True),
        lax.psum_scatter(grad_list[8], ("dp", "fsdp"), scatter_dimension=0, tiled=True),
        lax.psum_scatter(grad_list[9], ("dp", "fsdp"), scatter_dimension=0, tiled=True),
        lax.psum_scatter(grad_list[10], ("dp", "fsdp"), scatter_dimension=0, tiled=True),
        lax.psum_scatter(grad_list[11], ("dp", "fsdp"), scatter_dimension=0, tiled=True),
    )
    return (
        target_out,
        context_out,
        tokens_grad,
        reduced[0],
        reduced[1],
        reduced[2],
        reduced[3],
        reduced[4],
        reduced[5],
        reduced[6],
        reduced[7],
        reduced[8],
        reduced[9],
        reduced[10],
        reduced[11],
    )


def solution(mesh):
    return jax.shard_map(
        on_device,
        mesh=mesh,
        in_specs=(
            P(("dp", "fsdp"), None),
            P("dp", None),
            P(("dp", "fsdp")),
            P("dp", "fsdp"),
            P(("dp", "fsdp")),
            P(("dp", "fsdp")),
            P(("dp", "fsdp"), None),
            P(("dp", "fsdp")),
            P(("dp", "fsdp"), None),
            P(("dp", "fsdp")),
            P(("dp", "fsdp")),
            P(("dp", "fsdp")),
            P(("dp", "fsdp"), None),
            P(("dp", "fsdp")),
            P(("dp", "fsdp"), None),
            P(("dp", "fsdp")),
            P(("dp", "fsdp"), None),
        ),
        out_specs=(
            P(("dp", "fsdp"), None),
            P(("dp", "fsdp"), None),
            P(("dp", "fsdp"), None),
            P(("dp", "fsdp")),
            P(("dp", "fsdp")),
            P(("dp", "fsdp"), None),
            P(("dp", "fsdp")),
            P(("dp", "fsdp"), None),
            P(("dp", "fsdp")),
            P(("dp", "fsdp")),
            P(("dp", "fsdp")),
            P(("dp", "fsdp"), None),
            P(("dp", "fsdp")),
            P(("dp", "fsdp"), None),
            P(("dp", "fsdp")),
        ),
        check_vma=False,
    )
```

profile of v0, /device:TPU:0, one launch (start us, length us, event | category | flops | bytes accessed | tf_op | source)
XLA Modules:
  0.0 1098.9 jit_solution(1709478240370104122)
XLA Ops:
  7.3 1.8 convert_element_type.262
  10.7 1.8 convert_element_type.286
  12.6 1.8 convert_element_type.290
  17.5 6.0 all-gather.1
  28.5 3.5 all-to-all-start
  36.8 42.5 %all-reduce.16 = (bf16[3072]{0:T(1024)(128)(2,1)S(1)}, bf16[1024]{0:T(1024)(128)(2,1)S(1)}, bf16[1024]{0:T(1024)(128)(2,1)S(1)}, bf16[1024]{0:T(1024)(128)(2,1)S...) all-reduce(bf16[3072]{0:T(1024)(128)(2,1)S(1)} %dynamic-update-slic, ...), channel_id=1, replica_groups=mesh['dp'=8,'fsdp'=4] {'dp','fsdp'}, use_global_device_ids=true, to_apply=%add.2 | all-reduce | flops 9216 | bytes 36864
  79.3 41.1 %all-gather = bf16[32,1,128]{2,1,0:T(2,128)(2,1)S(1)} all-gather(bf16[1,1,128]{2,1,0:T(2,128)(2,1)S(1)} %convert_bitcast_fusion), channel_id=1, replica_groups=mesh['dp'=8,'fsdp'=4] {'dp','fsdp'}, dimensions={0}, use_global_device_ids=true | all-gather | bytes 8448 | tf_op jit(solution)/shard_map/all_gather | solution.py:241
  123.8 3.5 all-to-all-start.2
  128.2 11.0 %all-to-all-done.2 = bf16[4,64,1024]{2,1,0:T(8,128)(2,1)S(1)} async-done(((bf16[4,64,1024]{2,1,0:T(8,128)(2,1)}), bf16[4,64,1024]{2,1,0:T(8,128)(2,1)S(1)}, u32[]{:S(2)}, u32[]{:S(2)}) %all-to-all-start.2) | async-done | bytes 524320 | tf_op jit(solution)/shard_map/all_to_all | solution.py:269
  140.4 4.1 convolution_add_fusion.3
  144.5 6.9 all_gather.66
  153.6 8.9 all_gather.67
  164.9 2.3 fusion.181
  167.5 55.8 %all-gather.17.cloned.1.call-done = bf16[1024,4096]{1,0:T(8,128)(2,1)} async-done(((bf16[32,4096]{1,0:T(8,128)(2,1)}), bf16[1024,4096]{1,0:T(8,128)(2,1)}) %all-gather.17.cloned.1.call-update) | async-done | bytes 8388624 | tf_op jit(solution)/shard_map/all_gather | solution.py:240
  223.3 8.4 multiply_convert_fusion.1
  231.7 71.0 %all-gather.19.cloned.1.call-done = bf16[4096,1024]{1,0:T(8,128)(2,1)} async-done(((bf16[128,1024]{1,0:T(8,128)(2,1)}), bf16[4096,1024]{1,0:T(8,128)(2,1)}) %all-gather.19.cloned.1.call-update) | async-done | bytes 8388624 | tf_op jit(solution)/shard_map/all_gather | solution.py:242
  302.7 7.5 convert_reduce_fusion.1
  310.1 3.3 multiply_reduce_fusion.2
  316.1 1.7 multiply_reduce_fusion
  318.1 2.3 fusion.58
  320.3 2.4 copy.123
  323.0 2.1 convolution_convert_fusion
  325.1 2.0 copy.128
  327.6 4.9 convolution_add_fusion.2
  337.5 3.2 fusion.173
  342.2 2.6 copy.109
  344.8 2.4 subtract_convert_fusion.5
  348.0 3.8 fusion.182
  355.3 12.1 %reduce-scatter.9.cloned.1.call-done = bf16[64,1024]{1,0:T(8,128)(2,1)} async-done(((bf16[256,1024]{1,0:T(8,128)(2,1)}), bf16[64,1024]{1,0:T(8,128)(2,1)}) %reduce-scatter.9.cloned.1.call-update) | async-done | bytes 131088 | tf_op jit(solution)/shard_map/reduce_scatter | solution.py:328
  368.3 6.4 fusion.161
  375.8 8.2 fusion.165
  384.2 8.1 fusion.166
  396.1 4.0 copy.107
  400.1 17.1 %all-gather.13.cloned.1.call-done = bf16[1024,1024]{0,1:T(8,128)(2,1)} async-done(((bf16[256,1024]{0,1:T(8,128)(2,1)}), bf16[1024,1024]{0,1:T(8,128)(2,1)}) %all-gather.13.cloned.1.call-update) | async-done | bytes 2097168 | tf_op jit(solution)/shard_map/all_gather | solution.py:251
  417.2 10.6 fusion.178
  427.8 9.3 fusion.62
  437.2 1.7 fusion.179
  438.9 5.1 fusion.68
  444.1 2.1 fusion.168
  447.9 3.5 all-to-all-start.3
  452.9 10.1 all-to-all-done.3
  463.0 3.7 all-to-all-start.1
  466.7 20.3 %fusion.59 = bf16[256,1024]{1,0:T(8,128)(2,1)} fusion(f32[256,1024]{1,0:T(8,128)} %get-tuple-element.112, bf16[4096,1024]{1,0:T(8,128)(2,1)} %all-gather.19.cloned.1.call-done, bf16[1024,4096]{1,0:T(8,128)(2,1)} %all-gather.17.cloned.1.call-done, f32[4096]{0:T(1024)S(1)} %bitcast.101, f32[1024]{0:T(1024)S(1)} %convert_element_type.292, ...), kind=kOutput, calls=%fused_computation.91 | convolution fusion | flops 4366270464 | bytes 18380800 | tf_op jit(solution)/shard_map/dot_general | solution.py:181
  487.2 43.1 %all-reduce.15 = (f32[1024]{0:T(1024)S(1)}, f32[1024]{0:T(1024)S(1)}, f32[3072]{0:T(1024)S(1)}, f32[1024]{0:T(1024)S(1)}, f32[1024]{0:T(1024)S(1)}, /*index=5*/f...) all-reduce(f32[1024]{0:T(1024)S(1)} %get-tuple-element.22, ...), channel_id=4, replica_groups=mesh['dp'=8,'fsdp'=4] {'dp','fsdp'}, use_global_device_ids=true, to_apply=%region_28.34.clone | all-reduce | flops 13312 | bytes 106496
  538.5 23.2 %reduce-scatter.13.cloned.1.call-done = f32[32,1024]{1,0:T(8,128)} async-done(((f32[1024,1024]{1,0:T(8,128)}), f32[32,1024]{1,0:T(8,128)}) %reduce-scatter.13.cloned.1.call-update) | async-done | bytes 131088 | tf_op jit(solution)/shard_map/reduce_scatter | solution.py:384
  561.7 157.7 %reduce-scatter.11.cloned.1.call-done = f32[32,3072]{1,0:T(8,128)} async-done(((f32[1024,3072]{1,0:T(8,128)}), f32[32,3072]{1,0:T(8,128)}) %reduce-scatter.11.cloned.1.call-update) | async-done | bytes 393232 | tf_op jit(solution)/shard_map/reduce_scatter | solution.py:382
  719.5 184.8 %reduce-scatter.15.cloned.1.call-done = f32[32,4096]{1,0:T(8,128)} async-done(((f32[1024,4096]{1,0:T(8,128)}), f32[32,4096]{1,0:T(8,128)}) %reduce-scatter.15.cloned.1.call-update) | async-done | bytes 524304 | tf_op jit(solution)/shard_map/reduce_scatter | solution.py:388
  904.3 187.4 %reduce-scatter.17.cloned.1.call-done = f32[128,1024]{1,0:T(8,128)} async-done(((f32[4096,1024]{1,0:T(8,128)}), f32[128,1024]{1,0:T(8,128)}) %reduce-scatter.17.cloned.1.call-update) | async-done | bytes 524304 | tf_op jit(solution)/shard_map/reduce_scatter | solution.py:390
  (301 shorter events, 55.4 us)
Async XLA Ops:
  7.2 17.7 %copy-start = (bf16[256,1024]{1,0:T(8,128)(2,1)S(1)}, bf16[256,1024]{1,0:T(8,128)(2,1)}, u32[]{:S(2)}) copy-start(bf16[256,1024]{1,0:T(8,128)(2,1)} %param.43) | copy-start | bytes 1572868
  7.2 18.8 %copy-start.2 = (bf16[256,1024]{1,0:T(8,128)(2,1)S(1)}, bf16[256,1024]{1,0:T(8,128)(2,1)}, u32[]{:S(2)}) copy-start(bf16[256,1024]{1,0:T(8,128)(2,1)} %param.27) | copy-start | bytes 1572868
  7.2 133.2 %all-gather.9.cloned.1.call-start = ((), (), s32[]{:S(2)}) async-start(), calls=%async_computation.10 | async-start | bytes 6488064 | tf_op jit(solution)/shard_map/all_gather | solution.py:234
  9.0 155.9 %all-gather.15.cloned.1.call-start = ((), (), s32[]{:S(2)}) async-start(), calls=%async_computation.13 | async-start | bytes 2162688 | tf_op jit(solution)/shard_map/all_gather | solution.py:236
  10.7 212.6 %all-gather.17.cloned.1.call-start = ((), (), s32[]{:S(2)}) async-start(), calls=%async_computation.14 | async-start | bytes 8650752 | tf_op jit(solution)/shard_map/all_gather | solution.py:240
  12.5 290.1 %all-gather.19.cloned.1.call-start = ((), (), s32[]{:S(2)}) async-start(), calls=%async_computation.15 | async-start | bytes 8650752 | tf_op jit(solution)/shard_map/all_gather | solution.py:242
  26.1 8.9 copy-start.49
  26.1 8.9 copy-start.50
  26.1 8.9 copy-start.51
  26.1 8.9 copy-start.52
  26.1 8.9 copy-start.53
  26.1 8.9 copy-start.54
  26.1 9.1 copy-start.55
  28.5 95.3 %all-to-all-start = ((bf16[4,64,1024]{2,1,0:T(8,128)(2,1)}), bf16[4,64,1024]{2,1,0:T(8,128)(2,1)S(1)}, u32[]{:S(2)}, u32[]{:S(2)}) async-start(bf16[4,64,1024]{2,1,0:T(8,128)(2,1)} %bitcast.18), calls=%async_computation | async-start | bytes 1048576 | tf_op jit(solution)/shard_map/all_to_all | solution.py:268
  123.8 15.4 %all-to-all-start.2 = ((bf16[4,64,1024]{2,1,0:T(8,128)(2,1)}), bf16[4,64,1024]{2,1,0:T(8,128)(2,1)S(1)}, u32[]{:S(2)}, u32[]{:S(2)}) async-start(bf16[4,64,1024]{2,1,0:T(8,128)(2,1)} %bitcast.25), calls=%async_computation.2 | async-start | bytes 1048576 | tf_op jit(solution)/shard_map/all_to_all | solution.py:269
  127.3 224.9 %reduce-scatter.7.cloned.1.call-start = ((), (), s32[]{:S(2)}) async-start(), calls=%async_computation.16 | async-start | bytes 655360 | tf_op jit(solution)/shard_map/reduce_scatter | solution.py:325
  140.1 11.5 %copy-start.19 = (f32[64]{0:T(128)}, f32[64]{0:T(128)S(1)}, u32[]{:S(2)}) copy-start(f32[64]{0:T(128)S(1)} %broadcast_multiply_fusion.3) | copy-start | bytes 772
  140.3 11.3 %copy-start.44 = (f32[64]{0:T(128)}, f32[64]{0:T(128)S(1)}, u32[]{:S(2)}) copy-start(f32[64]{0:T(128)S(1)} %fusion.106) | copy-start | bytes 772
  140.3 11.3 %copy-start.25 = (f32[64]{0:T(128)}, f32[64]{0:T(128)S(1)}, u32[]{:S(2)}) copy-start(f32[64]{0:T(128)S(1)} %fusion.121) | copy-start | bytes 772
  151.6 12.0 %copy-start.14 = (bf16[256,1024]{0,1:T(8,128)(2,1)}, bf16[256,1024]{0,1:T(8,128)(2,1)S(1)}, u32[]{:S(2)}) copy-start(bf16[256,1024]{0,1:T(8,128)(2,1)S(1)} %copy.110) | copy-start | bytes 1572868
  153.1 11.8 %copy-start.11 = (bf16[64,16,32]{2,0,1:T(8,128)(2,1)}, bf16[64,16,32]{2,0,1:T(8,128)(2,1)S(1)}, u32[]{:S(2)}) copy-start(bf16[64,16,32]{2,0,1:T(8,128)(2,1)S(1)} %get-tuple-element.66) | copy-start | bytes 196612
  153.1 11.8 %copy-start.12 = (bf16[64,16,32]{2,0,1:T(8,128)(2,1)}, bf16[64,16,32]{2,0,1:T(8,128)(2,1)S(1)}, u32[]{:S(2)}) copy-start(bf16[64,16,32]{2,0,1:T(8,128)(2,1)S(1)} %get-tuple-element.67) | copy-start | bytes 196612
  167.2 146.2 %copy-start.27 = (f32[64]{0:T(128)}, f32[64]{0:T(128)S(1)}, u32[]{:S(2)}) copy-start(f32[64]{0:T(128)S(1)} %broadcast_multiply_fusion.2) | copy-start | bytes 772
  167.4 146.0 %copy-start.30 = (f32[64]{0:T(128)}, f32[64]{0:T(128)S(1)}, u32[]{:S(2)}) copy-start(f32[64]{0:T(128)S(1)} %fusion.122) | copy-start | bytes 772
  322.8 44.6 %reduce-scatter.9.cloned.1.call-start = ((), (), s32[]{:S(2)}) async-start(), calls=%async_computation.17 | async-start | bytes 655360 | tf_op jit(solution)/shard_map/reduce_scatter | solution.py:328
  327.2 68.9 %all-gather.11.cloned.1.call-start = ((), (), s32[]{:S(2)}) async-start(), calls=%async_computation.11 | async-start | bytes 2621440 | tf_op jit(solution)/shard_map/all_gather | solution.py:252
  327.5 9.1 copy-start.33
  327.5 9.1 copy-start.35
  327.6 9.1 copy-start.37
  327.6 9.1 copy-start.39
  335.0 82.2 %all-gather.13.cloned.1.call-start = ((), (), s32[]{:S(2)}) async-start(), calls=%async_computation.12 | async-start | bytes 2621440 | tf_op jit(solution)/shard_map/all_gather | solution.py:251
  348.0 213.7 %reduce-scatter.13.cloned.1.call-start = ((), (), s32[]{:S(2)}) async-start(), calls=%async_computation.19 | async-start | bytes 4325376 | tf_op jit(solution)/shard_map/reduce_scatter | solution.py:384
  351.8 367.6 %reduce-scatter.11.cloned.1.call-start = ((), (), s32[]{:S(2)}) async-start(), calls=%async_computation.18 | async-start | bytes 12976128 | tf_op jit(solution)/shard_map/reduce_scatter | solution.py:382
  353.5 14.8 %copy-start.20 = (f32[64]{0:T(128)S(1)}, f32[64]{0:T(128)}, u32[]{:S(2)}) copy-start(f32[64]{0:T(128)} %copy-done.19) | copy-start | bytes 772
  353.5 14.8 %copy-start.26 = (f32[64]{0:T(128)S(1)}, f32[64]{0:T(128)}, u32[]{:S(2)}) copy-start(f32[64]{0:T(128)} %copy-done.25) | copy-start | bytes 772
  374.7 529.5 %reduce-scatter.15.cloned.1.call-start = ((), (), s32[]{:S(2)}) async-start(), calls=%async_computation.20 | async-start | bytes 17301504 | tf_op jit(solution)/shard_map/reduce_scatter | solution.py:388
  384.0 707.7 %reduce-scatter.17.cloned.1.call-start = ((), (), s32[]{:S(2)}) async-start(), calls=%async_computation.21 | async-start | bytes 17301504 | tf_op jit(solution)/shard_map/reduce_scatter | solution.py:390
  393.0 24.2 %copy-start.16 = (bf16[256,16,32]{0,2,1:T(8,128)(2,1)S(1)}, bf16[256,16,32]{0,2,1:T(8,128)(2,1)}, u32[]{:S(2)}) copy-start(bf16[256,16,32]{0,2,1:T(8,128)(2,1)} %get-tuple-element.70) | copy-start | bytes 786436
  393.0 24.2 %copy-start.17 = (bf16[256,16,32]{0,2,1:T(8,128)(2,1)S(1)}, bf16[256,16,32]{0,2,1:T(8,128)(2,1)}, u32[]{:S(2)}) copy-start(bf16[256,16,32]{0,2,1:T(8,128)(2,1)} %get-tuple-element.71) | copy-start | bytes 786436
  427.8 9.3 copy-start.4
  446.3 20.4 %copy-start.24 = (f32[32,1,128]{2,1,0:T(1,128)S(1)}, f32[32,1,128]{2,1,0:T(1,128)}, u32[]{:S(2)}) copy-start(f32[32,1,128]{2,1,0:T(1,128)} %convert_element_type.324) | copy-start | bytes 49156
  447.9 15.1 %all-to-all-start.3 = ((bf16[4,64,1024]{2,1,0:T(8,128)(2,1)}), bf16[4,64,1024]{2,1,0:T(8,128)(2,1)S(1)}, u32[]{:S(2)}, u32[]{:S(2)}) async-start(bf16[4,64,1024]{2,1,0:T(8,128)(2,1)} %get-tuple-element.106), calls=%async_computation.5 | async-start | bytes 1048576 | tf_op jit(solution)/shard_map/all_to_all | solution.py:359
  463.0 73.2 %all-to-all-start.1 = ((bf16[4,64,1024]{2,1,0:T(8,128)(2,1)}), bf16[4,64,1024]{2,1,0:T(8,128)(2,1)S(1)}, u32[]{:S(2)}, u32[]{:S(2)}) async-start(bf16[4,64,1024]{2,1,0:T(8,128)(2,1)} %get-tuple-element.107), calls=%async_computation.1 | async-start | bytes 1048576 | tf_op jit(solution)/shard_map/all_to_all | solution.py:358
  466.7 20.5 %copy-start.18 = (f32[4096]{0:T(1024)S(1)}, f32[4096]{0:T(1024)}, u32[]{:S(2)}) copy-start(f32[4096]{0:T(1024)} %get-tuple-element.122) | copy-start | bytes 49156
  466.7 20.5 %copy-start.21 = (f32[1024]{0:T(1024)S(1)}, f32[1024]{0:T(1024)}, u32[]{:S(2)}) copy-start(f32[1024]{0:T(1024)} %get-tuple-element.20) | copy-start | bytes 12292
  466.7 20.5 %copy-start.22 = (f32[1024]{0:T(1024)S(1)}, f32[1024]{0:T(1024)}, u32[]{:S(2)}) copy-start(f32[1024]{0:T(1024)} %get-tuple-element.24) | copy-start | bytes 12292
  466.7 20.5 %copy-start.23 = (f32[1024]{0:T(1024)S(1)}, f32[1024]{0:T(1024)}, u32[]{:S(2)}) copy-start(f32[1024]{0:T(1024)} %get-tuple-element.45) | copy-start | bytes 12292
  535.0 556.7 %copy-start.1 = (bf16[256,1024]{1,0:T(8,128)(2,1)S(1)}, bf16[256,1024]{1,0:T(8,128)(2,1)}, u32[]{:S(2)}) copy-start(bf16[256,1024]{1,0:T(8,128)(2,1)} %param.43) | copy-start | bytes 1572868
  (26 other events, 80.3 us)
Sparse Core Ops, SparseCore 0:
  11.5 72.4 all-gather.8
  87.4 56.9 all-gather.14
  147.8 75.4 all-gather.16
  226.6 76.0 all-gather.18
  322.9 20.2 reduce-scatter.6
  345.7 21.6 reduce-scatter.8
  369.5 22.6 all-gather.10
  394.3 22.8 all-gather.12
  420.0 141.6 reduce-scatter.12
  568.2 151.2 reduce-scatter.10
  722.4 181.7 reduce-scatter.14
  907.1 184.5 reduce-scatter.16
where the time goes:
time: 1110 us; the launch traced here: 1100 us
  waiting for transfers between devices  731 us (66%)
  blocking collectives  148 us (13%)
  matrix products  115 us (10%)
  local copies, waits for them, and re-layouts  47 us (4%)
  other arithmetic  26.5 us (2%)
  between operations  16.6 us (1%)
  starting transfers between devices  14.8 us (1%)
    reduce_scatter x1, waiting for transfers between devices, on_device(): lax.psum_scatter(grad_list[10], ('dp', 'fsdp'), scatter_dimension=0, tile...  187 us
    reduce_scatter x1, waiting for transfers between devices, on_device(): lax.psum_scatter(grad_list[8], ('dp', 'fsdp'), scatter_dimension=0, tiled...  185 us
    reduce_scatter x1, waiting for transfers between devices, on_device(): lax.psum_scatter(grad_list[2], ('dp', 'fsdp'), scatter_dimension=0, tiled...  158 us
    unnamed x2, blocking collectives  85.6 us
    all_gather x1, waiting for transfers between devices, on_device(): lax.all_gather(shards[10], ('dp', 'fsdp'), axis=0, tiled=True)  71 us
    all_gather x1, waiting for transfers between devices, on_device(): lax.all_gather(shards[8], ('dp', 'fsdp'), axis=0, tiled=True)  55.8 us
    all_gather x1, blocking collectives, on_device(): lax.all_gather(shards[9], ('dp', 'fsdp'), axis=0, tiled=True)  41.1 us
    dot_general x2, matrix products, finish(): jnp.dot(activated, weights[10], preferred_element_type=jnp.float32)  25.5 us
  transfers between devices with their start and end apart: 16, of which 10 were waited for; matrix products, arithmetic and copies ran while one was open for 15% of the time, Pallas kernels for 0%

commit v1 on v0

--- a/solution.py
+++ b/solution.py
@@ -1,18 +1,1022 @@
+import functools
 import math
+import types
 
 import jax
 import jax.numpy as jnp
+import numpy as np
 from jax import lax
+from jax.experimental import pallas as pl
+from jax.experimental.pallas import tpu as pltpu
 from jax.sharding import PartitionSpec as P
 
 HEADS = 16
 HDIM = 64
 GRID = 14
 VIS_DEV = 64
-
-
 norm_eps = 1e-06
 masked_fill = -1e30
+FRAMES = 8
+EPS = 1e-06
+FILL = -1e30
+BF = jnp.bfloat16
+F32 = jnp.float32
+MESH = pl.DeviceIdType.MESH
+NT = (((1,), (1,)), ((), ()))
+NN = (((1,), (0,)), ((), ()))
+TN = (((0,), (0,)), ((), ()))
+
+
+def dot(a, b, dims=NN):
+    return lax.dot_general(a, b, dims, preferred_element_type=F32)
+
+
+def trig_table():
+    width = FRAMES + 2 * GRID
+    lane = np.arange(2 * HDIM)
+    pair = lane % (HDIM // 2)
+    axis = np.minimum(pair // 11, 2)
+    freq = np.exp(((pair - 11 * axis).astype(np.float32)) * np.float32(-math.log(10000.0) / 11.0))
+    sign = np.where(lane % HDIM < HDIM // 2, -1.0, 1.0)
+    table = np.zeros((128, 4 * HDIM), np.float32)
+    row = np.arange(width)
+    kind = np.where(row < FRAMES, 0, np.where(row < FRAMES + GRID, 1, 2))
+    coord = np.where(kind == 0, row, np.where(kind == 1, row - FRAMES, row - FRAMES - GRID))
+    angle = (coord[:, None].astype(np.float32) * freq[None, :].astype(np.float32)).astype(np.float64)
+    here = kind[:, None] == axis[None, :]
+    table[:width, : 2 * HDIM] = np.where(here, np.cos(angle), 0.0)
+    table[:width, 2 * HDIM :] = np.where(here, np.sin(angle) * sign[None, :], 0.0)
+    parts = []
+    rest = table
+    for _ in range(3):
+        part = rest.astype(jnp.bfloat16)
+        parts.append(part)
+        rest = rest - part.astype(np.float32)
+    return np.stack(parts)
+
+
+def norm_stats(v):
+    center = v - jnp.mean(v, axis=-1, keepdims=True)
+    inv = lax.rsqrt(jnp.mean(center * center, axis=-1, keepdims=True) + EPS)
+    return center * inv, inv
+
+
+def norm_back(v, gain, grad):
+    xhat, inv = norm_stats(v)
+    gg = grad * gain
+    dv = inv * (
+        gg - jnp.mean(gg, axis=-1, keepdims=True) - xhat * jnp.mean(gg * xhat, axis=-1, keepdims=True)
+    )
+    return (
+        dv,
+        jnp.sum(grad * xhat, axis=0, keepdims=True),
+        jnp.sum(grad, axis=0, keepdims=True),
+    )
+
+
+def swap_halves(u):
+    lane = lax.broadcasted_iota(jnp.int32, u.shape, 1)
+    return jnp.where(
+        lax.rem(lane, HDIM) < HDIM // 2,
+        pltpu.roll(u, u.shape[1] - HDIM // 2, 1),
+        pltpu.roll(u, HDIM // 2, 1),
+    )
+
+
+def column_segment(start, rows, ends):
+    row = start + lax.broadcasted_iota(jnp.int32, (rows, 1), 0)
+    seg = jnp.zeros((rows, 1), jnp.int32)
+    for end in ends:
+        seg += (row >= end).astype(jnp.int32)
+    return row, seg
+
+
+ALIASES = dict(N2="N1", PT="N1", D2="w2_v", D1="w1_v", DOo="wo_v", DQo="wqkv_v")
+
+
+class Sems:
+    def __init__(self, send, recv):
+        self.send, self.recv, self.used = send, recv, 0
+
+    def take(self):
+        at = self.used
+        self.used += 1
+        return self.send.at[at], self.recv.at[at]
+
+
+def layer_kernel(dims, names, *refs):
+    n, D, FF, T, V = dims
+    NF = 4
+    R = D // (n * NF)
+    RP = R * NF
+    HC = FF // (NF * n)
+    HF = FF // NF
+    C = D // NF
+    VP = V * NF
+    S_ = T * NF
+    last = n // 2 - 1
+    given = dict(zip(names, refs))
+    g = types.SimpleNamespace(**given, **{a: given[b] for a, b in ALIASES.items()})
+    sems = Sems(g.send_sems, g.recv_sems)
+    lsem = g.local_sems
+
+    p = lax.axis_index("dp")
+    f = lax.axis_index("fsdp")
+    f1 = f + 1 - 2 * lax.rem(f, 2)
+    f2 = lax.rem(f + 2, NF)
+    f3 = NF - 1 - f
+    par = lax.rem(p, 2)
+    half_p = lax.div(p, 2)
+    pos = (1 - par) * half_p + par * (n - 1 - half_p)
+
+    def idx(q):
+        q = lax.rem(q + 2 * n, n)
+        up = lax.div(q, n // 2)
+        return (1 - up) * (2 * q) + up * (2 * (n - 1 - q) + 1)
+
+    right, left = idx(pos + 1), idx(pos - 1)
+
+    pending = []
+
+    def remote(src, dst, to):
+        ss, rs = sems.take()
+        c = pltpu.make_async_remote_copy(
+            src_ref=src, dst_ref=dst, send_sem=ss, recv_sem=rs, device_id=to, device_id_type=MESH
+        )
+        c.start()
+        pending.append(c)
+        return c, ss, rs
+
+    def drain(*copies):
+        for c in copies:
+            pending[:] = [d for d in pending if d is not c]
+            c.wait_send()
+
+    def arrival(dst, ss, rs, to):
+        return pltpu.make_async_remote_copy(
+            src_ref=dst, dst_ref=dst, send_sem=ss, recv_sem=rs, device_id=to, device_id_type=MESH
+        )
+
+    to1, to2, to3 = {"fsdp": f1}, {"fsdp": f2}, {"fsdp": f3}
+    peers = ((f1, to1), (f2, to2), (f3, to3))
+
+    loads = {}
+    for i, (src, dst) in enumerate(
+        (
+            (g.wqkv, g.wqkv_v),
+            (g.w1, g.w1_v),
+            (g.wo, g.wo_v),
+            (g.small, g.small_v),
+            (g.tok, g.TA.at[f]),
+            (g.w2, g.w2_v),
+            (g.cot, g.CA.at[f]),
+            (g.trig, g.trig_v),
+        )
+    ):
+        c = pltpu.make_async_copy(src, dst, lsem.at[i])
+        c.start()
+        loads[i] = c
+
+    barrier = pltpu.get_barrier_semaphore()
+    for to in (to1, to2, to3, {"dp": right}, {"dp": left}):
+        pl.semaphore_signal(barrier, inc=1, device_id=to, device_id_type=MESH)
+
+    AS, AQ, WO, A1, A2 = g.AS, g.AQ, g.WO, g.A1, g.A2
+    TA, CA = g.TA, g.CA
+
+    loads[0].wait()
+    for j in range(NF):
+        for t in range(3):
+            g.sq[j, :, C * t : C * t + C] = g.wqkv_v[:, D * t + C * j : D * t + C * j + C].astype(BF)
+    loads[2].wait()
+    WO[p, f] = g.wo_v[...].astype(BF)
+    loads[3].wait()
+    AS[p, f] = g.small_v[...]
+    AQ[p, pl.ds(pl.multiple_of(R * f, R), R), :] = g.sq[f]
+    pl.semaphore_wait(barrier, 5)
+
+    def scatter(src, dst):
+        got = []
+        for fj, to in peers:
+            _, ss, rs = remote(src(fj), dst(f), to)
+            got.append(arrival(dst(fj), ss, rs, to))
+        return got
+
+    got_q = scatter(lambda j: g.sq.at[j], lambda j: AQ.at[p, pl.ds(pl.multiple_of(R * j, R), R), :])
+    got_s = scatter(lambda j: AS.at[p, f], lambda j: AS.at[p, j])
+
+    class AllGather4:
+        def __init__(self, slot):
+            self.slot = slot
+            _, self.sx, self.rx = remote(slot(f), slot(f), to2)
+            _, self.sc, self.rc = remote(slot(f), slot(f), to1)
+
+        def forward(self):
+            arrival(self.slot(f2), self.sx, self.rx, to2).wait_recv()
+            _, self.sd, self.rd = remote(self.slot(f2), self.slot(f2), to1)
+
+        def finish(self):
+            arrival(self.slot(f1), self.sc, self.rc, to1).wait_recv()
+            arrival(self.slot(f3), self.sd, self.rd, to1).wait_recv()
+
+    class ReduceScatter4:
+        def __init__(self, part, r1, xs, r2):
+            self.part, self.r1, self.xs, self.r2 = part, r1, xs, r2
+            self.ca, self.sa, self.ra = remote(part.at[f3], r1.at[1], to1)
+            self.cb, self.sb, self.rb = remote(part.at[f1], r1.at[0], to1)
+
+        def forward(self):
+            arrival(self.r1.at[1], self.sa, self.ra, to1).wait_recv()
+            self.xs[...] = (self.part[f2].astype(F32) + self.r1[1].astype(F32)).astype(BF)
+            _, self.sc, self.rc = remote(self.xs, self.r2, to2)
+
+        def finish(self):
+            arrival(self.r1.at[0], self.sb, self.rb, to1).wait_recv()
+            arrival(self.r2, self.sc, self.rc, to2).wait_recv()
+
+        def total(self):
+            return self.part[f].astype(F32) + self.r1[0].astype(F32) + self.r2[...].astype(F32)
+
+    class RingGather:
+        def __init__(self, view, rows):
+            self.view, self.rows = view, rows
+            self.arrivals = []
+
+        def step(self, r):
+            for a in self.arrivals:
+                a.wait_recv()
+            self.arrivals = []
+            h = self.rows // 2
+            spans = ((0, self.rows), (0, self.rows)) if r < last else ((0, h), (h, h))
+            for way, (s, c) in zip((1, -1), spans):
+                to, frm = ({"dp": right}, {"dp": left}) if way == 1 else ({"dp": left}, {"dp": right})
+                mine = self.view(idx(pos - way * r), s, c)
+                _, ss, rs = remote(mine, mine, to)
+                self.arrivals.append(arrival(self.view(idx(pos - way * (r + 1)), s, c), ss, rs, frm))
+
+        def finish(self):
+            for a in self.arrivals:
+                a.wait_recv()
+            self.arrivals = []
+
+    def rows_view(ref, offset):
+        return lambda slot, s, c: ref.at[slot, pl.ds(offset + s, c), :]
+
+    h = RP // 2
+    q_ring = [RingGather(rows_view(AQ, 0), h), RingGather(rows_view(AQ, h), h)]
+    w1_ring = [RingGather(rows_view(A1, 0), h), RingGather(rows_view(A1, h), h)]
+    w2_ring = [RingGather(rows_view(A2, 0), HC // 2), RingGather(rows_view(A2, HC // 2), HC // 2)]
+    o_ring = RingGather(lambda slot, s, c: WO.at[slot, f, pl.ds(s, c), :], R)
+    s_ring = RingGather(lambda slot, s, c: AS.at[slot, pl.ds(s, c)], NF)
+
+    class RingReduce:
+        def __init__(self, grads, start, rows, st, rr, rl, wire=BF):
+            self.G, self.o, self.rows, self.st, self.rr, self.rl = grads, start, rows, st, rr, rl
+            self.wire = wire
+            self.arrivals = []
+
+        def piece(self, ref, slot, s, c):
+            return ref.at[slot, pl.ds(self.o + s, c), :]
+
+        def step(self, r):
+            for a in self.arrivals:
+                a.wait_recv()
+            self.arrivals = []
+            o, rows = self.o, self.rows
+            hh = rows // 2
+            if r == 0:
+                far = idx(pos + n // 2)
+                self.st[pl.ds(o, rows), :] = self.G[far, pl.ds(o, rows), :].astype(self.wire)
+                for buf, s, to, frm in (
+                    (self.rr, 0, {"dp": right}, {"dp": left}),
+                    (self.rl, hh, {"dp": left}, {"dp": right}),
+                ):
+                    dst = self.piece(buf, 0, s, hh)
+                    _, ss, rs = remote(self.st.at[pl.ds(o + s, hh), :], dst, to)
+                    self.arrivals.append(arrival(dst, ss, rs, frm))
+                return
+            for way, buf, s, to, frm in (
+                (1, self.rr, 0, {"dp": right}, {"dp": left}),
+                (-1, self.rl, hh, {"dp": left}, {"dp": right}),
+            ):
+                c = idx(pos + way * (n // 2 - r))
+                if r == 1:
+                    other = hh - s
+                    buf[0, pl.ds(o + s, hh), :] = (
+                        buf[0, pl.ds(o + s, hh), :].astype(F32) + self.G[c, pl.ds(o + s, hh), :]
+                    ).astype(self.wire)
+                    buf[0, pl.ds(o + other, hh), :] = self.G[c, pl.ds(o + other, hh), :].astype(self.wire)
+                else:
+                    buf[r - 1, pl.ds(o, rows), :] = (
+                        buf[r - 1, pl.ds(o, rows), :].astype(F32) + self.G[c, pl.ds(o, rows), :]
+                    ).astype(self.wire)
+                src, dst = self.piece(buf, r - 1, 0, rows), self.piece(buf, r, 0, rows)
+                _, ss, rs = remote(src, dst, to)
+                self.arrivals.append(arrival(dst, ss, rs, frm))
+
+        def finish(self):
+            for a in self.arrivals:
+                a.wait_recv()
+            self.arrivals = []
+
+        def total(self):
+            o, rows = self.o, self.rows
+            return (
+                self.G[p, pl.ds(o, rows), :]
+                + self.rr[last, pl.ds(o, rows), :].astype(F32)
+                + self.rl[last, pl.ds(o, rows), :].astype(F32)
+            )
+
+    queue = []
+
+    def svc(count=1):
+        for _ in range(count):
+            if queue:
+                queue.pop(0)()
+
+    o_ring.step(0)
+    loads[1].wait()
+    for j in range(NF):
+        for t in range(n):
+            at = HC * (NF * t + j)
+            g.s1[j, :, HC * t : HC * t + HC] = g.w1_v[:, at : at + HC].astype(BF)
+    A1[p, pl.ds(pl.multiple_of(R * f, R), R), :] = g.s1[f]
+    for a in got_q:
+        a.wait_recv()
+    q_ring[0].step(0)
+    q_ring[1].step(0)
+    loads[4].wait()
+    tok_ag = AllGather4(lambda j: TA.at[j])
+    got_1 = scatter(lambda j: g.s1.at[j], lambda j: A1.at[p, pl.ds(pl.multiple_of(R * j, R), R), :])
+    for a in got_s:
+        a.wait_recv()
+    s_ring.step(0)
+    loads[5].wait()
+    A2[p] = g.w2_v[...].astype(BF)
+    o_ring.step(1)
+    q_ring[0].step(1)
+    q_ring[1].step(1)
+    loads[6].wait()
+    cot_ag = AllGather4(lambda j: CA.at[j])
+    s_ring.step(1)
+
+    ends = []
+    total_len = jnp.int32(0)
+    for k in range(g.lengths.shape[1]):
+        total_len = total_len + g.lengths[0, k]
+        ends.append(total_len)
+    row, seg = column_segment(0, S_, ends)
+    before = jnp.zeros((S_, 1), jnp.int32)
+    for k, end in enumerate(ends):
+        before += jnp.where(row >= end, g.lengths[0, k], 0)
+    place = row - before
+    img = GRID * GRID
+    frame = jnp.zeros((S_, 1), jnp.int32)
+    for t in range(1, FRAMES):
+        frame += (place >= img * t).astype(jnp.int32)
+    rest = place - img * frame
+    grow = jnp.zeros((S_, 1), jnp.int32)
+    for t in range(1, GRID):
+        grow += (rest >= GRID * t).astype(jnp.int32)
+    gcol = rest - GRID * grow
+    lane = lax.broadcasted_iota(jnp.int32, (S_, 128), 1)
+    hot = (lane == frame) | (lane == grow + FRAMES) | (lane == gcol + (FRAMES + GRID))
+    g.OH[...] = jnp.where(hot, 1.0, 0.0).astype(BF)
+    o_ring.step(2)
+    q_ring[0].step(2)
+    q_ring[1].step(2)
+    s_ring.step(2)
+    loads[7].wait()
+    g.CS[...] = sum(dot(g.OH[...], g.trig_v[k]) for k in range(3))
+    segrow = jnp.zeros((1, S_), jnp.int32)
+    keyrow = lax.broadcasted_iota(jnp.int32, (1, S_), 1)
+    for end in ends:
+        segrow += (keyrow >= end).astype(jnp.int32)
+    o_ring.step(3)
+    q_ring[0].step(3)
+    q_ring[1].step(3)
+    s_ring.step(3)
+
+    vis8 = jnp.concatenate([AS[p, j][4:6, :] for j in range(NF)], axis=0)
+    tri = (
+        lax.broadcasted_iota(jnp.int32, (128, 128), 0) <= lax.broadcasted_iota(jnp.int32, (128, 128), 1)
+    )
+    within = dot(vis8.astype(BF), jnp.where(tri, 1.0, 0.0).astype(BF))
+    base = jnp.zeros((1, 128), F32)
+    pieces, vpieces = [], []
+    for k in range(8):
+        pieces.append(within[k : k + 1, :] + base)
+        vpieces.append(vis8[k : k + 1, :])
+        base = base + jnp.sum(vis8[k : k + 1, :], axis=1, keepdims=True)
+    incl = jnp.concatenate(pieces, axis=1)
+    visrow = jnp.concatenate(vpieces, axis=1)
+    rank = jnp.where(visrow > 0.5, incl - 1.0, -1.0).astype(jnp.int32)
+    SM = g.SM
+    sel = lax.broadcasted_iota(jnp.int32, (VP, S_), 0) == rank
+    SM[...] = jnp.where(sel, 1.0, 0.0).astype(BF)
+    segv_col = jnp.sum(jnp.where(sel, segrow, 0).astype(F32), axis=1, keepdims=True).astype(jnp.int32)
+    seg8 = jnp.broadcast_to(segrow.astype(F32), (8, S_)).astype(BF)
+    segv_row = dot(seg8, SM[...], NT)[0:1, :].astype(jnp.int32)
+
+    tok_ag.forward()
+    s_ring.finish()
+    VEC, BQ = g.VEC, g.BQ
+    lane128 = lax.broadcasted_iota(jnp.int32, (n, 128), 1)
+    rows0 = [AS[:, j, 0, :] for j in range(NF)]
+    rows1 = [AS[:, j, 1, :] for j in range(NF)]
+    rows2 = [AS[:, j, 2, :] for j in range(NF)]
+
+    def rounded(v):
+        return v.astype(BF).astype(F32)
+
+    def turn(v, by):
+        by = by % 128
+        return v if by == 0 else pltpu.roll(v, by, 1)
+
+    def put_row(k, piece):
+        for q in range(n):
+            VEC[k : k + 1, 128 * q : 128 * q + 128] = rounded(piece[q : q + 1, :])
+
+    for k in range(6):
+        src = rows0 if k < 4 else rows1
+        piece = jnp.zeros((n, 128), F32)
+        for j in range(NF):
+            piece = jnp.where(lax.div(lane128, R) == j, turn(src[j], R * (j - k % 4)), piece)
+        put_row(k, piece)
+    for q in range(n):
+        VEC[6:7, 128 * q : 128 * q + 128] = rounded(AS[q, f][3:4, :])
+    t0 = jnp.where(lane128 < 96, rows2[0], turn(rows2[1], 96))
+    t1 = jnp.where(lane128 < 64, turn(rows2[1], -32), turn(rows2[2], 64))
+    t2 = jnp.where(lane128 < 32, turn(rows2[2], -64), turn(rows2[3], 32))
+    for q in range(n):
+        for k, t in enumerate((t0, t1, t2)):
+            BQ[0:1, 384 * q + 128 * k : 384 * q + 128 * k + 128] = rounded(t[q : q + 1, :])
+
+    def vec(k):
+        return VEC[k : k + 1, :]
+
+    tok_ag.finish()
+    N1 = g.N1
+
+    def norm_one(b, _):
+        xhat, _inv = norm_stats(TA[b].astype(F32))
+        N1[b] = (xhat * vec(0) + vec(1)).astype(BF)
+        return 0
+
+    lax.fori_loop(0, NF, norm_one, 0)
+    cot_ag.forward()
+    for a in got_1:
+        a.wait_recv()
+    w1_ring[0].step(0)
+    w1_ring[1].step(0)
+    for r in q_ring:
+        r.finish()
+    o_ring.finish()
+    wo_ag = AllGather4(lambda j: WO.at[:, j])
+
+    queue += [
+        lambda: w1_ring[0].step(1),
+        lambda: w1_ring[1].step(1),
+        lambda: w2_ring[0].step(0),
+        lambda: w1_ring[0].step(2),
+        lambda: w1_ring[1].step(2),
+        lambda: w2_ring[1].step(0),
+        lambda: w1_ring[0].step(3),
+        lambda: w1_ring[1].step(3),
+        lambda: w2_ring[0].step(1),
+        lambda: w2_ring[1].step(1),
+        lambda: w2_ring[0].step(2),
+        lambda: w2_ring[1].step(2),
+        lambda: w2_ring[0].step(3),
+        lambda: w2_ring[1].step(3),
+    ]
+
+    Q, K, W = g.Q, g.K, g.W
+    AQf = lambda s: AQ[:, :, s].reshape(D, -1)
+
+    def project(b, _):
+        cs = g.CS[pl.ds(pl.multiple_of(b * T, T), T), :]
+        for t, dst in enumerate((Q, K, W)):
+            out = dot(N1[b], AQ[:, :, C * t : C * t + C].reshape(D, C))
+            out = out + BQ[0:1, pl.ds(pl.multiple_of(D * t + C * f, 128), C)]
+            rows = pl.ds(pl.multiple_of(b * T, T), T)
+            if t == 2:
+                dst[rows, :] = out.astype(BF)
+                continue
+            for hh in range(C // 128):
+                u = out[:, 128 * hh : 128 * hh + 128]
+                u = (u * cs[:, :128] + swap_halves(u) * cs[:, 128:]).astype(BF)
+                dst[rows, 128 * hh : 128 * hh + 128] = u * BF(0.125) if t == 0 else u
+        return 0
+
+    lax.fori_loop(0, NF, project, 0)
+    svc(2)
+
+    QV, KV, WV = g.QV, g.KV, g.WV
+    for src, dst in ((Q, QV), (K, KV), (W, WV)):
+        dst[...] = dot(SM[...], src[...]).astype(BF)
+    OV, PV = g.OV, g.PV
+    lane_c = lax.broadcasted_iota(jnp.int32, (1, C), 1)
+    hmask = [jnp.where(lax.div(lane_c, HDIM) == hd, 1.0, 0.0) for hd in range(C // HDIM)]
+
+    def softmax(s):
+        e = jnp.exp(s - jnp.max(s, axis=-1, keepdims=True))
+        return e * (1.0 / jnp.sum(e, axis=-1, keepdims=True))
+
+    same_v = segv_col == segv_row
+    acc = jnp.zeros((VP, C), F32)
+    for hd in range(C // HDIM):
+        s = dot(QV[...] * hmask[hd].astype(BF), KV[...], NT)
+        pr = softmax(jnp.where(same_v, s, FILL))
+        PV[hd] = pr
+        acc += dot(pr.astype(BF), WV[...]) * hmask[hd]
+    OV[f] = acc.astype(BF)
+    ov_ag = AllGather4(lambda j: OV.at[j])
+    wo_ag.forward()
+    svc(2)
+
+    OA = g.OA
+
+    def target_head(hd):
+        def block(b, _):
+            rows = pl.ds(pl.multiple_of(b * T, T), T)
+            s = dot(Q[rows, :] * hmask[hd].astype(BF), K[...], NT)
+            _, segq = column_segment(b * T, T, ends)
+            pr = softmax(jnp.where(segq == segrow, s, FILL)).astype(BF)
+            o = dot(pr, W[...])
+            OA[f, rows, HDIM * hd : HDIM * hd + HDIM] = o[:, HDIM * hd : HDIM * hd + HDIM].astype(BF)
+            return 0
+
+        lax.fori_loop(0, NF, block, 0)
+
+    cot_ag.finish()
+    target_head(0)
+    ov_ag.forward()
+    svc(2)
+    XV, N1V, DY = g.XV, g.N1V, g.DY
+    for k in range(4):
+        cols = slice(256 * k, 256 * k + 256)
+        XV[:, cols] = dot(SM[...], TA[:, :, cols].reshape(S_, 256)).astype(BF)
+        DY[:, cols] = dot(SM[...], CA[:, :, cols].reshape(S_, 256)).astype(BF)
+        N1V[:, cols] = dot(SM[...], N1[:, :, cols].reshape(S_, 256)).astype(BF)
+    svc(2)
+
+    ov_ag.finish()
+    wo_ag.finish()
+
+    def out_project(parts, cols):
+        return sum(
+            dot(parts(j), WO[n // NF * j : n // NF * (j + 1), :, :, cols].reshape(C, -1)) for j in range(NF)
+        )
+
+    X1V, N2V = g.X1V, g.N2V
+    for k in range(4):
+        cols = slice(256 * k, 256 * k + 256)
+        X1V[:, cols] = XV[:, cols].astype(F32) + (out_project(lambda j: OV[j], cols) + VEC[4:5, cols])
+    xhat, _inv = norm_stats(X1V[...])
+    N2V[...] = (xhat * vec(2) + vec(3)).astype(BF)
+    svc(2)
+    target_head(1)
+    svc(1)
+    for r in w1_ring:
+        pass
+    while queue and len(queue) > 6:
+        svc(1)
+    for r in w1_ring:
+        r.finish()
+
+    GV, GP = g.GV, g.GP
+
+    def gelu_parts(hid):
+        cdf = 0.5 * (1.0 + lax.erf(hid * (1.0 / math.sqrt(2.0))))
+        return cdf
+
+    for k in range(4):
+        cols = slice(256 * k, 256 * k + 256)
+        hid = dot(N2V[...], A1[:, :, cols].reshape(D, 256)) + VEC[6:7, cols]
+        cdf = gelu_parts(hid)
+        GV[:, cols] = (hid * cdf).astype(BF)
+        GP[:, cols] = cdf + hid * (jnp.exp(-0.5 * hid * hid) * (1.0 / math.sqrt(2.0 * math.pi)))
+    svc(1)
+    G2, G1, GQ, GO = g.G2, g.G1, g.GQ, g.GO
+
+    def outer(dst, lhs, rhs, width):
+        def one(k, _):
+            a = lhs[:, pl.ds(pl.multiple_of(128 * k, 128), 128)]
+            dst[k] = dot(a, rhs[...], TN)
+            return 0
+
+        lax.fori_loop(0, n, one, 0)
+
+    outer(G2, GV, DY, D)
+    svc(1)
+    hc = HC // 2
+    g2_ring = [
+        RingReduce(G2, 0, hc, g.st2, g.rr2, g.rl2),
+        RingReduce(G2, hc, hc, g.st2, g.rr2, g.rl2),
+    ]
+    hr = RP // 2
+    g1_ring = [
+        RingReduce(G1, 0, hr, g.st1, g.rr1, g.rl1),
+        RingReduce(G1, hr, hr, g.st1, g.rr1, g.rl1),
+    ]
+    gq_ring = [
+        RingReduce(GQ, 0, hr, g.stq, g.rrq, g.rlq),
+        RingReduce(GQ, hr, hr, g.stq, g.rrq, g.rlq),
+    ]
+    go_ring = RingReduce(GO, 0, R, g.sto, g.rro, g.rlo)
+    gs_ring = RingReduce(g.VG, 0, 16, g.sts, g.rrs, g.rls, F32)
+    queue += [lambda: g2_ring[0].step(0), lambda: g2_ring[1].step(0)]
+    target_head(2)
+    svc(2)
+    target_head(3)
+    oa_ag = AllGather4(lambda j: OA.at[j])
+    svc(2)
+    while queue:
+        svc(1)
+    for r in w2_ring:
+        r.finish()
+    queue += [
+        lambda: g2_ring[0].step(1),
+        lambda: g2_ring[1].step(1),
+        lambda: g2_ring[0].step(2),
+        lambda: g2_ring[1].step(2),
+        lambda: g2_ring[0].step(3),
+        lambda: g2_ring[1].step(3),
+    ]
+
+    DH, PN = g.DH, g.PN
+    VG = g.VG
+    zero_row = jnp.zeros((1, 128), F32)
+
+    def put_grad(k, vrow):
+        for q in range(n):
+            VG[q, k : k + 1, :] = vrow[:, 128 * q : 128 * q + 128]
+
+    for k in range(4):
+        cols = slice(256 * k, 256 * k + 256)
+        dg = dot(DY[...], A2[:, :, :].reshape(HF, D)[256 * k : 256 * k + 256, :], NT)
+        dh = (dg * GP[:, cols]).astype(BF)
+        DH[:, cols] = dh
+        dc1 = jnp.sum(dh.astype(F32), axis=0, keepdims=True)
+        for q in range(2):
+            for j in range(NF):
+                VG[2 * k + q, 9 + j : 10 + j, :] = jnp.where(f == j, dc1[:, 128 * q : 128 * q + 128], zero_row)
+    svc(1)
+    for k in range(4):
+        cols = slice(256 * k, 256 * k + 256)
+        part = dot(DH[...], A1[2 * k : 2 * k + 2, :, :].reshape(256, HF), NT).astype(BF)
+        PN[:, :, cols] = part.reshape(NF, V, 256)
+    n2_rs = ReduceScatter4(PN, g.PNr1, g.PNxs, g.PNr2)
+    outer(G1, N2V, DH, HF)
+    svc(2)
+    n2_rs.forward()
+    queue += [
+        lambda: g1_ring[0].step(0),
+        lambda: g1_ring[1].step(0),
+        lambda: g1_ring[0].step(1),
+        lambda: g1_ring[1].step(1),
+        lambda: g1_ring[0].step(2),
+        lambda: g1_ring[1].step(2),
+        lambda: g1_ring[0].step(3),
+        lambda: g1_ring[1].step(3),
+    ]
+    PF = g.PF
+    for k in range(4):
+        cols = slice(256 * k, 256 * k + 256)
+        part = dot(GV[...], A2[:, :, cols].reshape(HF, 256)).astype(BF)
+        PF[:, :, cols] = part.reshape(NF, V, 256)
+    oa_ag.forward()
+    svc(1)
+    mine = pl.ds(pl.multiple_of(V * f, V), V)
+    n2_rs.finish()
+    dn2 = n2_rs.total()
+    dyo = DY[mine, :].astype(F32)
+    dv, dgain, dshift = norm_back(X1V[mine, :], vec(2), dn2)
+    dx1 = dyo + dv
+    g.DX1[...] = dx1
+    dP = dx1.astype(BF)
+    g.DP[f] = dP
+    dp_ag = AllGather4(lambda j: g.DP.at[j])
+    put_grad(2, dgain)
+    put_grad(3, dshift)
+    put_grad(4, jnp.sum(dP.astype(F32), axis=0, keepdims=True))
+    put_grad(5, jnp.sum(dyo, axis=0, keepdims=True))
+    pf_rs = ReduceScatter4(PF, g.PFr1, g.PFxs, g.PFr2)
+    svc(2)
+    OT = g.OT
+    for j in range(NF):
+        ot = OV[j].astype(F32).T.astype(BF)
+        OT[n // NF * j : n // NF * (j + 1)] = ot.reshape(n // NF, NF, R, VP)
+    dp_ag.forward()
+    svc(1)
+    pf_rs.forward()
+    dp_ag.finish()
+    DPv = lambda: g.DP[...].reshape(VP, D)
+    go = dot(OT[:, f].reshape(n * R, VP), DPv())
+    GO[...] = go.reshape(n, R, D)
+    wo_heads = WO[pl.ds(n // NF * f, n // NF)].reshape(C, D)
+    dO = dot(DPv(), wo_heads, NT).astype(BF)
+    g.DO[...] = dO
+    svc(1)
+    queue += [lambda: go_ring.step(0)]
+
+    DO = g.DO
+    dq = jnp.zeros((VP, C), F32)
+    dk = jnp.zeros((VP, C), F32)
+    dw = jnp.zeros((VP, C), F32)
+    for hd in range(C // HDIM):
+        pr = PV[hd]
+        dp = dot(DO[...] * hmask[hd].astype(BF), WV[...], NT)
+        ds = (pr * (dp - jnp.sum(pr * dp, axis=-1, keepdims=True))).astype(BF)
+        dq += dot(ds, KV[...]) * hmask[hd]
+        dk += dot(ds, QV[...], TN) * hmask[hd]
+        dw += dot(pr.astype(BF), DO[...], TN) * hmask[hd]
+    csv = sum(dot(dot(SM[...], g.OH[...]).astype(BF), g.trig_v[k]) for k in range(3))
+    DPRE = g.DPRE
+    for t, (grad, scale) in enumerate(((dq, 0.125), (dk, 1.0))):
+        for hh in range(C // 128):
+            u = grad[:, 128 * hh : 128 * hh + 128]
+            u = u * csv[:, :128] - swap_halves(u) * csv[:, 128:]
+            DPRE[:, C * t + 128 * hh : C * t + 128 * hh + 128] = (u * scale).astype(BF)
+    DPRE[:, 2 * C :] = dw.astype(BF)
+    svc(2)
+    BG = g.BG
+    BG[...] = jnp.zeros(BG.shape, F32)
+    db = jnp.sum(DPRE[...].astype(F32), axis=0, keepdims=True)
+    for t in range(3):
+        BG[0:1, pl.ds(pl.multiple_of(D * t + C * f, 128), C)] = db[:, C * t : C * t + C]
+    for q in range(n):
+        for t in range(3):
+            VG[q, 6 + t : 7 + t, :] = BG[0:1, 384 * q + 128 * t : 384 * q + 128 * t + 128]
+        VG[q, 13:16, :] = jnp.zeros((3, 128), F32)
+
+    drain(n2_rs.ca, n2_rs.cb)
+    for k in range(4):
+        part = dot(DPRE[...], AQ[2 * k : 2 * k + 2, :, :].reshape(256, 3 * C), NT).astype(BF)
+        PN[:, :, 256 * k : 256 * k + 256] = part.reshape(NF, V, 256)
+    n1_rs = ReduceScatter4(PN, g.PMr1, g.PMxs, g.PMr2)
+    outer(GQ, N1V, DPRE, 3 * C)
+    svc(2)
+    queue += [
+        lambda: go_ring.step(1),
+        lambda: gq_ring[0].step(0),
+        lambda: gq_ring[1].step(0),
+        lambda: go_ring.step(2),
+        lambda: gq_ring[0].step(1),
+        lambda: gq_ring[1].step(1),
+        lambda: go_ring.step(3),
+        lambda: gq_ring[0].step(2),
+        lambda: gq_ring[1].step(2),
+        lambda: gq_ring[0].step(3),
+        lambda: gq_ring[1].step(3),
+    ]
+    n1_rs.forward()
+    pf_rs.finish()
+    out_own = X1V[mine, :] + (pf_rs.total() + vec(5))
+    g.CO[f] = out_own.astype(BF)
+    co_ag = AllGather4(lambda j: g.CO.at[j])
+    svc(1)
+    n1_rs.finish()
+    dv, dgain, dshift = norm_back(XV[mine, :].astype(F32), vec(0), n1_rs.total())
+    g.DX[f] = (g.DX1[...] + dv).astype(BF)
+    dx_ag = AllGather4(lambda j: g.DX.at[j])
+    put_grad(0, dgain)
+    put_grad(1, dshift)
+    gs_ring.step(0)
+    co_ag.forward()
+    svc(2)
+
+    oa_ag.finish()
+    N2 = g.N2
+
+    def target_mid(b, _):
+        rows = pl.ds(pl.multiple_of(b * T, T), T)
+        for k in range(4):
+            cols = slice(256 * k, 256 * k + 256)
+            g.X1B[:, cols] = TA[b, :, cols].astype(F32) + (
+                out_project(lambda j: OA[j, rows, :], cols) + VEC[4:5, cols]
+            )
+        x1 = g.X1B[...]
+        xh, _i = norm_stats(x1)
+        N2[b] = (xh * vec(2) + vec(3)).astype(BF)
+
+        @pl.when(b == f)
+        def _():
+            g.X1H[...] = x1
+
+        return 0
+
+    lax.fori_loop(0, NF, target_mid, 0)
+    dx_ag.forward()
+    gs_ring.step(1)
+    svc(2)
+    GT, PT = g.GT, g.PT
+
+    def target_hidden(b, _):
+        for k in range(4):
+            cols = slice(256 * k, 256 * k + 256)
+            hid = dot(N2[b], A1[:, :, cols].reshape(D, 256)) + VEC[6:7, cols]
+            GT[b, :, cols] = (hid * gelu_parts(hid)).astype(BF)
+        return 0
+
+    lax.fori_loop(0, 2, target_hidden, 0)
+    gs_ring.step(2)
+    svc(2)
+    lax.fori_loop(2, 4, target_hidden, 0)
+    gs_ring.step(3)
+    svc(2)
+
+    def target_out(b, _):
+        for k in range(4):
+            cols = slice(256 * k, 256 * k + 256)
+            PT[b, :, cols] = dot(GT[b], A2[:, :, cols].reshape(HF, 256)).astype(BF)
+        return 0
+
+    lax.fori_loop(0, NF, target_out, 0)
+    pt_rs = ReduceScatter4(PT, g.PTr1, g.PTxs, g.PTr2)
+    svc(2)
+
+    def home(src, dst):
+        s = SM[:, pl.ds(pl.multiple_of(T * f, 128), T)]
+        for k in range(4):
+            cols = slice(256 * k, 256 * k + 256)
+            dst[:, cols] = dot(s, src[:, :, cols].reshape(VP, 256), TN).astype(BF)
+
+    outs = []
+
+    def store(src, dst, k):
+        c = pltpu.make_async_copy(src, dst, lsem.at[8 + k])
+        c.start()
+        outs.append(c)
+
+    co_ag.finish()
+    home(g.CO, g.CH)
+    store(g.CH, g.ctx_o, 0)
+    pt_rs.forward()
+    svc(1)
+    dx_ag.finish()
+    home(g.DX, g.DXH)
+    store(g.DXH, g.dx_o, 1)
+    gs_ring.finish()
+    SG = g.SG
+    SG[f] = gs_ring.total()
+    got_g = scatter(lambda j: SG.at[f], lambda j: SG.at[j])
+    for k, ring in enumerate(g2_ring):
+        ring.finish()
+        g.D2[hc * k : hc * k + hc, :] = ring.total()
+    store(g.D2, g.g2_o, 2)
+    svc(1)
+    E1, EQ = g.E1, g.EQ
+    while queue and len(queue) > 4:
+        svc(1)
+    for k, ring in enumerate(g1_ring):
+        ring.finish()
+        E1[2 * k : 2 * k + 2] = ring.total().astype(BF).reshape(2, R, HF)
+    F1 = g.F1
+    F1[f] = E1[f]
+    got_e1 = scatter(lambda j: E1.at[j], lambda j: F1.at[j])
+    svc(2)
+    pt_rs.finish()
+    g.TO[...] = (g.X1H[...] + (pt_rs.total() + vec(5))).astype(BF)
+    store(g.TO, g.tgt_o, 3)
+    svc(2)
+    go_ring.finish()
+    g.DOo[...] = go_ring.total()
+    store(g.DOo, g.go_o, 4)
+    for a in got_e1:
+        a.wait_recv()
+    for j in range(NF):
+        for t in range(n):
+            at = HC * (NF * t + j)
+            g.D1[:, at : at + HC] = F1[j, :, HC * t : HC * t + HC].astype(F32)
+    store(g.D1, g.g1_o, 5)
+    for a in got_g:
+        a.wait_recv()
+    g.SGo[...] = SG[0] + SG[1] + SG[2] + SG[3]
+    store(g.SGo, g.sg_o, 6)
+    while queue:
+        svc(1)
+    for k, ring in enumerate(gq_ring):
+        ring.finish()
+        EQ[2 * k : 2 * k + 2] = ring.total().astype(BF).reshape(2, R, 3 * C)
+    FQ = g.FQ
+    FQ[f] = EQ[f]
+    got_eq = scatter(lambda j: EQ.at[j], lambda j: FQ.at[j])
+    for a in got_eq:
+        a.wait_recv()
+    for j in range(NF):
+        for t in range(3):
+            g.DQo[:, D * t + C * j : D * t + C * j + C] = FQ[j, :, C * t : C * t + C].astype(F32)
+    store(g.DQo, g.gq_o, 7)
+    for c in outs:
+        c.wait()
+    for c in pending:
+        c.wait_send()
+
+
+def run_layer(n, tokens, cot, lengths, small, wqkv, wo, w1, w2, V):
+    T, D = tokens.shape
+    NF = 4
+    FF = w1.shape[1]
+    R = wo.shape[0]
+    RP = R * NF
+    HC = w2.shape[0]
+    HF = HC * n
+    C = D // NF
+    VP = V * NF
+    S_ = T * NF
+    h2 = n // 2
+    B, F = BF, F32
+    vm = pltpu.VMEM
+    scratch = dict(
+        wqkv_v=vm((R, 3 * D), F), w1_v=vm((R, FF), F), wo_v=vm((R, D), F), w2_v=vm((HC, D), F),
+        small_v=vm((8, 128), F), trig_v=vm((3, 128, 256), B),
+        sq=vm((NF, R, 3 * C), B), s1=vm((NF, R, HF), B),
+        AS=vm((n, NF, 8, 128), F), AQ=vm((n, RP, 3 * C), B), WO=vm((n, NF, R, D), B),
+        A1=vm((n, RP, HF), B), A2=vm((n, HC, D), B),
+        TA=vm((NF, T, D), B), CA=vm((NF, T, D), B), N1=vm((NF, T, D), B),
+        OH=vm((S_, 128), B), CS=vm((S_, 256), F), SM=vm((VP, S_), B),
+        VEC=vm((8, D), F), BQ=vm((8, 3 * D), F), BG=vm((8, 3 * D), F),
+        Q=vm((S_, C), B), K=vm((S_, C), B), W=vm((S_, C), B),
+        QV=vm((VP, C), B), KV=vm((VP, C), B), WV=vm((VP, C), B),
+        OV=vm((NF, VP, C), B), PV=vm((C // HDIM, VP, VP), F), OA=vm((NF, S_, C), B),
+        XV=vm((VP, D), B), N1V=vm((VP, D), B), DY=vm((VP, D), B),
+        X1V=vm((VP, D), F), N2V=vm((VP, D), B), GV=vm((VP, HF), B), GP=vm((VP, HF), F),
+        G2=vm((n, HC, D), F), G1=vm((n, RP, HF), F), GQ=vm((n, RP, 3 * C), F), GO=vm((n, R, D), F),
+        VG=vm((n, 16, 128), F),
+        st2=vm((HC, D), B), rr2=vm((h2, HC, D), B), rl2=vm((h2, HC, D), B),
+        st1=vm((RP, HF), B), rr1=vm((h2, RP, HF), B), rl1=vm((h2, RP, HF), B),
+        stq=vm((RP, 3 * C), B), rrq=vm((h2, RP, 3 * C), B), rlq=vm((h2, RP, 3 * C), B),
+        sto=vm((R, D), B), rro=vm((h2, R, D), B), rlo=vm((h2, R, D), B),
+        sts=vm((16, 128), F), rrs=vm((h2, 16, 128), F), rls=vm((h2, 16, 128), F),
+        DH=vm((VP, HF), B), PN=vm((NF, V, D), B), PF=vm((NF, V, D), B),
+        PNr1=vm((2, V, D), B), PNxs=vm((V, D), B), PNr2=vm((V, D), B),
+        PMr1=vm((2, V, D), B), PMxs=vm((V, D), B), PMr2=vm((V, D), B),
+        PFr1=vm((2, V, D), B), PFxs=vm((V, D), B), PFr2=vm((V, D), B),
+        DX1=vm((V, D), F), DP=vm((NF, V, D), B), OT=vm((n, NF, R, VP), B), DO=vm((VP, C), B),
+        DPRE=vm((VP, 3 * C), B), CO=vm((NF, V, D), B), DX=vm((NF, V, D), B),
+        X1B=vm((T, D), F), X1H=vm((T, D), F), GT=vm((NF, T, HF), B),
+        PTr1=vm((2, T, D), B), PTxs=vm((T, D), B), PTr2=vm((T, D), B),
+        CH=vm((T, D), B), DXH=vm((T, D), B), TO=vm((T, D), B),
+        SG=vm((NF, 16, 128), F), SGo=vm((16, 128), F),
+        E1=vm((NF, R, HF), B), F1=vm((NF, R, HF), B), EQ=vm((NF, R, 3 * C), B), FQ=vm((NF, R, 3 * C), B),
+        send_sems=pltpu.SemaphoreType.DMA((200,)), recv_sems=pltpu.SemaphoreType.DMA((200,)),
+        local_sems=pltpu.SemaphoreType.DMA((16,)),
+    )
+    arr = jax.ShapeDtypeStruct
+    ins = dict(
+        lengths=lengths, tok=tokens, cot=cot, small=small, wqkv=wqkv, wo=wo, w1=w1, w2=w2,
+        trig=jnp.asarray(trig_table()),
+    )
+    outs = dict(
+        tgt_o=arr((T, D), B), ctx_o=arr((T, D), B), dx_o=arr((T, D), B), gq_o=arr((R, 3 * D), F),
+        go_o=arr((R, D), F), g1_o=arr((R, FF), F), g2_o=arr((HC, D), F), sg_o=arr((16, 128), F),
+    )
+    names = [*ins, *outs, *scratch]
+    any_spec = pl.BlockSpec(memory_space=pl.ANY)
+    return pl.pallas_call(
+        functools.partial(layer_kernel, (n, D, FF, T, V), names),
+        out_shape=list(outs.values()),
+        in_specs=[pl.BlockSpec(memory_space=pltpu.SMEM)] + [any_spec] * 8,
+        out_specs=[any_spec] * 8,
+        scratch_shapes=list(scratch.values()),
+        compiler_params=pltpu.CompilerParams(
+            collective_id=0, has_side_effects=True, vmem_limit_bytes=67043328
+        ),
+        name="layer",
+    )(*ins.values())
+
+
+def on_device(
+    tokens, lengths, visibility_mask, visible_counts, ln1_gain, ln1_bias, qkv_weight, qkv_bias,
+    out_weight, out_bias, ln2_gain, ln2_bias, fc1_weight, fc1_bias, fc2_weight, fc2_bias, context_cot,
+):
+    n = lax.axis_size("dp")
+    f = lax.axis_index("fsdp")
+    R = ln1_gain.shape[0]
+    running = jnp.cumsum(visibility_mask)
+    visible = (visibility_mask * (running <= visible_counts[0, 0]).astype(jnp.int32)).astype(F32)
+    pad = lambda k: jnp.zeros((k,), F32)
+    small = jnp.concatenate(
+        [
+            ln1_gain, ln1_bias, ln2_gain, ln2_bias,
+            out_bias, fc2_bias, pad(64),
+            qkv_bias, pad(32),
+            fc1_bias,
+            visible, pad(256),
+        ]
+    ).reshape(8, 128)
+    tgt, ctx, dx, gq, go, g1, g2, sg = run_layer(
+        n, tokens, context_cot, lengths, small, qkv_weight, out_weight, fc1_weight, fc2_weight, VIS_DEV
+    )
+
+    def own(k):
+        return lax.dynamic_slice(sg[k], (R * f,), (R,))
+
+    gbq = lax.dynamic_slice(sg[6:9].reshape(-1), (3 * R * f,), (3 * R,))
+    gb1 = lax.dynamic_slice(sg[9:13].reshape(-1), (4 * R * f,), (4 * R,))
+    return (tgt, ctx, dx, own(0), own(1), gq, gbq, go, own(4), own(2), own(3), g1, gb1, g2, own(5))
 
 
 def layer_norm(inputs, scale_vec, shift_vec):
@@ -184,7 +1188,7 @@
     return (result, middle, second, hidden, activated)
 
 
-def on_device(
+def gathered_device(
     tokens,
     lengths,
     visibility_mask,
@@ -409,45 +1413,23 @@
     )
 
 
+def per_device(tokens, *rest):
+    n, group = lax.axis_size("dp"), lax.axis_size("fsdp")
+    out_rows = rest[7].shape[0]
+    fits = group == 4 and n == 8 and out_rows * group == 128
+    return (on_device if fits else gathered_device)(tokens, *rest)
+
+
 def solution(mesh):
+    both = ("dp", "fsdp")
+    vec, mat = P(both), P(both, None)
     return jax.shard_map(
-        on_device,
+        per_device,
         mesh=mesh,
         in_specs=(
-            P(("dp", "fsdp"), None),
-            P("dp", None),
-            P(("dp", "fsdp")),
-            P("dp", "fsdp"),
-            P(("dp", "fsdp")),
-            P(("dp", "fsdp")),
-            P(("dp", "fsdp"), None),
-            P(("dp", "fsdp")),
-            P(("dp", "fsdp"), None),
-            P(("dp", "fsdp")),
-            P(("dp", "fsdp")),
-            P(("dp", "fsdp")),
-            P(("dp", "fsdp"), None),
-            P(("dp", "fsdp")),
-            P(("dp", "fsdp"), None),
-            P(("dp", "fsdp")),
-            P(("dp", "fsdp"), None),
+            mat, P("dp", None), vec, P("dp", "fsdp"), vec, vec, mat, vec, mat, vec, vec, vec,
+            mat, vec, mat, vec, mat,
         ),
-        out_specs=(
-            P(("dp", "fsdp"), None),
-            P(("dp", "fsdp"), None),
-            P(("dp", "fsdp"), None),
-            P(("dp", "fsdp")),
-            P(("dp", "fsdp")),
-            P(("dp", "fsdp"), None),
-            P(("dp", "fsdp")),
-            P(("dp", "fsdp"), None),
-            P(("dp", "fsdp")),
-            P(("dp", "fsdp")),
-            P(("dp", "fsdp")),
-            P(("dp", "fsdp"), None),
-            P(("dp", "fsdp")),
-            P(("dp", "fsdp"), None),
-            P(("dp", "fsdp")),
-        ),
+        out_specs=(mat, mat, mat, vec, vec, mat, vec, mat, vec, vec, vec, mat, vec, mat, vec),
         check_vma=False,
     )

time: 1110 us -> 178 us (0.16)
  waiting for transfers between devices: 731 us -> 0 us
  Pallas kernels: 0 us -> 162 us
  blocking collectives: 148 us -> 0 us
  matrix products: 115 us -> 0 us
  local copies, waits for them, and re-layouts: 47 us -> 14.2 us
  other arithmetic: 26.5 us -> 0.42 us
  between operations: 16.6 us -> 1.4 us
  starting transfers between devices: 14.8 us -> 0 us
    reduce_scatter x6 -> x0, waiting for transfers between devices: 565 us -> none  [the longest x1 187 us: on_device(): lax.psum_scatter(grad_list[10], ('dp', 'fsdp'), scatter_dimension=0, tile...]
    pallas_call x0 -> x1, Pallas kernels: none -> 162 us  [run_layer(): pl.pallas_call(functools.partial(layer_kernel, (n, D, FF, T, V), names),...]
    all_gather x6 -> x0, waiting for transfers between devices: 144 us -> none  [the longest x1 71 us: on_device(): lax.all_gather(shards[10], ('dp', 'fsdp'), axis=0, tiled=True)]
    dot_general x22 -> x0, matrix products: 104 us -> none  [the longest x2 25.5 us: finish(): jnp.dot(activated, weights[10], preferred_element_type=jnp.float32)]
    unnamed x2 -> x0, blocking collectives: 85.6 us -> none
    all_gather x4 -> x0, blocking collectives: 62.8 us -> none  [the longest x1 41.1 us: on_device(): lax.all_gather(shards[9], ('dp', 'fsdp'), axis=0, tiled=True)]
    all_to_all x4 -> x0, waiting for transfers between devices: 21.2 us -> none  [the longest x1 11 us: on_device(): lax.all_to_all(send_cot, 'fsdp', split_axis=0, concat_axis=0, tiled=True)]
    gather x14 -> x0, local copies, waits for them, and re-layouts: 14.7 us -> none  [the longest x1 1.5 us: on_device(): cos_home, sin_home = rope_tables(jnp.take(places, home_rows))]
  transfers between devices with their start and end apart: 16 -> 0, of which waited for: 10 -> 0; matrix products, arithmetic and copies ran while one was open for 15% -> 0% of each run, Pallas kernels for 0% -> 0%
where the time goes in v1:
time: 178 us
  Pallas kernels  162 us (91%)
  local copies, waits for them, and re-layouts  14.2 us (8%)
    pallas_call x1, Pallas kernels, run_layer(): pl.pallas_call(functools.partial(layer_kernel, (n, D, FF, T, V), names),...  162 us
    unnamed x39, local copies, waits for them, and re-layouts  9.5 us

profile of v1, /device:TPU:0, one launch (start us, length us, event | category | flops | bytes accessed | tf_op | source)
XLA Modules:
  0.0 177.7 jit_solution(10652674718448832308)
XLA Ops:
  0.6 0.0 copy-start.7
  0.7 0.7 copy-done.7
  1.3 0.3 reduce-window.9
  1.6 0.1 slice.31
  1.7 0.1 slice_reduce_fusion
  2.5 0.1 fusion
  2.6 0.0 copy-start.15
  2.6 0.0 copy-start.11
  2.6 0.0 copy-start.12
  2.6 0.0 copy-start.13
  2.6 0.0 copy-start.14
  2.6 0.0 copy-start.8
  2.7 0.0 copy-start.9
  2.7 0.0 copy-start.10
  2.7 0.6 copy-done.15
  3.2 0.0 copy-done.11
  3.3 0.0 copy-done.12
  3.3 0.0 copy-done.13
  3.3 0.0 copy-done.14
  3.3 0.0 copy-done.8
  3.3 0.0 copy-done.9
  3.3 0.0 copy-done.10
  3.4 0.7 concatenate.3
  4.0 161.6 %layer.1 = (bf16[256,1024]{1,0:T(8,128)(2,1)}, bf16[256,1024]{1,0:T(8,128)(2,1)}, bf16[256,1024]{1,0:T(8,128)(2,1)}, f32[32,3072]{1,0:T(8,128)}, f32[32,1024]{1,...) custom-call(s32[1,6]{1,0:T(1,128)} %refs_0_.1, bf16[256,1024]{1,0:T(8,128)(2,1)} %refs_1_.1, ...), custom_call_target="tpu_custom_call" | custom-call | tf_op jit(solution)/shard_map/layer/pallas_call | solution.py:978
  165.7 0.9 fusion.7
  166.6 0.6 fusion.5
  167.2 0.6 fusion.3
  167.7 0.0 copy-start.6
  167.7 0.6 fusion.1
  168.3 0.1 copy-done.6
  168.4 0.6 dynamic_slice.40
  169.0 0.6 dynamic_slice.47
  169.6 0.0 copy-start.3
  169.6 1.9 %copy.41 = bf16[256,1024]{1,0:T(8,128)(2,1)} copy(bf16[256,1024]{1,0:T(8,128)(2,1)} %get-tuple-element.58) | data formatting | bytes 1048576
  171.5 0.0 copy-done.3
  171.6 0.0 copy-start.2
  171.6 0.8 copy.42
  172.3 0.4 copy-done.2
  172.8 0.0 copy-start.4
  172.8 0.8 copy.43
  173.6 0.4 copy-done.4
  174.0 0.7 copy.44
  174.7 0.2 copy-done.5
  175.0 0.7 copy.45
  175.6 0.0 copy-done.1
  175.6 0.8 copy.46
  176.4 0.4 copy-done
  176.9 0.8 copy.47
  (9 shorter events, 0.1 us)
Async XLA Ops:
  0.6 0.7 copy-start.7
  2.6 0.7 copy-start.15
  2.6 0.7 copy-start.11
  2.6 0.7 copy-start.12
  2.6 0.7 copy-start.13
  2.6 0.7 copy-start.14
  2.6 0.7 copy-start.8
  2.7 0.7 copy-start.9
  2.7 0.7 copy-start.10
  167.7 0.7 copy-start.6
  169.6 1.9 %copy-start.3 = (bf16[256,1024]{1,0:T(8,128)(2,1)S(1)}, bf16[256,1024]{1,0:T(8,128)(2,1)}, u32[]{:S(2)}) copy-start(bf16[256,1024]{1,0:T(8,128)(2,1)} %get-tuple-element.59) | copy-start | bytes 1572868
  171.6 1.2 copy-start.2
  172.8 1.2 copy-start.4
  174.0 1.0 copy-start.5
  174.0 1.7 copy-start.1
  175.6 1.2 copy-start

commit v2 on v0

--- a/solution.py
+++ b/solution.py
@@ -1,18 +1,1071 @@
+import functools
 import math
+import types
 
 import jax
 import jax.numpy as jnp
+import numpy as np
 from jax import lax
+from jax.experimental import pallas as pl
+from jax.experimental.pallas import tpu as pltpu
 from jax.sharding import PartitionSpec as P
 
 HEADS = 16
 HDIM = 64
 GRID = 14
 VIS_DEV = 64
-
-
 norm_eps = 1e-06
 masked_fill = -1e30
+FRAMES = 8
+EPS = 1e-06
+FILL = -1e30
+BF = jnp.bfloat16
+F32 = jnp.float32
+MESH = pl.DeviceIdType.MESH
+NT = (((1,), (1,)), ((), ()))
+NN = (((1,), (0,)), ((), ()))
+TN = (((0,), (0,)), ((), ()))
+
+
+def dot(a, b, dims=NN):
+    return lax.dot_general(a, b, dims, preferred_element_type=F32)
+
+
+def trig_table():
+    width = FRAMES + 2 * GRID
+    lane = np.arange(2 * HDIM)
+    pair = lane % (HDIM // 2)
+    axis = np.minimum(pair // 11, 2)
+    freq = np.exp(((pair - 11 * axis).astype(np.float32)) * np.float32(-math.log(10000.0) / 11.0))
+    sign = np.where(lane % HDIM < HDIM // 2, -1.0, 1.0)
+    table = np.zeros((128, 4 * HDIM), np.float32)
+    row = np.arange(width)
+    kind = np.where(row < FRAMES, 0, np.where(row < FRAMES + GRID, 1, 2))
+    coord = np.where(kind == 0, row, np.where(kind == 1, row - FRAMES, row - FRAMES - GRID))
+    angle = (coord[:, None].astype(np.float32) * freq[None, :].astype(np.float32)).astype(np.float64)
+    here = kind[:, None] == axis[None, :]
+    table[:width, : 2 * HDIM] = np.where(here, np.cos(angle), 0.0)
+    table[:width, 2 * HDIM :] = np.where(here, np.sin(angle) * sign[None, :], 0.0)
+    parts = []
+    rest = table
+    for _ in range(3):
+        part = rest.astype(jnp.bfloat16)
+        parts.append(part)
+        rest = rest - part.astype(np.float32)
+    return np.stack(parts)
+
+
+def norm_stats(v):
+    center = v - jnp.mean(v, axis=-1, keepdims=True)
+    inv = lax.rsqrt(jnp.mean(center * center, axis=-1, keepdims=True) + EPS)
+    return center * inv, inv
+
+
+def norm_back(v, gain, grad):
+    xhat, inv = norm_stats(v)
+    gg = grad * gain
+    dv = inv * (
+        gg - jnp.mean(gg, axis=-1, keepdims=True) - xhat * jnp.mean(gg * xhat, axis=-1, keepdims=True)
+    )
+    return (
+        dv,
+        jnp.sum(grad * xhat, axis=0, keepdims=True),
+        jnp.sum(grad, axis=0, keepdims=True),
+    )
+
+
+def swap_halves(u):
+    lane = lax.broadcasted_iota(jnp.int32, u.shape, 1)
+    return jnp.where(
+        lax.rem(lane, HDIM) < HDIM // 2,
+        pltpu.roll(u, u.shape[1] - HDIM // 2, 1),
+        pltpu.roll(u, HDIM // 2, 1),
+    )
+
+
+def column_segment(start, rows, ends):
+    row = start + lax.broadcasted_iota(jnp.int32, (rows, 1), 0)
+    seg = jnp.zeros((rows, 1), jnp.int32)
+    for end in ends:
+        seg += (row >= end).astype(jnp.int32)
+    return row, seg
+
+
+ALIASES = dict(N2="N1", PT="N1", D2="w2_v", D1="w1_v", DOo="wo_v", DQo="wqkv_v")
+
+
+class Sems:
+    def __init__(self, send, recv):
+        self.send, self.recv, self.used = send, recv, 0
+
+    def take(self):
+        at = self.used
+        self.used += 1
+        return self.send.at[at], self.recv.at[at]
+
+
+def layer_kernel(dims, names, *refs):
+    n, D, FF, T, V = dims
+    NF = 4
+    R = D // (n * NF)
+    RP = R * NF
+    HC = FF // (NF * n)
+    HF = FF // NF
+    C = D // NF
+    VP = V * NF
+    S_ = T * NF
+    last = n // 2 - 1
+    given = dict(zip(names, refs))
+    g = types.SimpleNamespace(**given, **{a: given[b] for a, b in ALIASES.items()})
+    sems = Sems(g.send_sems, g.recv_sems)
+    lsem = g.local_sems
+
+    p = lax.axis_index("dp")
+    f = lax.axis_index("fsdp")
+    f1 = f + 1 - 2 * lax.rem(f, 2)
+    f2 = lax.rem(f + 2, NF)
+    f3 = NF - 1 - f
+    par = lax.rem(p, 2)
+    half_p = lax.div(p, 2)
+    pos = (1 - par) * half_p + par * (n - 1 - half_p)
+
+    def idx(q):
+        q = lax.rem(q + 2 * n, n)
+        up = lax.div(q, n // 2)
+        return (1 - up) * (2 * q) + up * (2 * (n - 1 - q) + 1)
+
+    right, left = idx(pos + 1), idx(pos - 1)
+
+    pending = []
+
+    def remote(src, dst, to):
+        ss, rs = sems.take()
+        c = pltpu.make_async_remote_copy(
+            src_ref=src, dst_ref=dst, send_sem=ss, recv_sem=rs, device_id=to, device_id_type=MESH
+        )
+        c.start()
+        pending.append(c)
+        return c, ss, rs
+
+    def drain(*copies):
+        for c in copies:
+            pending[:] = [d for d in pending if d is not c]
+            c.wait_send()
+
+    def arrival(dst, ss, rs, to):
+        return pltpu.make_async_remote_copy(
+            src_ref=dst, dst_ref=dst, send_sem=ss, recv_sem=rs, device_id=to, device_id_type=MESH
+        )
+
+    to1, to2, to3 = {"fsdp": f1}, {"fsdp": f2}, {"fsdp": f3}
+    peers = ((f1, to1), (f2, to2), (f3, to3))
+
+    loads = {}
+    for i, (src, dst) in enumerate(
+        (
+            (g.wqkv, g.wqkv_v),
+            (g.w1, g.w1_v),
+            (g.wo, g.wo_v),
+            (g.small, g.small_v),
+            (g.tok, g.TA.at[f]),
+            (g.w2, g.w2_v),
+            (g.cot, g.CA.at[f]),
+            (g.trig, g.trig_v),
+        )
+    ):
+        c = pltpu.make_async_copy(src, dst, lsem.at[i])
+        c.start()
+        loads[i] = c
+
+    barrier = pltpu.get_barrier_semaphore()
+    for to in (to1, to2, to3, {"dp": right}, {"dp": left}):
+        pl.semaphore_signal(barrier, inc=1, device_id=to, device_id_type=MESH)
+
+    AS, AQ, WO, A1, A2 = g.AS, g.AQ, g.WO, g.A1, g.A2
+    TA, CA = g.TA, g.CA
+
+    loads[0].wait()
+    for j in range(NF):
+        for t in range(3):
+            g.sq[j, :, C * t : C * t + C] = g.wqkv_v[:, D * t + C * j : D * t + C * j + C].astype(BF)
+    AQ[p, pl.ds(pl.multiple_of(R * f, R), R), :] = g.sq[f]
+    loads[3].wait()
+    AS[p, f] = g.small_v[...]
+    loads[5].wait()
+    A2[p] = g.w2_v[...].astype(BF)
+    loads[2].wait()
+    WO[p, f] = g.wo_v[...].astype(BF)
+    pl.semaphore_wait(barrier, 5)
+
+    def scatter(src, dst):
+        got = []
+        for fj, to in peers:
+            _, ss, rs = remote(src(fj), dst(f), to)
+            got.append(arrival(dst(fj), ss, rs, to))
+        return got
+
+    class AllGather4:
+        def __init__(self, slot):
+            self.slot = slot
+            _, ss, rs = remote(slot(f), slot(f), to2)
+            self.across = arrival(slot(f2), ss, rs, to2)
+            _, ss, rs = remote(slot(f), slot(f), to1)
+            self.beside = arrival(slot(f1), ss, rs, to1)
+
+        def forward(self):
+            self.done = False
+            self.across.wait_recv()
+            _, ss, rs = remote(self.slot(f2), self.slot(f2), to1)
+            self.passed = arrival(self.slot(f3), ss, rs, to1)
+
+        def finish(self):
+            if not self.done:
+                self.done = True
+                self.beside.wait_recv()
+                self.passed.wait_recv()
+
+    class ReduceScatter4:
+        def __init__(self, part, r1, xs, r2):
+            self.part, self.r1, self.xs, self.r2 = part, r1, xs, r2
+            self.ca, ss, rs = remote(part.at[f3], r1.at[1], to1)
+            self.other = arrival(r1.at[1], ss, rs, to1)
+            self.cb, ss, rs = remote(part.at[f1], r1.at[0], to1)
+            self.own = arrival(r1.at[0], ss, rs, to1)
+
+        def forward(self):
+            self.other.wait_recv()
+            self.xs[...] = (self.part[f2].astype(F32) + self.r1[1].astype(F32)).astype(BF)
+            _, ss, rs = remote(self.xs, self.r2, to2)
+            self.across = arrival(self.r2, ss, rs, to2)
+
+        def finish(self):
+            self.own.wait_recv()
+            self.across.wait_recv()
+
+        def total(self):
+            return self.part[f].astype(F32) + self.r1[0].astype(F32) + self.r2[...].astype(F32)
+
+    class RingGather:
+        def __init__(self, view, rows):
+            self.view, self.rows = view, rows
+            self.arrivals = []
+
+        def step(self, r):
+            for a in self.arrivals:
+                a.wait_recv()
+            self.arrivals = []
+            h = self.rows // 2
+            spans = ((0, self.rows), (0, self.rows)) if r < last else ((0, h), (h, h))
+            for way, (s, c) in zip((1, -1), spans):
+                to, frm = ({"dp": right}, {"dp": left}) if way == 1 else ({"dp": left}, {"dp": right})
+                mine = self.view(idx(pos - way * r), s, c)
+                _, ss, rs = remote(mine, mine, to)
+                self.arrivals.append(arrival(self.view(idx(pos - way * (r + 1)), s, c), ss, rs, frm))
+
+        def finish(self):
+            for a in self.arrivals:
+                a.wait_recv()
+            self.arrivals = []
+
+    def rows_view(ref, offset):
+        return lambda slot, s, c: ref.at[slot, pl.ds(offset + s, c), :]
+
+    h = RP // 2
+    q_ring = [RingGather(rows_view(AQ, 0), h), RingGather(rows_view(AQ, h), h)]
+    w1_ring = [RingGather(rows_view(A1, 0), h), RingGather(rows_view(A1, h), h)]
+    w2_ring = [RingGather(rows_view(A2, 0), HC // 2), RingGather(rows_view(A2, HC // 2), HC // 2)]
+    o_ring = RingGather(lambda slot, s, c: WO.at[slot, f, pl.ds(s, c), :], R)
+    s_ring = RingGather(lambda slot, s, c: AS.at[slot, pl.ds(s, c)], NF)
+
+    class RingReduce:
+        def __init__(self, grads, start, rows, st, rr, rl, wire=BF):
+            self.G, self.o, self.rows, self.st, self.rr, self.rl = grads, start, rows, st, rr, rl
+            self.wire = wire
+            self.arrivals = []
+
+        def piece(self, ref, slot, s, c):
+            return ref.at[slot, pl.ds(self.o + s, c), :]
+
+        def step(self, r):
+            for a in self.arrivals:
+                a.wait_recv()
+            self.arrivals = []
+            o, rows = self.o, self.rows
+            hh = rows // 2
+            if r == 0:
+                far = idx(pos + n // 2)
+                self.st[pl.ds(o, rows), :] = self.G[far, pl.ds(o, rows), :].astype(self.wire)
+                for buf, s, to, frm in (
+                    (self.rr, 0, {"dp": right}, {"dp": left}),
+                    (self.rl, hh, {"dp": left}, {"dp": right}),
+                ):
+                    dst = self.piece(buf, 0, s, hh)
+                    _, ss, rs = remote(self.st.at[pl.ds(o + s, hh), :], dst, to)
+                    self.arrivals.append(arrival(dst, ss, rs, frm))
+                return
+            for way, buf, s, to, frm in (
+                (1, self.rr, 0, {"dp": right}, {"dp": left}),
+                (-1, self.rl, hh, {"dp": left}, {"dp": right}),
+            ):
+                c = idx(pos + way * (n // 2 - r))
+                if r == 1:
+                    other = hh - s
+                    buf[0, pl.ds(o + s, hh), :] = (
+                        buf[0, pl.ds(o + s, hh), :].astype(F32) + self.G[c, pl.ds(o + s, hh), :]
+                    ).astype(self.wire)
+                    buf[0, pl.ds(o + other, hh), :] = self.G[c, pl.ds(o + other, hh), :].astype(self.wire)
+                else:
+                    buf[r - 1, pl.ds(o, rows), :] = (
+                        buf[r - 1, pl.ds(o, rows), :].astype(F32) + self.G[c, pl.ds(o, rows), :]
+                    ).astype(self.wire)
+                src, dst = self.piece(buf, r - 1, 0, rows), self.piece(buf, r, 0, rows)
+                _, ss, rs = remote(src, dst, to)
+                self.arrivals.append(arrival(dst, ss, rs, frm))
+
+        def finish(self):
+            for a in self.arrivals:
+                a.wait_recv()
+            self.arrivals = []
+
+        def total(self):
+            o, rows = self.o, self.rows
+            return (
+                self.G[p, pl.ds(o, rows), :]
+                + self.rr[last, pl.ds(o, rows), :].astype(F32)
+                + self.rl[last, pl.ds(o, rows), :].astype(F32)
+            )
+
+    st = types.SimpleNamespace(oa=[None, None])
+    N1, N2, GT, PT = g.N1, g.N2, g.GT, g.PT
+    VEC, BQ, BG, VG = g.VEC, g.BQ, g.BG, g.VG
+    Q, K, W, QV, KV, WV = g.Q, g.K, g.W, g.QV, g.KV, g.WV
+    SM, OV, PV, OA, OT = g.SM, g.OV, g.PV, g.OA, g.OT
+    XV, N1V, DY, X1V, N2V = g.XV, g.N1V, g.DY, g.X1V, g.N2V
+    GV, GP, DH, PN, PF = g.GV, g.GP, g.DH, g.PN, g.PF
+    G2, G1, GQ, GO = g.G2, g.G1, g.GQ, g.GO
+    DO, DPRE = g.DO, g.DPRE
+    E1, F1, EQ, FQ, SG = g.E1, g.F1, g.EQ, g.FQ, g.SG
+    blocks = [slice(256 * k, 256 * k + 256) for k in range(D // 256)]
+    mine = pl.ds(pl.multiple_of(V * f, V), V)
+    hc, hr = HC // 2, RP // 2
+    g2_ring = [
+        RingReduce(G2, 0, hc, g.st2, g.rr2, g.rl2),
+        RingReduce(G2, hc, hc, g.st2, g.rr2, g.rl2),
+    ]
+    g1_ring = [
+        RingReduce(G1, 0, hr, g.st1, g.rr1, g.rl1),
+        RingReduce(G1, hr, hr, g.st1, g.rr1, g.rl1),
+    ]
+    gq_ring = [
+        RingReduce(GQ, 0, hr, g.stq, g.rrq, g.rlq),
+        RingReduce(GQ, hr, hr, g.stq, g.rrq, g.rlq),
+    ]
+    go_ring = RingReduce(GO, 0, R, g.sto, g.rro, g.rlo)
+    gs_ring = RingReduce(VG, 0, 16, g.sts, g.rrs, g.rls, F32)
+
+    def finish(*rings):
+        for r in rings:
+            r.finish()
+
+    def received(copies):
+        for c in copies:
+            c.wait_recv()
+
+    outs = []
+
+    def store(src, dst, k):
+        c = pltpu.make_async_copy(src, dst, lsem.at[8 + k])
+        c.start()
+        outs.append(c)
+
+    def vec(k):
+        return VEC[k : k + 1, :]
+
+    def start():
+        st.q = scatter(lambda j: g.sq.at[j], lambda j: AQ.at[p, pl.ds(pl.multiple_of(R * j, R), R), :])
+        st.s = scatter(lambda j: AS.at[p, f], lambda j: AS.at[p, j])
+        q_ring[0].arrivals = list(st.q)
+        s_ring.arrivals = st.s
+
+    def cast_fc1():
+        loads[1].wait()
+        for j in range(NF):
+            for t in range(n):
+                at = HC * (NF * t + j)
+                g.s1[j, :, HC * t : HC * t + HC] = g.w1_v[:, at : at + HC].astype(BF)
+        A1[p, pl.ds(pl.multiple_of(R * f, R), R), :] = g.s1[f]
+        st.w1 = scatter(lambda j: g.s1.at[j], lambda j: A1.at[p, pl.ds(pl.multiple_of(R * j, R), R), :])
+        w1_ring[0].arrivals = list(st.w1)
+
+    def tokens_start():
+        loads[4].wait()
+        st.tok = AllGather4(lambda j: TA.at[j])
+
+    def cot_start():
+        loads[6].wait()
+        st.cot = AllGather4(lambda j: CA.at[j])
+
+    def wo_start():
+        o_ring.finish()
+        st.wo = AllGather4(lambda j: WO.at[:, j])
+
+    ends = []
+    total_len = jnp.int32(0)
+    for k in range(g.lengths.shape[1]):
+        total_len = total_len + g.lengths[0, k]
+        ends.append(total_len)
+
+    def key_segments():
+        keyrow = lax.broadcasted_iota(jnp.int32, (1, S_), 1)
+        segrow = jnp.zeros((1, S_), jnp.int32)
+        for end in ends:
+            segrow += (keyrow >= end).astype(jnp.int32)
+        return segrow
+
+    def layout():
+        row, _seg = column_segment(0, S_, ends)
+        before = jnp.zeros((S_, 1), jnp.int32)
+        for k, end in enumerate(ends):
+            before += jnp.where(row >= end, g.lengths[0, k], 0)
+        place = row - before
+        img = GRID * GRID
+        frame = jnp.zeros((S_, 1), jnp.int32)
+        for t in range(1, FRAMES):
+            frame += (place >= img * t).astype(jnp.int32)
+        rest = place - img * frame
+        grow = jnp.zeros((S_, 1), jnp.int32)
+        for t in range(1, GRID):
+            grow += (rest >= GRID * t).astype(jnp.int32)
+        gcol = rest - GRID * grow
+        lane = lax.broadcasted_iota(jnp.int32, (S_, 128), 1)
+        hot = (lane == frame) | (lane == grow + FRAMES) | (lane == gcol + (FRAMES + GRID))
+        g.OH[...] = jnp.where(hot, 1.0, 0.0).astype(BF)
+        loads[7].wait()
+        g.CS[...] = sum(dot(g.OH[...], g.trig_v[k]) for k in range(3))
+
+    def visible():
+        if s_ring.arrivals is st.s:
+            received(st.s)
+            s_ring.arrivals = []
+        vis8 = jnp.concatenate([AS[p, j][4:6, :] for j in range(NF)], axis=0)
+        above = lax.broadcasted_iota(jnp.int32, (128, 128), 0)
+        tri = above <= lax.broadcasted_iota(jnp.int32, (128, 128), 1)
+        within = dot(vis8.astype(BF), jnp.where(tri, 1.0, 0.0).astype(BF))
+        base = jnp.zeros((1, 128), F32)
+        pieces, vpieces = [], []
+        for k in range(8):
+            pieces.append(within[k : k + 1, :] + base)
+            vpieces.append(vis8[k : k + 1, :])
+            base = base + jnp.sum(vis8[k : k + 1, :], axis=1, keepdims=True)
+        incl = jnp.concatenate(pieces, axis=1)
+        visrow = jnp.concatenate(vpieces, axis=1)
+        rank = jnp.where(visrow > 0.5, incl - 1.0, -1.0).astype(jnp.int32)
+        sel = lax.broadcasted_iota(jnp.int32, (VP, S_), 0) == rank
+        SM[...] = jnp.where(sel, 1.0, 0.0).astype(BF)
+
+    def rounded(v):
+        return v.astype(BF).astype(F32)
+
+    def turn(v, by):
+        by = by % 128
+        return v if by == 0 else pltpu.roll(v, by, 1)
+
+    def small_vectors():
+        s_ring.finish()
+        lane128 = lax.broadcasted_iota(jnp.int32, (n, 128), 1)
+        rows0 = [AS[:, j, 0, :] for j in range(NF)]
+        rows1 = [AS[:, j, 1, :] for j in range(NF)]
+        rows2 = [AS[:, j, 2, :] for j in range(NF)]
+        for k in range(6):
+            src = rows0 if k < 4 else rows1
+            piece = jnp.zeros((n, 128), F32)
+            for j in range(NF):
+                piece = jnp.where(lax.div(lane128, R) == j, turn(src[j], R * (j - k % 4)), piece)
+            for q in range(n):
+                VEC[k : k + 1, 128 * q : 128 * q + 128] = rounded(piece[q : q + 1, :])
+        for q in range(n):
+            VEC[6:7, 128 * q : 128 * q + 128] = rounded(AS[q, f][3:4, :])
+        t0 = jnp.where(lane128 < 96, rows2[0], turn(rows2[1], 96))
+        t1 = jnp.where(lane128 < 64, turn(rows2[1], -32), turn(rows2[2], 64))
+        t2 = jnp.where(lane128 < 32, turn(rows2[2], -64), turn(rows2[3], 32))
+        for q in range(n):
+            for k, t in enumerate((t0, t1, t2)):
+                BQ[0:1, 384 * q + 128 * k : 384 * q + 128 * k + 128] = rounded(t[q : q + 1, :])
+
+    def first_norm():
+        st.tok.finish()
+
+        def block(b, _):
+            xhat, _inv = norm_stats(TA[b].astype(F32))
+            N1[b] = (xhat * vec(0) + vec(1)).astype(BF)
+            return 0
+
+        lax.fori_loop(0, NF, block, 0)
+
+    def project_half(part):
+        finish(*q_ring)
+
+        def block(b, _):
+            rows = pl.ds(pl.multiple_of(b * T, T), T)
+            cs = g.CS[rows, :]
+            for t, dst in enumerate((Q, K, W)):
+                out = dot(N1[b], AQ[:, :, C * t : C * t + C].reshape(D, C))
+                out = out + BQ[0:1, pl.ds(pl.multiple_of(D * t + C * f, 128), C)]
+                if t == 2:
+                    dst[rows, :] = out.astype(BF)
+                    continue
+                for hh in range(C // 128):
+                    u = out[:, 128 * hh : 128 * hh + 128]
+                    u = (u * cs[:, :128] + swap_halves(u) * cs[:, 128:]).astype(BF)
+                    dst[rows, 128 * hh : 128 * hh + 128] = u * BF(0.125) if t == 0 else u
+            return 0
+
+        lax.fori_loop(NF // 2 * part, NF // 2 * (part + 1), block, 0)
+
+    lane_c = lax.broadcasted_iota(jnp.int32, (1, C), 1)
+    hmask = [jnp.where(lax.div(lane_c, HDIM) == hd, 1.0, 0.0) for hd in range(C // HDIM)]
+
+    def softmax(s):
+        e = jnp.exp(s - jnp.max(s, axis=-1, keepdims=True))
+        return e * (1.0 / jnp.sum(e, axis=-1, keepdims=True))
+
+    def context_attention():
+        for src, dst in ((Q, QV), (K, KV), (W, WV)):
+            dst[...] = dot(SM[...], src[...]).astype(BF)
+        segrow = key_segments()
+        seg8 = jnp.broadcast_to(segrow.astype(F32), (8, S_)).astype(BF)
+        segv_row = dot(seg8, SM[...], NT)[0:1, :].astype(jnp.int32)
+        segv_col = jnp.sum(SM[...].astype(F32) * segrow.astype(F32), axis=1, keepdims=True).astype(jnp.int32)
+        same = segv_col == segv_row
+        acc = jnp.zeros((VP, C), F32)
+        for hd in range(C // HDIM):
+            s = dot(QV[...] * hmask[hd].astype(BF), KV[...], NT)
+            pr = softmax(jnp.where(same, s, FILL))
+            PV[hd] = pr
+            acc += dot(pr.astype(BF), WV[...]) * hmask[hd]
+        OV[f] = acc.astype(BF)
+        st.ov = AllGather4(lambda j: OV.at[j])
+
+    def attend_target(b, pair):
+        rows = slice(T * b, T * b + T)
+        _, segq = column_segment(b * T, T, ends)
+        same = segq == key_segments()
+        for hd in (2 * pair, 2 * pair + 1):
+            s = dot(Q[rows, :] * hmask[hd].astype(BF), K[...], NT)
+            pr = softmax(jnp.where(same, s, FILL)).astype(BF)
+            o = dot(pr, W[...])
+            cols = slice(HDIM * hd, HDIM * hd + HDIM)
+            OA[f, rows, cols] = o[:, cols].astype(BF)
+
+    def oa_start(part):
+        rows = pl.ds(S_ // 2 * part, S_ // 2)
+        st.oa[part] = AllGather4(lambda j: OA.at[j, rows, :])
+
+    def select_rows():
+        for cols in blocks:
+            XV[:, cols] = dot(SM[...], TA[:, :, cols].reshape(S_, 256)).astype(BF)
+            N1V[:, cols] = dot(SM[...], N1[:, :, cols].reshape(S_, 256)).astype(BF)
+
+    def select_cot():
+        st.cot.finish()
+        for cols in blocks:
+            DY[:, cols] = dot(SM[...], CA[:, :, cols].reshape(S_, 256)).astype(BF)
+
+    def out_project(parts, cols):
+        heads = [WO[n // NF * j : n // NF * (j + 1), :, :, cols].reshape(C, -1) for j in range(NF)]
+        return sum(dot(parts(j), heads[j]) for j in range(NF))
+
+    def context_middle():
+        st.wo.finish()
+        st.ov.finish()
+        for cols in blocks:
+            X1V[:, cols] = XV[:, cols].astype(F32) + (out_project(lambda j: OV[j], cols) + VEC[4:5, cols])
+        xhat, _inv = norm_stats(X1V[...])
+        N2V[...] = (xhat * vec(2) + vec(3)).astype(BF)
+
+    def normal_cdf(hid):
+        return 0.5 * (1.0 + lax.erf(hid * (1.0 / math.sqrt(2.0))))
+
+    def context_hidden():
+        finish(*w1_ring)
+        for cols in blocks:
+            hid = dot(N2V[...], A1[:, :, cols].reshape(D, 256)) + VEC[6:7, cols]
+            cdf = normal_cdf(hid)
+            GV[:, cols] = (hid * cdf).astype(BF)
+            GP[:, cols] = cdf + hid * (jnp.exp(-0.5 * hid * hid) * (1.0 / math.sqrt(2.0 * math.pi)))
+
+    def outer(dst, lhs, rhs):
+        def one(k, _):
+            a = lhs[:, pl.ds(pl.multiple_of(128 * k, 128), 128)]
+            dst[k] = dot(a, rhs[...], TN)
+            return 0
+
+        lax.fori_loop(0, n, one, 0)
+
+    def put_grad(k, vrow):
+        for q in range(n):
+            VG[q, k : k + 1, :] = vrow[:, 128 * q : 128 * q + 128]
+
+    def fc2_grad():
+        outer(G2, GV, DY)
+
+    def hidden_grad():
+        finish(*w2_ring)
+        for k, cols in enumerate(blocks):
+            dg = dot(DY[...], A2[...].reshape(HF, D)[256 * k : 256 * k + 256, :], NT)
+            dh = (dg * GP[:, cols]).astype(BF)
+            DH[:, cols] = dh
+            dc1 = jnp.sum(dh.astype(F32), axis=0, keepdims=True)
+            for q in range(2):
+                for j in range(NF):
+                    piece = dc1[:, 128 * q : 128 * q + 128]
+                    VG[2 * k + q, 9 + j : 10 + j, :] = jnp.where(f == j, piece, jnp.zeros((1, 128), F32))
+
+    def second_grad():
+        for k, cols in enumerate(blocks):
+            part = dot(DH[...], A1[2 * k : 2 * k + 2].reshape(256, HF), NT).astype(BF)
+            PN[:, :, cols] = part.reshape(NF, V, 256)
+        st.n2 = ReduceScatter4(PN, g.PNr1, g.PNxs, g.PNr2)
+
+    def fc1_grad():
+        outer(G1, N2V, DH)
+
+    def context_partial():
+        for cols in blocks:
+            part = dot(GV[...], A2[:, :, cols].reshape(HF, 256)).astype(BF)
+            PF[:, :, cols] = part.reshape(NF, V, 256)
+        st.pf = ReduceScatter4(PF, g.PFr1, g.PFxs, g.PFr2)
+
+    def second_norm_back():
+        st.n2.finish()
+        dyo = DY[mine, :].astype(F32)
+        dv, dgain, dshift = norm_back(X1V[mine, :], vec(2), st.n2.total())
+        dx1 = dyo + dv
+        g.DX1[...] = dx1
+        low = dx1.astype(BF)
+        g.DP[f] = low
+        st.dp = AllGather4(lambda j: g.DP.at[j])
+        put_grad(2, dgain)
+        put_grad(3, dshift)
+        put_grad(4, jnp.sum(low.astype(F32), axis=0, keepdims=True))
+        put_grad(5, jnp.sum(dyo, axis=0, keepdims=True))
+
+    def transpose_attended():
+        st.ov.finish()
+        for j in range(NF):
+            ot = OV[j].astype(F32).T.astype(BF)
+            OT[n // NF * j : n // NF * (j + 1)] = ot.reshape(n // NF, NF, R, VP)
+
+    def out_grad():
+        st.dp.finish()
+        go = dot(OT[:, f].reshape(n * R, VP), g.DP[...].reshape(VP, D))
+        GO[...] = go.reshape(n, R, D)
+
+    def attended_grad():
+        st.dp.finish()
+        st.wo.finish()
+        wo_heads = WO[pl.ds(n // NF * f, n // NF)].reshape(C, D)
+        DO[...] = dot(g.DP[...].reshape(VP, D), wo_heads, NT).astype(BF)
+
+    def attention_back():
+        dq = jnp.zeros((VP, C), F32)
+        dk = jnp.zeros((VP, C), F32)
+        dw = jnp.zeros((VP, C), F32)
+        for hd in range(C // HDIM):
+            pr = PV[hd]
+            dp = dot(DO[...] * hmask[hd].astype(BF), WV[...], NT)
+            ds = (pr * (dp - jnp.sum(pr * dp, axis=-1, keepdims=True))).astype(BF)
+            dq += dot(ds, KV[...]) * hmask[hd]
+            dk += dot(ds, QV[...], TN) * hmask[hd]
+            dw += dot(pr.astype(BF), DO[...], TN) * hmask[hd]
+        csv = sum(dot(dot(SM[...], g.OH[...]).astype(BF), g.trig_v[k]) for k in range(3))
+        for t, (grad, scale) in enumerate(((dq, 0.125), (dk, 1.0))):
+            for hh in range(C // 128):
+                u = grad[:, 128 * hh : 128 * hh + 128]
+                u = u * csv[:, :128] - swap_halves(u) * csv[:, 128:]
+                DPRE[:, C * t + 128 * hh : C * t + 128 * hh + 128] = (u * scale).astype(BF)
+        DPRE[:, 2 * C :] = dw.astype(BF)
+
+    def qkv_grad():
+        outer(GQ, N1V, DPRE)
+
+    def qkv_bias_grad():
+        BG[...] = jnp.zeros(BG.shape, F32)
+        db = jnp.sum(DPRE[...].astype(F32), axis=0, keepdims=True)
+        for t in range(3):
+            BG[0:1, pl.ds(pl.multiple_of(D * t + C * f, 128), C)] = db[:, C * t : C * t + C]
+        for q in range(n):
+            for t in range(3):
+                VG[q, 6 + t : 7 + t, :] = BG[0:1, 384 * q + 128 * t : 384 * q + 128 * t + 128]
+            VG[q, 13:16, :] = jnp.zeros((3, 128), F32)
+
+    def first_grad():
+        drain(st.n2.ca, st.n2.cb)
+        for k, cols in enumerate(blocks):
+            part = dot(DPRE[...], AQ[2 * k : 2 * k + 2].reshape(256, 3 * C), NT).astype(BF)
+            PN[:, :, cols] = part.reshape(NF, V, 256)
+        st.n1 = ReduceScatter4(PN, g.PMr1, g.PMxs, g.PMr2)
+
+    def first_norm_back():
+        st.n1.finish()
+        dv, dgain, dshift = norm_back(XV[mine, :].astype(F32), vec(0), st.n1.total())
+        g.DX[f] = (g.DX1[...] + dv).astype(BF)
+        st.dx = AllGather4(lambda j: g.DX.at[j])
+        put_grad(0, dgain)
+        put_grad(1, dshift)
+
+    def context_result():
+        st.pf.finish()
+        g.CO[f] = (X1V[mine, :] + (st.pf.total() + vec(5))).astype(BF)
+        st.co = AllGather4(lambda j: g.CO.at[j])
+
+    def home(src, dst):
+        s = SM[:, pl.ds(pl.multiple_of(T * f, 128), T)]
+        for cols in blocks:
+            dst[:, cols] = dot(s, src[:, :, cols].reshape(VP, 256), TN).astype(BF)
+
+    def home_context():
+        st.co.finish()
+        home(g.CO, g.CH)
+        store(g.CH, g.ctx_o, 0)
+
+    def home_grad():
+        st.dx.finish()
+        home(g.DX, g.DXH)
+        store(g.DXH, g.dx_o, 1)
+
+    def target_middle(b):
+        st.wo.finish()
+        st.oa[b // 2].finish()
+        for cols in blocks:
+            g.X1B[:, cols] = TA[b, :, cols].astype(F32) + (
+                out_project(lambda j: OA[j, T * b : T * b + T, :], cols) + VEC[4:5, cols]
+            )
+        x1 = g.X1B[...]
+        xh, _inv = norm_stats(x1)
+        N2[b] = (xh * vec(2) + vec(3)).astype(BF)
+
+        @pl.when(f == b)
+        def _():
+            g.X1H[...] = x1
+
+    def target_hidden(b):
+        finish(*w1_ring)
+        for cols in blocks:
+            hid = dot(N2[b], A1[:, :, cols].reshape(D, 256)) + VEC[6:7, cols]
+            GT[b, :, cols] = (hid * normal_cdf(hid)).astype(BF)
+
+    def target_out(b):
+        finish(*w2_ring)
+        for cols in blocks:
+            PT[b, :, cols] = dot(GT[b], A2[:, :, cols].reshape(HF, 256)).astype(BF)
+        if b == NF - 1:
+            st.pt = ReduceScatter4(PT, g.PTr1, g.PTxs, g.PTr2)
+
+    def target_result():
+        st.pt.finish()
+        g.TO[...] = (g.X1H[...] + (st.pt.total() + vec(5))).astype(BF)
+        store(g.TO, g.tgt_o, 3)
+
+    def fc2_grad_done():
+        finish(*g2_ring)
+        for k, ring in enumerate(g2_ring):
+            g.D2[hc * k : hc * k + hc, :] = ring.total()
+        store(g.D2, g.g2_o, 2)
+
+    def fc1_grad_trade():
+        finish(*g1_ring)
+        for k, ring in enumerate(g1_ring):
+            E1[2 * k : 2 * k + 2] = ring.total().astype(BF).reshape(2, R, HF)
+        F1[f] = E1[f]
+        st.e1 = scatter(lambda j: E1.at[j], lambda j: F1.at[j])
+
+    def fc1_grad_done():
+        received(st.e1)
+        for j in range(NF):
+            for t in range(n):
+                at = HC * (NF * t + j)
+                g.D1[:, at : at + HC] = F1[j, :, HC * t : HC * t + HC].astype(F32)
+        store(g.D1, g.g1_o, 5)
+
+    def out_grad_done():
+        go_ring.finish()
+        g.DOo[...] = go_ring.total()
+        store(g.DOo, g.go_o, 4)
+
+    def qkv_grad_trade():
+        finish(*gq_ring)
+        for k, ring in enumerate(gq_ring):
+            EQ[2 * k : 2 * k + 2] = ring.total().astype(BF).reshape(2, R, 3 * C)
+        FQ[f] = EQ[f]
+        st.eq = scatter(lambda j: EQ.at[j], lambda j: FQ.at[j])
+
+    def qkv_grad_done():
+        received(st.eq)
+        for j in range(NF):
+            for t in range(3):
+                g.DQo[:, D * t + C * j : D * t + C * j + C] = FQ[j, :, C * t : C * t + C].astype(F32)
+        store(g.DQo, g.gq_o, 7)
+
+    def small_grad_trade():
+        gs_ring.finish()
+        SG[f] = gs_ring.total()
+        st.sg = scatter(lambda j: SG.at[f], lambda j: SG.at[j])
+
+    def small_grad_done():
+        received(st.sg)
+        g.SGo[...] = SG[0] + SG[1] + SG[2] + SG[3]
+        store(g.SGo, g.sg_o, 6)
+
+    start()
+    cast_fc1()
+    tokens_start()
+    cot_start()
+    o_ring.step(0)
+    w2_ring[0].step(0)
+    layout()
+    w2_ring[1].step(0)
+    o_ring.step(1)
+    q_ring[0].step(0)
+    q_ring[1].step(0)
+    s_ring.step(0)
+    visible()
+    w1_ring[0].step(0)
+    o_ring.step(2)
+    q_ring[0].step(1)
+    q_ring[1].step(1)
+    s_ring.step(1)
+    w1_ring[0].step(1)
+    st.tok.forward()
+    o_ring.step(3)
+    q_ring[0].step(2)
+    q_ring[1].step(2)
+    s_ring.step(2)
+    w1_ring[1].step(0)
+    wo_start()
+    w1_ring[0].step(2)
+    q_ring[0].step(3)
+    st.cot.forward()
+    q_ring[1].step(3)
+    s_ring.step(3)
+    select_cot()
+    w1_ring[1].step(1)
+    w1_ring[0].step(3)
+    w2_ring[0].step(1)
+    small_vectors()
+    first_norm()
+    project_half(0)
+    st.wo.forward()
+    w1_ring[1].step(2)
+    project_half(1)
+    context_attention()
+    w2_ring[1].step(1)
+    select_rows()
+    w2_ring[0].step(2)
+    attend_target(0, 0)
+    w1_ring[1].step(3)
+    attend_target(0, 1)
+    st.ov.forward()
+    attend_target(1, 0)
+    w2_ring[1].step(2)
+    context_middle()
+    transpose_attended()
+    w2_ring[0].step(3)
+    attend_target(1, 1)
+    oa_start(0)
+    context_hidden()
+    fc2_grad()
+    g2_ring[0].step(0)
+    g2_ring[1].step(0)
+    w2_ring[1].step(3)
+    attend_target(2, 0)
+    attend_target(2, 1)
+    g2_ring[0].step(1)
+    g2_ring[1].step(1)
+    st.oa[0].forward()
+    attend_target(3, 0)
+    hidden_grad()
+    second_grad()
+    g2_ring[0].step(2)
+    fc1_grad()
+    g1_ring[0].step(0)
+    g1_ring[1].step(0)
+    st.n2.forward()
+    context_partial()
+    target_middle(0)
+    g2_ring[1].step(2)
+    attend_target(3, 1)
+    g2_ring[0].step(3)
+    oa_start(1)
+    second_norm_back()
+    g1_ring[0].step(1)
+    st.pf.forward()
+    target_middle(1)
+    target_hidden(0)
+    g1_ring[1].step(1)
+    target_hidden(1)
+    target_out(0)
+    target_out(1)
+    st.oa[1].forward()
+    g2_ring[1].step(3)
+    target_middle(2)
+    g1_ring[0].step(2)
+    st.dp.forward()
+    target_middle(3)
+    target_hidden(2)
+    g1_ring[1].step(2)
+    attended_grad()
+    attention_back()
+    qkv_grad()
+    gq_ring[0].step(0)
+    gq_ring[1].step(0)
+    out_grad()
+    go_ring.step(0)
+    g1_ring[0].step(3)
+    first_grad()
+    qkv_bias_grad()
+    context_result()
+    target_hidden(3)
+    target_out(2)
+    g1_ring[1].step(3)
+    st.n1.forward()
+    gq_ring[0].step(1)
+    target_out(3)
+    fc2_grad_done()
+    gq_ring[1].step(1)
+    go_ring.step(1)
+    st.co.forward()
+    st.pt.forward()
+    first_norm_back()
+    gs_ring.step(0)
+    home_context()
+    fc1_grad_trade()
+    gq_ring[0].step(2)
+    gq_ring[1].step(2)
+    go_ring.step(2)
+    gs_ring.step(1)
+    gq_ring[0].step(3)
+    gq_ring[1].step(3)
+    target_result()
+    go_ring.step(3)
+    gs_ring.step(2)
+    st.dx.forward()
+    home_grad()
+    qkv_grad_trade()
+    fc1_grad_done()
+    out_grad_done()
+    gs_ring.step(3)
+    small_grad_trade()
+    qkv_grad_done()
+    small_grad_done()
+    for c in outs:
+        c.wait()
+    for c in pending:
+        c.wait_send()
+
+
+def run_layer(n, tokens, cot, lengths, small, wqkv, wo, w1, w2, V):
+    T, D = tokens.shape
+    NF = 4
+    FF = w1.shape[1]
+    R = wo.shape[0]
+    RP = R * NF
+    HC = w2.shape[0]
+    HF = HC * n
+    C = D // NF
+    VP = V * NF
+    S_ = T * NF
+    h2 = n // 2
+    B, F = BF, F32
+    vm = pltpu.VMEM
+    scratch = dict(
+        wqkv_v=vm((R, 3 * D), F), w1_v=vm((R, FF), F), wo_v=vm((R, D), F), w2_v=vm((HC, D), F),
+        small_v=vm((8, 128), F), trig_v=vm((3, 128, 256), B),
+        sq=vm((NF, R, 3 * C), B), s1=vm((NF, R, HF), B),
+        AS=vm((n, NF, 8, 128), F), AQ=vm((n, RP, 3 * C), B), WO=vm((n, NF, R, D), B),
+        A1=vm((n, RP, HF), B), A2=vm((n, HC, D), B),
+        TA=vm((NF, T, D), B), CA=vm((NF, T, D), B), N1=vm((NF, T, D), B),
+        OH=vm((S_, 128), B), CS=vm((S_, 256), F), SM=vm((VP, S_), B),
+        VEC=vm((8, D), F), BQ=vm((8, 3 * D), F), BG=vm((8, 3 * D), F),
+        Q=vm((S_, C), B), K=vm((S_, C), B), W=vm((S_, C), B),
+        QV=vm((VP, C), B), KV=vm((VP, C), B), WV=vm((VP, C), B),
+        OV=vm((NF, VP, C), B), PV=vm((C // HDIM, VP, VP), F), OA=vm((NF, S_, C), B),
+        XV=vm((VP, D), B), N1V=vm((VP, D), B), DY=vm((VP, D), B),
+        X1V=vm((VP, D), F), N2V=vm((VP, D), B), GV=vm((VP, HF), B), GP=vm((VP, HF), F),
+        G2=vm((n, HC, D), F), G1=vm((n, RP, HF), F), GQ=vm((n, RP, 3 * C), F), GO=vm((n, R, D), F),
+        VG=vm((n, 16, 128), F),
+        st2=vm((HC, D), B), rr2=vm((h2, HC, D), B), rl2=vm((h2, HC, D), B),
+        st1=vm((RP, HF), B), rr1=vm((h2, RP, HF), B), rl1=vm((h2, RP, HF), B),
+        stq=vm((RP, 3 * C), B), rrq=vm((h2, RP, 3 * C), B), rlq=vm((h2, RP, 3 * C), B),
+        sto=vm((R, D), B), rro=vm((h2, R, D), B), rlo=vm((h2, R, D), B),
+        sts=vm((16, 128), F), rrs=vm((h2, 16, 128), F), rls=vm((h2, 16, 128), F),
+        DH=vm((VP, HF), B), PN=vm((NF, V, D), B), PF=vm((NF, V, D), B),
+        PNr1=vm((2, V, D), B), PNxs=vm((V, D), B), PNr2=vm((V, D), B),
+        PMr1=vm((2, V, D), B), PMxs=vm((V, D), B), PMr2=vm((V, D), B),
+        PFr1=vm((2, V, D), B), PFxs=vm((V, D), B), PFr2=vm((V, D), B),
+        DX1=vm((V, D), F), DP=vm((NF, V, D), B), OT=vm((n, NF, R, VP), B), DO=vm((VP, C), B),
+        DPRE=vm((VP, 3 * C), B), CO=vm((NF, V, D), B), DX=vm((NF, V, D), B),
+        X1B=vm((T, D), F), X1H=vm((T, D), F), GT=vm((NF, T, HF), B),
+        PTr1=vm((2, T, D), B), PTxs=vm((T, D), B), PTr2=vm((T, D), B),
+        CH=vm((T, D), B), DXH=vm((T, D), B), TO=vm((T, D), B),
+        SG=vm((NF, 16, 128), F), SGo=vm((16, 128), F),
+        E1=vm((NF, R, HF), B), F1=vm((NF, R, HF), B), EQ=vm((NF, R, 3 * C), B), FQ=vm((NF, R, 3 * C), B),
+        send_sems=pltpu.SemaphoreType.DMA((200,)), recv_sems=pltpu.SemaphoreType.DMA((200,)),
+        local_sems=pltpu.SemaphoreType.DMA((16,)),
+    )
+    arr = jax.ShapeDtypeStruct
+    ins = dict(
+        lengths=lengths, tok=tokens, cot=cot, small=small, wqkv=wqkv, wo=wo, w1=w1, w2=w2,
+        trig=jnp.asarray(trig_table()),
+    )
+    outs = dict(
+        tgt_o=arr((T, D), B), ctx_o=arr((T, D), B), dx_o=arr((T, D), B), gq_o=arr((R, 3 * D), F),
+        go_o=arr((R, D), F), g1_o=arr((R, FF), F), g2_o=arr((HC, D), F), sg_o=arr((16, 128), F),
+    )
+    names = [*ins, *outs, *scratch]
+    any_spec = pl.BlockSpec(memory_space=pl.ANY)
+    return pl.pallas_call(
+        functools.partial(layer_kernel, (n, D, FF, T, V), names),
+        out_shape=list(outs.values()),
+        in_specs=[pl.BlockSpec(memory_space=pltpu.SMEM)] + [any_spec] * 8,
+        out_specs=[any_spec] * 8,
+        scratch_shapes=list(scratch.values()),
+        compiler_params=pltpu.CompilerParams(
+            collective_id=0, has_side_effects=True, vmem_limit_bytes=67043328
+        ),
+        name="layer",
+    )(*ins.values())
+
+
+def on_device(
+    tokens, lengths, visibility_mask, visible_counts, ln1_gain, ln1_bias, qkv_weight, qkv_bias,
+    out_weight, out_bias, ln2_gain, ln2_bias, fc1_weight, fc1_bias, fc2_weight, fc2_bias, context_cot,
+):
+    n = lax.axis_size("dp")
+    f = lax.axis_index("fsdp")
+    R = ln1_gain.shape[0]
+    running = jnp.cumsum(visibility_mask)
+    visible = (visibility_mask * (running <= visible_counts[0, 0]).astype(jnp.int32)).astype(F32)
+    pad = lambda k: jnp.zeros((k,), F32)
+    small = jnp.concatenate(
+        [
+            ln1_gain, ln1_bias, ln2_gain, ln2_bias,
+            out_bias, fc2_bias, pad(64),
+            qkv_bias, pad(32),
+            fc1_bias,
+            visible, pad(256),
+        ]
+    ).reshape(8, 128)
+    tgt, ctx, dx, gq, go, g1, g2, sg = run_layer(
+        n, tokens, context_cot, lengths, small, qkv_weight, out_weight, fc1_weight, fc2_weight, VIS_DEV
+    )
+
+    def own(k):
+        return lax.dynamic_slice(sg[k], (R * f,), (R,))
+
+    gbq = lax.dynamic_slice(sg[6:9].reshape(-1), (3 * R * f,), (3 * R,))
+    gb1 = lax.dynamic_slice(sg[9:13].reshape(-1), (4 * R * f,), (4 * R,))
+    return (tgt, ctx, dx, own(0), own(1), gq, gbq, go, own(4), own(2), own(3), g1, gb1, g2, own(5))
 
 
 def layer_norm(inputs, scale_vec, shift_vec):
@@ -184,7 +1237,7 @@
     return (result, middle, second, hidden, activated)
 
 
-def on_device(
+def gathered_device(
     tokens,
     lengths,
     visibility_mask,
@@ -409,45 +1462,23 @@
     )
 
 
+def per_device(tokens, *rest):
+    n, group = lax.axis_size("dp"), lax.axis_size("fsdp")
+    out_rows = rest[7].shape[0]
+    fits = group == 4 and n == 8 and out_rows * group == 128
+    return (on_device if fits else gathered_device)(tokens, *rest)
+
+
 def solution(mesh):
+    both = ("dp", "fsdp")
+    vec, mat = P(both), P(both, None)
     return jax.shard_map(
-        on_device,
+        per_device,
         mesh=mesh,
         in_specs=(
-            P(("dp", "fsdp"), None),
-            P("dp", None),
-            P(("dp", "fsdp")),
-            P("dp", "fsdp"),
-            P(("dp", "fsdp")),
-            P(("dp", "fsdp")),
-            P(("dp", "fsdp"), None),
-            P(("dp", "fsdp")),
-            P(("dp", "fsdp"), None),
-            P(("dp", "fsdp")),
-            P(("dp", "fsdp")),
-            P(("dp", "fsdp")),
-            P(("dp", "fsdp"), None),
-            P(("dp", "fsdp")),
-            P(("dp", "fsdp"), None),
-            P(("dp", "fsdp")),
-            P(("dp", "fsdp"), None),
+            mat, P("dp", None), vec, P("dp", "fsdp"), vec, vec, mat, vec, mat, vec, vec, vec,
+            mat, vec, mat, vec, mat,
         ),
-        out_specs=(
-            P(("dp", "fsdp"), None),
-            P(("dp", "fsdp"), None),
-            P(("dp", "fsdp"), None),
-            P(("dp", "fsdp")),
-            P(("dp", "fsdp")),
-            P(("dp", "fsdp"), None),
-            P(("dp", "fsdp")),
-            P(("dp", "fsdp"), None),
-            P(("dp", "fsdp")),
-            P(("dp", "fsdp")),
-            P(("dp", "fsdp")),
-            P(("dp", "fsdp"), None),
-            P(("dp", "fsdp")),
-            P(("dp", "fsdp"), None),
-            P(("dp", "fsdp")),
-        ),
+        out_specs=(mat, mat, mat, vec, vec, mat, vec, mat, vec, vec, vec, mat, vec, mat, vec),
         check_vma=False,
     )

time: 1110 us -> 154 us (0.14)
  waiting for transfers between devices: 731 us -> 0 us
  blocking collectives: 148 us -> 0 us
  Pallas kernels: 0 us -> 138 us
  matrix products: 115 us -> 0 us
  local copies, waits for them, and re-layouts: 47 us -> 14.2 us
  other arithmetic: 26.5 us -> 0.42 us
  between operations: 16.6 us -> 1.4 us
  starting transfers between devices: 14.8 us -> 0 us
    reduce_scatter x6 -> x0, waiting for transfers between devices: 565 us -> none  [the longest x1 187 us: on_device(): lax.psum_scatter(grad_list[10], ('dp', 'fsdp'), scatter_dimension=0, tile...]
    all_gather x6 -> x0, waiting for transfers between devices: 144 us -> none  [the longest x1 71 us: on_device(): lax.all_gather(shards[10], ('dp', 'fsdp'), axis=0, tiled=True)]
    pallas_call x0 -> x1, Pallas kernels: none -> 138 us  [run_layer(): pl.pallas_call(functools.partial(layer_kernel, (n, D, FF, T, V), names),...]
    dot_general x22 -> x0, matrix products: 104 us -> none  [the longest x2 25.5 us: finish(): jnp.dot(activated, weights[10], preferred_element_type=jnp.float32)]
    unnamed x2 -> x0, blocking collectives: 85.6 us -> none
    all_gather x4 -> x0, blocking collectives: 62.8 us -> none  [the longest x1 41.1 us: on_device(): lax.all_gather(shards[9], ('dp', 'fsdp'), axis=0, tiled=True)]
    all_to_all x4 -> x0, waiting for transfers between devices: 21.2 us -> none  [the longest x1 11 us: on_device(): lax.all_to_all(send_cot, 'fsdp', split_axis=0, concat_axis=0, tiled=True)]
    gather x14 -> x0, local copies, waits for them, and re-layouts: 14.7 us -> none  [the longest x1 1.5 us: on_device(): cos_home, sin_home = rope_tables(jnp.take(places, home_rows))]
  transfers between devices with their start and end apart: 16 -> 0, of which waited for: 10 -> 0; matrix products, arithmetic and copies ran while one was open for 15% -> 0% of each run, Pallas kernels for 0% -> 0%
where the time goes in v2:
time: 154 us
  Pallas kernels  138 us (90%)
  local copies, waits for them, and re-layouts  14.2 us (9%)
    pallas_call x1, Pallas kernels, run_layer(): pl.pallas_call(functools.partial(layer_kernel, (n, D, FF, T, V), names),...  138 us
    unnamed x39, local copies, waits for them, and re-layouts  9.5 us

profile of v2, /device:TPU:0, one launch (start us, length us, event | category | flops | bytes accessed | tf_op | source)
XLA Modules:
  0.0 153.7 jit_solution(15170895675480181468)
XLA Ops:
  0.6 0.0 copy-start.7
  0.7 0.7 copy-done.7
  1.3 0.3 reduce-window.9
  1.6 0.1 slice.31
  1.7 0.1 slice_reduce_fusion
  2.5 0.1 fusion
  2.6 0.0 copy-start.15
  2.6 0.0 copy-start.11
  2.6 0.0 copy-start.12
  2.6 0.0 copy-start.13
  2.6 0.0 copy-start.14
  2.6 0.0 copy-start.8
  2.7 0.0 copy-start.9
  2.7 0.0 copy-start.10
  2.7 0.6 copy-done.15
  3.2 0.0 copy-done.11
  3.3 0.0 copy-done.12
  3.3 0.0 copy-done.13
  3.3 0.0 copy-done.14
  3.3 0.0 copy-done.8
  3.3 0.0 copy-done.9
  3.3 0.0 copy-done.10
  3.4 0.7 concatenate.3
  4.0 137.7 %layer.1 = (bf16[256,1024]{1,0:T(8,128)(2,1)}, bf16[256,1024]{1,0:T(8,128)(2,1)}, bf16[256,1024]{1,0:T(8,128)(2,1)}, f32[32,3072]{1,0:T(8,128)}, f32[32,1024]{1,...) custom-call(s32[1,6]{1,0:T(1,128)} %refs_0_.1, bf16[256,1024]{1,0:T(8,128)(2,1)} %refs_1_.1, ...), custom_call_target="tpu_custom_call" | custom-call | tf_op jit(solution)/shard_map/layer/pallas_call | solution.py:1027
  141.7 0.9 fusion.7
  142.7 0.6 fusion.5
  143.2 0.6 fusion.3
  143.8 0.0 copy-start.6
  143.8 0.6 fusion.1
  144.4 0.1 copy-done.6
  144.5 0.6 dynamic_slice.40
  145.1 0.6 dynamic_slice.47
  145.7 0.0 copy-start.3
  145.7 1.9 %copy.41 = bf16[256,1024]{1,0:T(8,128)(2,1)} copy(bf16[256,1024]{1,0:T(8,128)(2,1)} %get-tuple-element.58) | data formatting | bytes 1048576
  147.6 0.0 copy-done.3
  147.6 0.0 copy-start.2
  147.6 0.8 copy.42
  148.4 0.4 copy-done.2
  148.9 0.0 copy-start.4
  148.9 0.8 copy.43
  149.7 0.4 copy-done.4
  150.1 0.7 copy.44
  150.8 0.2 copy-done.5
  151.1 0.7 copy.45
  151.7 0.0 copy-done.1
  151.7 0.8 copy.46
  152.5 0.4 copy-done
  152.9 0.8 copy.47
  (9 shorter events, 0.1 us)
Async XLA Ops:
  0.6 0.7 copy-start.7
  2.6 0.7 copy-start.15
  2.6 0.7 copy-start.11
  2.6 0.7 copy-start.12
  2.6 0.7 copy-start.13
  2.6 0.7 copy-start.14
  2.6 0.7 copy-start.8
  2.7 0.7 copy-start.9
  2.7 0.7 copy-start.10
  143.8 0.7 copy-start.6
  145.7 1.9 %copy-start.3 = (bf16[256,1024]{1,0:T(8,128)(2,1)S(1)}, bf16[256,1024]{1,0:T(8,128)(2,1)}, u32[]{:S(2)}) copy-start(bf16[256,1024]{1,0:T(8,128)(2,1)} %get-tuple-element.59) | copy-start | bytes 1572868
  147.6 1.2 copy-start.2
  148.9 1.2 copy-start.4
  150.1 1.0 copy-start.5
  150.1 1.7 %copy-start.1 = (f32[32,4096]{1,0:T(8,128)S(1)}, f32[32,4096]{1,0:T(8,128)}, u32[]{:S(2)}) copy-start(f32[32,4096]{1,0:T(8,128)} %get-tuple-element.69) | copy-start | bytes 1572868
  151.7 1.2 copy-start

commit v3 on v2

--- a/solution.py
+++ b/solution.py
@@ -91,7 +91,7 @@
     return row, seg
 
 
-ALIASES = dict(N2="N1", PT="N1", D2="w2_v", D1="w1_v", DOo="wo_v", DQo="wqkv_v")
+ALIASES = dict(N2="N1", PT="N1", D2="w2_v", DOo="wo_v")
 
 
 class Sems:
@@ -166,7 +166,7 @@
             (g.wqkv, g.wqkv_v),
             (g.w1, g.w1_v),
             (g.wo, g.wo_v),
-            (g.small, g.small_v),
+            (g.mask, g.mask_v),
             (g.tok, g.TA.at[f]),
             (g.w2, g.w2_v),
             (g.cot, g.CA.at[f]),
@@ -176,6 +176,10 @@
         c = pltpu.make_async_copy(src, dst, lsem.at[i])
         c.start()
         loads[i] = c
+    vectors = []
+    for k in range(8):
+        vectors.append(pltpu.make_async_copy(given["in%d" % k], given["v%d" % k], lsem.at[8 + k]))
+        vectors[k].start()
 
     barrier = pltpu.get_barrier_semaphore()
     for to in (to1, to2, to3, {"dp": right}, {"dp": left}):
@@ -189,8 +193,28 @@
         for t in range(3):
             g.sq[j, :, C * t : C * t + C] = g.wqkv_v[:, D * t + C * j : D * t + C * j + C].astype(BF)
     AQ[p, pl.ds(pl.multiple_of(R * f, R), R), :] = g.sq[f]
+    for c in vectors:
+        c.wait()
     loads[3].wait()
-    AS[p, f] = g.small_v[...]
+    SV = g.small_v
+    SV[...] = jnp.zeros(SV.shape, F32)
+    for k in range(8):
+        row, at = ((0, R * k), (1, R * (k - 4)), (2, 0), (3, 0))[0 if k < 4 else 1 if k < 6 else k - 4]
+        value = given["v%d" % k][...]
+        width = value.shape[1]
+        wide = value if width == 128 else jnp.concatenate([value, jnp.zeros((1, 128 - width), F32)], axis=1)
+        SV[row : row + 1, :] += wide if at == 0 else pltpu.roll(wide, at, 1)
+    mask = g.mask_v[...].astype(F32)
+    below = lax.broadcasted_iota(jnp.int32, (128, 128), 0) <= lax.broadcasted_iota(jnp.int32, (128, 128), 1)
+    tri = jnp.where(below, 1.0, 0.0).astype(BF)
+    count = g.counts[0, 0].astype(F32)
+    before = jnp.zeros((1, 1), F32)
+    for k in range(2):
+        ones = mask[:, 128 * k : 128 * k + 128]
+        running = dot(jnp.broadcast_to(ones, (8, 128)).astype(BF), tri)[0:1, :] + before
+        SV[4 + k : 5 + k, :] = jnp.where(running <= count, ones, 0.0)
+        before = before + jnp.sum(ones, axis=1, keepdims=True)
+    AS[p, f] = SV[...]
     loads[5].wait()
     A2[p] = g.w2_v[...].astype(BF)
     loads[2].wait()
@@ -782,11 +806,7 @@
 
     def fc1_grad_done():
         received(st.e1)
-        for j in range(NF):
-            for t in range(n):
-                at = HC * (NF * t + j)
-                g.D1[:, at : at + HC] = F1[j, :, HC * t : HC * t + HC].astype(F32)
-        store(g.D1, g.g1_o, 5)
+        store(F1, g.g1_o, 5)
 
     def out_grad_done():
         go_ring.finish()
@@ -802,10 +822,7 @@
 
     def qkv_grad_done():
         received(st.eq)
-        for j in range(NF):
-            for t in range(3):
-                g.DQo[:, D * t + C * j : D * t + C * j + C] = FQ[j, :, C * t : C * t + C].astype(F32)
-        store(g.DQo, g.gq_o, 7)
+        store(FQ, g.gq_o, 7)
 
     def small_grad_trade():
         gs_ring.finish()
@@ -964,7 +981,7 @@
         c.wait_send()
 
 
-def run_layer(n, tokens, cot, lengths, small, wqkv, wo, w1, w2, V):
+def run_layer(n, tokens, cot, lengths, mask, counts, vectors, wqkv, wo, w1, w2, V):
     T, D = tokens.shape
     NF = 4
     FF = w1.shape[1]
@@ -1011,23 +1028,26 @@
         SG=vm((NF, 16, 128), F), SGo=vm((16, 128), F),
         E1=vm((NF, R, HF), B), F1=vm((NF, R, HF), B), EQ=vm((NF, R, 3 * C), B), FQ=vm((NF, R, 3 * C), B),
         send_sems=pltpu.SemaphoreType.DMA((200,)), recv_sems=pltpu.SemaphoreType.DMA((200,)),
-        local_sems=pltpu.SemaphoreType.DMA((16,)),
+        local_sems=pltpu.SemaphoreType.DMA((16,)), mask_v=vm((1, T), jnp.int32),
     )
     arr = jax.ShapeDtypeStruct
     ins = dict(
-        lengths=lengths, tok=tokens, cot=cot, small=small, wqkv=wqkv, wo=wo, w1=w1, w2=w2,
-        trig=jnp.asarray(trig_table()),
-    )
+        lengths=lengths, counts=counts, tok=tokens, cot=cot, mask=mask.reshape(1, T), wqkv=wqkv, wo=wo,
+        w1=w1, w2=w2, trig=jnp.asarray(trig_table()),
+    )
+    for k, v in enumerate(vectors):
+        ins["in%d" % k] = v.reshape(1, -1)
+        scratch["v%d" % k] = vm((1, v.shape[0]), F)
     outs = dict(
-        tgt_o=arr((T, D), B), ctx_o=arr((T, D), B), dx_o=arr((T, D), B), gq_o=arr((R, 3 * D), F),
-        go_o=arr((R, D), F), g1_o=arr((R, FF), F), g2_o=arr((HC, D), F), sg_o=arr((16, 128), F),
+        tgt_o=arr((T, D), B), ctx_o=arr((T, D), B), dx_o=arr((T, D), B), gq_o=arr((NF, R, 3 * C), B),
+        go_o=arr((R, D), F), g1_o=arr((NF, R, HF), B), g2_o=arr((HC, D), F), sg_o=arr((16, 128), F),
     )
     names = [*ins, *outs, *scratch]
     any_spec = pl.BlockSpec(memory_space=pl.ANY)
     return pl.pallas_call(
         functools.partial(layer_kernel, (n, D, FF, T, V), names),
         out_shape=list(outs.values()),
-        in_specs=[pl.BlockSpec(memory_space=pltpu.SMEM)] + [any_spec] * 8,
+        in_specs=[pl.BlockSpec(memory_space=pltpu.SMEM)] * 2 + [any_spec] * (len(ins) - 2),
         out_specs=[any_spec] * 8,
         scratch_shapes=list(scratch.values()),
         compiler_params=pltpu.CompilerParams(
@@ -1037,35 +1057,98 @@
     )(*ins.values())
 
 
+def outputs_kernel(dims, count, *refs):
+    n, R, C, HC = dims
+    NF = 4
+    f = lax.axis_index("fsdp")
+    tgt, ctx, dx, gq, go, g1, g2, sg = refs[:8]
+    tgt_o, ctx_o, dx_o, gq_o, go_o, g1_o, g2_o = refs[8:15]
+    vec_o = refs[15:23]
+    bufs = refs[23:31]
+    gq_w, g1_w, sem_in, sem_out = refs[31:]
+    loads = []
+    for k, (src, dst) in enumerate(zip((gq, g1, sg, g2, tgt, ctx, dx, go), bufs)):
+        c = pltpu.make_async_copy(src, dst, sem_in.at[k])
+        c.start()
+        loads.append(c)
+    stores = []
+
+    def store(src, dst):
+        c = pltpu.make_async_copy(src, dst, sem_out.at[len(stores)])
+        c.start()
+        stores.append(c)
+
+    D = NF * C
+    loads[0].wait()
+    for j in range(NF):
+        for t in range(3):
+            gq_w[:, D * t + C * j : D * t + C * j + C] = bufs[0][j, :, C * t : C * t + C].astype(F32)
+    store(gq_w, gq_o)
+    loads[1].wait()
+    for j in range(NF):
+        for t in range(n):
+            at = HC * (NF * t + j)
+            g1_w[:, at : at + HC] = bufs[1][j, :, HC * t : HC * t + HC].astype(F32)
+    store(g1_w, g1_o)
+    for k, out in enumerate((g2_o, tgt_o, ctx_o, dx_o, go_o)):
+        loads[3 + k].wait()
+        store(bufs[3 + k], out)
+    loads[2].wait()
+    small = bufs[2]
+    for k in range(6):
+        vec_o[k][...] = pltpu.roll(small[k : k + 1, :], lax.rem(128 - R * f, 128), 1)[:, :R]
+    rows = jnp.concatenate([small[6 + t : 7 + t, :] for t in range(3)], axis=1)
+    vec_o[6][...] = pltpu.roll(rows, lax.rem(384 - 3 * R * f, 384), 1)[:, : 3 * R]
+    mine = jnp.zeros((1, 128), F32)
+    for j in range(NF):
+        mine = jnp.where(f == j, small[9 + j : 10 + j, :], mine)
+    vec_o[7][...] = mine
+    for c in stores:
+        c.wait()
+
+
+def write_outputs(n, parts, R, D, FF, HC):
+    NF = 4
+    C = D // NF
+    tgt = parts[0]
+    arr = jax.ShapeDtypeStruct
+    any_spec = pl.BlockSpec(memory_space=pl.ANY)
+    order = [parts[k] for k in (3, 5, 7, 6, 0, 1, 2, 4)]
+    big = [
+        arr(tgt.shape, BF), arr(tgt.shape, BF), arr(tgt.shape, BF),
+        arr((R, 3 * D), F32), arr((R, D), F32), arr((R, FF), F32), arr((HC, D), F32),
+    ]
+    small = [arr((1, w), F32) for w in (R,) * 6 + (3 * R, 4 * R)]
+    return pl.pallas_call(
+        functools.partial(outputs_kernel, (n, R, C, HC), 8),
+        out_shape=big + small,
+        in_specs=[any_spec] * 8,
+        out_specs=[any_spec] * 7 + [pl.BlockSpec(memory_space=pltpu.VMEM)] * 8,
+        scratch_shapes=[pltpu.VMEM(a.shape, a.dtype) for a in order]
+        + [
+            pltpu.VMEM((R, 3 * D), F32), pltpu.VMEM((R, FF), F32),
+            pltpu.SemaphoreType.DMA((8,)), pltpu.SemaphoreType.DMA((8,)),
+        ],
+        name="outputs",
+    )(*parts)
+
+
 def on_device(
     tokens, lengths, visibility_mask, visible_counts, ln1_gain, ln1_bias, qkv_weight, qkv_bias,
     out_weight, out_bias, ln2_gain, ln2_bias, fc1_weight, fc1_bias, fc2_weight, fc2_bias, context_cot,
 ):
     n = lax.axis_size("dp")
-    f = lax.axis_index("fsdp")
-    R = ln1_gain.shape[0]
-    running = jnp.cumsum(visibility_mask)
-    visible = (visibility_mask * (running <= visible_counts[0, 0]).astype(jnp.int32)).astype(F32)
-    pad = lambda k: jnp.zeros((k,), F32)
-    small = jnp.concatenate(
-        [
-            ln1_gain, ln1_bias, ln2_gain, ln2_bias,
-            out_bias, fc2_bias, pad(64),
-            qkv_bias, pad(32),
-            fc1_bias,
-            visible, pad(256),
-        ]
-    ).reshape(8, 128)
-    tgt, ctx, dx, gq, go, g1, g2, sg = run_layer(
-        n, tokens, context_cot, lengths, small, qkv_weight, out_weight, fc1_weight, fc2_weight, VIS_DEV
-    )
-
-    def own(k):
-        return lax.dynamic_slice(sg[k], (R * f,), (R,))
-
-    gbq = lax.dynamic_slice(sg[6:9].reshape(-1), (3 * R * f,), (3 * R,))
-    gb1 = lax.dynamic_slice(sg[9:13].reshape(-1), (4 * R * f,), (4 * R,))
-    return (tgt, ctx, dx, own(0), own(1), gq, gbq, go, own(4), own(2), own(3), g1, gb1, g2, own(5))
+    R, D = out_weight.shape
+    vectors = (ln1_gain, ln1_bias, ln2_gain, ln2_bias, out_bias, fc2_bias, qkv_bias, fc1_bias)
+    parts = run_layer(
+        n, tokens, context_cot, lengths, visibility_mask, visible_counts, vectors,
+        qkv_weight, out_weight, fc1_weight, fc2_weight, VIS_DEV,
+    )
+    tgt, ctx, dx, gq, go, g1, g2, *small = write_outputs(
+        n, parts, R, D, fc1_weight.shape[1], fc2_weight.shape[0]
+    )
+    gg1, gb1, gg2, gb2, gbo, gc2, gbq, gc1 = [v.reshape(-1) for v in small]
+    return (tgt, ctx, dx, gg1, gb1, gq, gbq, go, gbo, gg2, gb2, g1, gc1, g2, gc2)
 
 
 def layer_norm(inputs, scale_vec, shift_vec):

time: 154 us -> 143 us (0.929)
  local copies, waits for them, and re-layouts: 14.2 us -> 0 us
  Pallas kernels: 138 us -> 141 us
    unnamed x39 -> x0, local copies, waits for them, and re-layouts: 9.5 us -> none
    pallas_call x0 -> x1, Pallas kernels: none -> 3.33 us  [write_outputs(): pl.pallas_call(functools.partial(outputs_kernel, (n, R, C, HC), 8), out_s...]
    dynamic_slice x5 -> x0, local copies, waits for them, and re-layouts: 2.92 us -> none  [the longest x3 1.75 us: own(): return lax.dynamic_slice(sg[k], (R * f,), (R,))]
where the time goes in v3:
time: 143 us
  Pallas kernels  141 us (99%)
  between operations  1.51 us (1%)
    pallas_call x1, Pallas kernels, run_layer(): pl.pallas_call(functools.partial(layer_kernel, (n, D, FF, T, V), names),...  138 us
    pallas_call x1, Pallas kernels, write_outputs(): pl.pallas_call(functools.partial(outputs_kernel, (n, R, C, HC), 8), out_s...  3.33 us

profile of v3, /device:TPU:0, one launch (start us, length us, event | category | flops | bytes accessed | tf_op | source)
XLA Modules:
  0.0 142.7 jit_solution(17590361188583556744)
XLA Ops:
  1.3 137.9 %layer.1 = (bf16[256,1024]{1,0:T(8,128)(2,1)}, bf16[256,1024]{1,0:T(8,128)(2,1)}, bf16[256,1024]{1,0:T(8,128)(2,1)}, bf16[4,32,768]{2,1,0:T(8,128)(2,1)}, f32[32...) custom-call(s32[1,6]{1,0:T(1,128)} %refs_0_.1, ...), custom_call_target="tpu_custom_call" | custom-call | tf_op jit(solution)/shard_map/layer/pallas_call | solution.py:1047
  139.2 3.3 %outputs.1 = (bf16[256,1024]{1,0:T(8,128)(2,1)}, bf16[256,1024]{1,0:T(8,128)(2,1)}, bf16[256,1024]{1,0:T(8,128)(2,1)}, f32[32,3072]{1,0:T(8,128)}, f32[32,1024]{...) custom-call(bf16[256,1024]{1,0:T(8,128)(2,1)} %get-tuple-element.38., ...), custom_call_target="tpu_custom_call" | custom-call | tf_op jit(solution)/shard_map/outputs/pallas_call | solution.py:1122

commit v4 on v3

--- a/solution.py
+++ b/solution.py
@@ -91,17 +91,23 @@
     return row, seg
 
 
-ALIASES = dict(N2="N1", PT="N1", D2="w2_v", DOo="wo_v")
+ALIASES = dict(N2="N1", PT="N1", D2="w2_v", DOo="wo_v", X1B="GP")
 
 
 class Sems:
     def __init__(self, send, recv):
-        self.send, self.recv, self.used = send, recv, 0
+        self.send, self.recv, self.sends, self.recvs = send, recv, 0, 0
+
+    def take_send(self):
+        self.sends += 1
+        return self.send.at[self.sends - 1]
+
+    def take_recv(self):
+        self.recvs += 1
+        return self.recv.at[self.recvs - 1]
 
     def take(self):
-        at = self.used
-        self.used += 1
-        return self.send.at[at], self.recv.at[at]
+        return self.take_send(), self.take_recv()
 
 
 def layer_kernel(dims, names, *refs):
@@ -138,12 +144,20 @@
 
     pending = []
 
-    def remote(src, dst, to):
-        ss, rs = sems.take()
+    def launch(src, dst, ss, rs, to):
         c = pltpu.make_async_remote_copy(
             src_ref=src, dst_ref=dst, send_sem=ss, recv_sem=rs, device_id=to, device_id_type=MESH
         )
         c.start()
+        return c
+
+    def received(copies):
+        for c in copies:
+            c.wait_recv()
+
+    def remote(src, dst, to):
+        ss, rs = sems.take()
+        c = launch(src, dst, ss, rs, to)
         pending.append(c)
         return c, ss, rs
 
@@ -159,6 +173,10 @@
 
     to1, to2, to3 = {"fsdp": f1}, {"fsdp": f2}, {"fsdp": f3}
     peers = ((f1, to1), (f2, to2), (f3, to3))
+
+    barrier = pltpu.get_barrier_semaphore()
+    for to in (to1, to2, to3, {"dp": right}, {"dp": left}):
+        pl.semaphore_signal(barrier, inc=1, device_id=to, device_id_type=MESH)
 
     loads = {}
     for i, (src, dst) in enumerate(
@@ -181,52 +199,27 @@
         vectors.append(pltpu.make_async_copy(given["in%d" % k], given["v%d" % k], lsem.at[8 + k]))
         vectors[k].start()
 
-    barrier = pltpu.get_barrier_semaphore()
-    for to in (to1, to2, to3, {"dp": right}, {"dp": left}):
-        pl.semaphore_signal(barrier, inc=1, device_id=to, device_id_type=MESH)
-
     AS, AQ, WO, A1, A2 = g.AS, g.AQ, g.WO, g.A1, g.A2
     TA, CA = g.TA, g.CA
 
+    loads[5].wait()
+    A2[p] = g.w2_v[...].astype(BF)
     loads[0].wait()
     for j in range(NF):
         for t in range(3):
             g.sq[j, :, C * t : C * t + C] = g.wqkv_v[:, D * t + C * j : D * t + C * j + C].astype(BF)
     AQ[p, pl.ds(pl.multiple_of(R * f, R), R), :] = g.sq[f]
-    for c in vectors:
-        c.wait()
-    loads[3].wait()
-    SV = g.small_v
-    SV[...] = jnp.zeros(SV.shape, F32)
-    for k in range(8):
-        row, at = ((0, R * k), (1, R * (k - 4)), (2, 0), (3, 0))[0 if k < 4 else 1 if k < 6 else k - 4]
-        value = given["v%d" % k][...]
-        width = value.shape[1]
-        wide = value if width == 128 else jnp.concatenate([value, jnp.zeros((1, 128 - width), F32)], axis=1)
-        SV[row : row + 1, :] += wide if at == 0 else pltpu.roll(wide, at, 1)
-    mask = g.mask_v[...].astype(F32)
-    below = lax.broadcasted_iota(jnp.int32, (128, 128), 0) <= lax.broadcasted_iota(jnp.int32, (128, 128), 1)
-    tri = jnp.where(below, 1.0, 0.0).astype(BF)
-    count = g.counts[0, 0].astype(F32)
-    before = jnp.zeros((1, 1), F32)
-    for k in range(2):
-        ones = mask[:, 128 * k : 128 * k + 128]
-        running = dot(jnp.broadcast_to(ones, (8, 128)).astype(BF), tri)[0:1, :] + before
-        SV[4 + k : 5 + k, :] = jnp.where(running <= count, ones, 0.0)
-        before = before + jnp.sum(ones, axis=1, keepdims=True)
-    AS[p, f] = SV[...]
-    loads[5].wait()
-    A2[p] = g.w2_v[...].astype(BF)
     loads[2].wait()
     WO[p, f] = g.wo_v[...].astype(BF)
     pl.semaphore_wait(barrier, 5)
 
-    def scatter(src, dst):
-        got = []
+    def scatter(src, dst, three):
+        ss, rs = sems.take()
         for fj, to in peers:
-            _, ss, rs = remote(src(fj), dst(f), to)
-            got.append(arrival(dst(fj), ss, rs, to))
-        return got
+            launch(src(fj), dst(f), ss, rs, to)
+        got = arrival(three, ss, rs, to1)
+        pending.append(got)
+        return (got,)
 
     class AllGather4:
         def __init__(self, slot):
@@ -270,86 +263,89 @@
             return self.part[f].astype(F32) + self.r1[0].astype(F32) + self.r2[...].astype(F32)
 
     class RingGather:
-        def __init__(self, view, rows):
-            self.view, self.rows = view, rows
-            self.arrivals = []
+        def __init__(self, view, pair, rows):
+            self.view, self.pair, self.rows = view, pair, rows
+            self.before, self.flight = (), None
+            self.ss = sems.take_send()
+
+        def landed(self):
+            received(self.before)
+            self.before = ()
+            if self.flight is not None:
+                self.flight.wait_recv()
+                self.flight.wait_send()
+                self.flight = None
 
         def step(self, r):
-            for a in self.arrivals:
-                a.wait_recv()
-            self.arrivals = []
+            self.landed()
             h = self.rows // 2
             spans = ((0, self.rows), (0, self.rows)) if r < last else ((0, h), (h, h))
+            rs = sems.take_recv()
             for way, (s, c) in zip((1, -1), spans):
-                to, frm = ({"dp": right}, {"dp": left}) if way == 1 else ({"dp": left}, {"dp": right})
-                mine = self.view(idx(pos - way * r), s, c)
-                _, ss, rs = remote(mine, mine, to)
-                self.arrivals.append(arrival(self.view(idx(pos - way * (r + 1)), s, c), ss, rs, frm))
+                piece = self.view(idx(pos - way * r), s, c)
+                launch(piece, piece, self.ss, rs, {"dp": right if way == 1 else left})
+            both = self.pair if r < last else self.view(0, 0, self.rows)
+            self.flight = arrival(both, self.ss, rs, {"dp": left})
 
         def finish(self):
-            for a in self.arrivals:
-                a.wait_recv()
-            self.arrivals = []
-
-    def rows_view(ref, offset):
-        return lambda slot, s, c: ref.at[slot, pl.ds(offset + s, c), :]
-
-    h = RP // 2
-    q_ring = [RingGather(rows_view(AQ, 0), h), RingGather(rows_view(AQ, h), h)]
-    w1_ring = [RingGather(rows_view(A1, 0), h), RingGather(rows_view(A1, h), h)]
-    w2_ring = [RingGather(rows_view(A2, 0), HC // 2), RingGather(rows_view(A2, HC // 2), HC // 2)]
-    o_ring = RingGather(lambda slot, s, c: WO.at[slot, f, pl.ds(s, c), :], R)
-    s_ring = RingGather(lambda slot, s, c: AS.at[slot, pl.ds(s, c)], NF)
+            self.landed()
+
+    def row_rings(ref):
+        h = ref.shape[1] // 2
+
+        def ring(offset):
+            view = lambda slot, s, c: ref.at[slot, pl.ds(offset + s, c), :]
+            return RingGather(view, ref.at[pl.ds(0, 2), pl.ds(offset, h), :], h)
+
+        return [ring(0), ring(h)]
+
+    q_ring, w1_ring, w2_ring = row_rings(AQ), row_rings(A1), row_rings(A2)
+    o_ring = RingGather(lambda slot, s, c: WO.at[slot, f, pl.ds(s, c), :], WO.at[pl.ds(0, 2), f], R)
+    s_ring = RingGather(lambda slot, s, c: AS.at[slot, pl.ds(s, c)], AS.at[pl.ds(0, 2)], NF)
 
     class RingReduce:
         def __init__(self, grads, start, rows, st, rr, rl, wire=BF):
             self.G, self.o, self.rows, self.st, self.rr, self.rl = grads, start, rows, st, rr, rl
             self.wire = wire
-            self.arrivals = []
-
-        def piece(self, ref, slot, s, c):
-            return ref.at[slot, pl.ds(self.o + s, c), :]
+            self.flight = None
+            self.ss = sems.take_send()
+
+        def landed(self):
+            if self.flight is not None:
+                self.flight.wait_recv()
+                self.flight.wait_send()
+                self.flight = None
 
         def step(self, r):
-            for a in self.arrivals:
-                a.wait_recv()
-            self.arrivals = []
+            self.landed()
             o, rows = self.o, self.rows
             hh = rows // 2
+            whole = pl.ds(o, rows)
+            rs = sems.take_recv()
+            ways = ((1, self.rr, 0, {"dp": right}), (-1, self.rl, hh, {"dp": left}))
             if r == 0:
                 far = idx(pos + n // 2)
-                self.st[pl.ds(o, rows), :] = self.G[far, pl.ds(o, rows), :].astype(self.wire)
-                for buf, s, to, frm in (
-                    (self.rr, 0, {"dp": right}, {"dp": left}),
-                    (self.rl, hh, {"dp": left}, {"dp": right}),
-                ):
-                    dst = self.piece(buf, 0, s, hh)
-                    _, ss, rs = remote(self.st.at[pl.ds(o + s, hh), :], dst, to)
-                    self.arrivals.append(arrival(dst, ss, rs, frm))
+                self.st[whole, :] = self.G[far, whole, :].astype(self.wire)
+                for _, buf, s, to in ways:
+                    half = pl.ds(o + s, hh)
+                    launch(self.st.at[half, :], buf.at[0, half, :], self.ss, rs, to)
+                self.flight = arrival(self.st.at[whole, :], self.ss, rs, {"dp": left})
                 return
-            for way, buf, s, to, frm in (
-                (1, self.rr, 0, {"dp": right}, {"dp": left}),
-                (-1, self.rl, hh, {"dp": left}, {"dp": right}),
-            ):
+            for way, buf, s, to in ways:
                 c = idx(pos + way * (n // 2 - r))
                 if r == 1:
-                    other = hh - s
-                    buf[0, pl.ds(o + s, hh), :] = (
-                        buf[0, pl.ds(o + s, hh), :].astype(F32) + self.G[c, pl.ds(o + s, hh), :]
-                    ).astype(self.wire)
-                    buf[0, pl.ds(o + other, hh), :] = self.G[c, pl.ds(o + other, hh), :].astype(self.wire)
+                    half, other = pl.ds(o + s, hh), pl.ds(o + hh - s, hh)
+                    total = buf[0, half, :].astype(F32) + self.G[c, half, :]
+                    buf[0, half, :] = total.astype(self.wire)
+                    buf[0, other, :] = self.G[c, other, :].astype(self.wire)
                 else:
-                    buf[r - 1, pl.ds(o, rows), :] = (
-                        buf[r - 1, pl.ds(o, rows), :].astype(F32) + self.G[c, pl.ds(o, rows), :]
-                    ).astype(self.wire)
-                src, dst = self.piece(buf, r - 1, 0, rows), self.piece(buf, r, 0, rows)
-                _, ss, rs = remote(src, dst, to)
-                self.arrivals.append(arrival(dst, ss, rs, frm))
+                    total = buf[r - 1, whole, :].astype(F32) + self.G[c, whole, :]
+                    buf[r - 1, whole, :] = total.astype(self.wire)
+                launch(buf.at[r - 1, whole, :], buf.at[r, whole, :], self.ss, rs, to)
+            self.flight = arrival(self.rr.at[pl.ds(0, 2), whole, :], self.ss, rs, {"dp": left})
 
         def finish(self):
-            for a in self.arrivals:
-                a.wait_recv()
-            self.arrivals = []
+            self.landed()
 
         def total(self):
             o, rows = self.o, self.rows
@@ -391,10 +387,6 @@
         for r in rings:
             r.finish()
 
-    def received(copies):
-        for c in copies:
-            c.wait_recv()
-
     outs = []
 
     def store(src, dst, k):
@@ -406,10 +398,34 @@
         return VEC[k : k + 1, :]
 
     def start():
-        st.q = scatter(lambda j: g.sq.at[j], lambda j: AQ.at[p, pl.ds(pl.multiple_of(R * j, R), R), :])
-        st.s = scatter(lambda j: AS.at[p, f], lambda j: AS.at[p, j])
-        q_ring[0].arrivals = list(st.q)
-        s_ring.arrivals = st.s
+        part = lambda j: AQ.at[p, pl.ds(pl.multiple_of(R * j, R), R), :]
+        q_ring[0].before = scatter(lambda j: g.sq.at[j], part, AQ.at[0, pl.ds(0, 3 * R), :])
+
+    def small_start():
+        for c in vectors:
+            c.wait()
+        loads[3].wait()
+        SV = g.small_v
+        SV[...] = jnp.zeros(SV.shape, F32)
+        for k in range(8):
+            row, at = ((0, R * k), (1, R * (k - 4)), (2, 0), (3, 0))[0 if k < 4 else 1 if k < 6 else k - 4]
+            value = given["v%d" % k][...]
+            width = value.shape[1]
+            wide = value if width == 128 else jnp.concatenate([value, jnp.zeros((1, 128 - width), F32)], axis=1)
+            SV[row : row + 1, :] += wide if at == 0 else pltpu.roll(wide, at, 1)
+        mask = g.mask_v[...].astype(F32)
+        below = lax.broadcasted_iota(jnp.int32, (128, 128), 0) <= lax.broadcasted_iota(jnp.int32, (128, 128), 1)
+        tri = jnp.where(below, 1.0, 0.0).astype(BF)
+        count = g.counts[0, 0].astype(F32)
+        before = jnp.zeros((1, 1), F32)
+        for k in range(2):
+            ones = mask[:, 128 * k : 128 * k + 128]
+            running = dot(jnp.broadcast_to(ones, (8, 128)).astype(BF), tri)[0:1, :] + before
+            SV[4 + k : 5 + k, :] = jnp.where(running <= count, ones, 0.0)
+            before = before + jnp.sum(ones, axis=1, keepdims=True)
+        AS[p, f] = SV[...]
+        st.s = scatter(lambda j: AS.at[p, f], lambda j: AS.at[p, j], AS.at[0, pl.ds(0, 3)])
+        s_ring.before = st.s
 
     def cast_fc1():
         loads[1].wait()
@@ -418,8 +434,8 @@
                 at = HC * (NF * t + j)
                 g.s1[j, :, HC * t : HC * t + HC] = g.w1_v[:, at : at + HC].astype(BF)
         A1[p, pl.ds(pl.multiple_of(R * f, R), R), :] = g.s1[f]
-        st.w1 = scatter(lambda j: g.s1.at[j], lambda j: A1.at[p, pl.ds(pl.multiple_of(R * j, R), R), :])
-        w1_ring[0].arrivals = list(st.w1)
+        part = lambda j: A1.at[p, pl.ds(pl.multiple_of(R * j, R), R), :]
+        w1_ring[0].before = scatter(lambda j: g.s1.at[j], part, A1.at[0, pl.ds(0, 3 * R), :])
 
     def tokens_start():
         loads[4].wait()
@@ -468,9 +484,9 @@
         g.CS[...] = sum(dot(g.OH[...], g.trig_v[k]) for k in range(3))
 
     def visible():
-        if s_ring.arrivals is st.s:
-            received(st.s)
-            s_ring.arrivals = []
+        if s_ring.before:
+            received(s_ring.before)
+            s_ring.before = ()
         vis8 = jnp.concatenate([AS[p, j][4:6, :] for j in range(NF)], axis=0)
         above = lax.broadcasted_iota(jnp.int32, (128, 128), 0)
         tri = above <= lax.broadcasted_iota(jnp.int32, (128, 128), 1)
@@ -619,12 +635,17 @@
             GP[:, cols] = cdf + hid * (jnp.exp(-0.5 * hid * hid) * (1.0 / math.sqrt(2.0 * math.pi)))
 
     def outer(dst, lhs, rhs):
+        for k, cols in enumerate(blocks):
+            g.LT[cols, :] = lhs[:, cols].astype(F32).T.astype(BF)
+
         def one(k, _):
-            a = lhs[:, pl.ds(pl.multiple_of(128 * k, 128), 128)]
-            dst[k] = dot(a, rhs[...], TN)
+            rows = pl.ds(pl.multiple_of(512 * k, 512), 512)
+            for c in range(dst.shape[2] // 256):
+                cols = slice(256 * c, 256 * c + 256)
+                dst[pl.ds(4 * k, 4), :, cols] = dot(g.LT[rows, :], rhs[:, cols]).reshape(4, 128, 256)
             return 0
 
-        lax.fori_loop(0, n, one, 0)
+        lax.fori_loop(0, n // 4, one, 0)
 
     def put_grad(k, vrow):
         for q in range(n):
@@ -802,7 +823,7 @@
         for k, ring in enumerate(g1_ring):
             E1[2 * k : 2 * k + 2] = ring.total().astype(BF).reshape(2, R, HF)
         F1[f] = E1[f]
-        st.e1 = scatter(lambda j: E1.at[j], lambda j: F1.at[j])
+        st.e1 = scatter(lambda j: E1.at[j], lambda j: F1.at[j], F1.at[pl.ds(0, 3)])
 
     def fc1_grad_done():
         received(st.e1)
@@ -818,7 +839,7 @@
         for k, ring in enumerate(gq_ring):
             EQ[2 * k : 2 * k + 2] = ring.total().astype(BF).reshape(2, R, 3 * C)
         FQ[f] = EQ[f]
-        st.eq = scatter(lambda j: EQ.at[j], lambda j: FQ.at[j])
+        st.eq = scatter(lambda j: EQ.at[j], lambda j: FQ.at[j], FQ.at[pl.ds(0, 3)])
 
     def qkv_grad_done():
         received(st.eq)
@@ -827,7 +848,7 @@
     def small_grad_trade():
         gs_ring.finish()
         SG[f] = gs_ring.total()
-        st.sg = scatter(lambda j: SG.at[f], lambda j: SG.at[j])
+        st.sg = scatter(lambda j: SG.at[f], lambda j: SG.at[j], SG.at[pl.ds(0, 3)])
 
     def small_grad_done():
         received(st.sg)
@@ -835,144 +856,145 @@
         store(g.SGo, g.sg_o, 6)
 
     start()
+    small_start()
     cast_fc1()
     tokens_start()
     cot_start()
+    w2_ring[0].step(0)
     o_ring.step(0)
-    w2_ring[0].step(0)
     layout()
-    w2_ring[1].step(0)
-    o_ring.step(1)
     q_ring[0].step(0)
     q_ring[1].step(0)
     s_ring.step(0)
     visible()
     w1_ring[0].step(0)
-    o_ring.step(2)
+    o_ring.step(1)
     q_ring[0].step(1)
     q_ring[1].step(1)
     s_ring.step(1)
     w1_ring[0].step(1)
+    o_ring.step(2)
+    q_ring[0].step(2)
     st.tok.forward()
-    o_ring.step(3)
-    q_ring[0].step(2)
     q_ring[1].step(2)
     s_ring.step(2)
-    w1_ring[1].step(0)
-    wo_start()
     w1_ring[0].step(2)
+    o_ring.step(3)
     q_ring[0].step(3)
-    st.cot.forward()
     q_ring[1].step(3)
     s_ring.step(3)
+    st.cot.forward()
+    w1_ring[1].step(0)
+    w1_ring[0].step(3)
+    wo_start()
     select_cot()
-    w1_ring[1].step(1)
-    w1_ring[0].step(3)
-    w2_ring[0].step(1)
     small_vectors()
     first_norm()
+    w2_ring[1].step(0)
     project_half(0)
-    st.wo.forward()
-    w1_ring[1].step(2)
+    w1_ring[1].step(1)
     project_half(1)
+    select_rows()
     context_attention()
     w2_ring[1].step(1)
-    select_rows()
+    attend_target(2, 0)
+    w2_ring[0].step(1)
+    attend_target(1, 0)
+    w1_ring[1].step(2)
+    st.wo.forward()
+    attend_target(1, 1)
+    attend_target(0, 0)
+    st.ov.forward()
+    attend_target(0, 1)
     w2_ring[0].step(2)
-    attend_target(0, 0)
-    w1_ring[1].step(3)
-    attend_target(0, 1)
-    st.ov.forward()
-    attend_target(1, 0)
-    w2_ring[1].step(2)
     context_middle()
     transpose_attended()
+    oa_start(0)
+    attend_target(2, 1)
+    w1_ring[1].step(3)
+    attend_target(3, 0)
+    w2_ring[1].step(2)
+    attend_target(3, 1)
+    oa_start(1)
     w2_ring[0].step(3)
-    attend_target(1, 1)
-    oa_start(0)
     context_hidden()
     fc2_grad()
     g2_ring[0].step(0)
     g2_ring[1].step(0)
+    st.oa[0].forward()
     w2_ring[1].step(3)
-    attend_target(2, 0)
-    attend_target(2, 1)
     g2_ring[0].step(1)
     g2_ring[1].step(1)
-    st.oa[0].forward()
-    attend_target(3, 0)
+    st.oa[1].forward()
     hidden_grad()
     second_grad()
-    g2_ring[0].step(2)
     fc1_grad()
     g1_ring[0].step(0)
     g1_ring[1].step(0)
+    context_partial()
     st.n2.forward()
-    context_partial()
     target_middle(0)
+    target_middle(1)
+    g2_ring[0].step(2)
+    st.pf.forward()
     g2_ring[1].step(2)
-    attend_target(3, 1)
-    g2_ring[0].step(3)
-    oa_start(1)
+    target_hidden(0)
+    target_middle(2)
+    g1_ring[0].step(1)
+    target_middle(3)
     second_norm_back()
-    g1_ring[0].step(1)
-    st.pf.forward()
-    target_middle(1)
-    target_hidden(0)
+    target_hidden(2)
+    target_hidden(3)
+    context_result()
+    target_hidden(1)
     g1_ring[1].step(1)
-    target_hidden(1)
     target_out(0)
     target_out(1)
-    st.oa[1].forward()
     g2_ring[1].step(3)
-    target_middle(2)
+    st.dp.forward()
+    target_out(2)
+    target_out(3)
+    attended_grad()
     g1_ring[0].step(2)
-    st.dp.forward()
-    target_middle(3)
-    target_hidden(2)
-    g1_ring[1].step(2)
-    attended_grad()
     attention_back()
+    first_grad()
     qkv_grad()
     gq_ring[0].step(0)
     gq_ring[1].step(0)
     out_grad()
     go_ring.step(0)
+    qkv_bias_grad()
+    st.n1.forward()
+    st.co.forward()
+    st.pt.forward()
+    g1_ring[1].step(2)
+    home_context()
     g1_ring[0].step(3)
-    first_grad()
-    qkv_bias_grad()
-    context_result()
-    target_hidden(3)
-    target_out(2)
-    g1_ring[1].step(3)
-    st.n1.forward()
     gq_ring[0].step(1)
-    target_out(3)
-    fc2_grad_done()
+    first_norm_back()
+    gs_ring.step(0)
     gq_ring[1].step(1)
     go_ring.step(1)
-    st.co.forward()
-    st.pt.forward()
-    first_norm_back()
-    gs_ring.step(0)
-    home_context()
+    g1_ring[1].step(3)
+    gq_ring[0].step(2)
+    gs_ring.step(1)
+    gq_ring[1].step(2)
+    target_result()
+    go_ring.step(2)
+    st.dx.forward()
     fc1_grad_trade()
-    gq_ring[0].step(2)
-    gq_ring[1].step(2)
-    go_ring.step(2)
-    gs_ring.step(1)
+    home_grad()
     gq_ring[0].step(3)
+    gs_ring.step(2)
     gq_ring[1].step(3)
-    target_result()
+    fc1_grad_done()
     go_ring.step(3)
-    gs_ring.step(2)
-    st.dx.forward()
-    home_grad()
+    gs_ring.step(3)
+    g2_ring[0].step(3)
     qkv_grad_trade()
-    fc1_grad_done()
     out_grad_done()
-    gs_ring.step(3)
     small_grad_trade()
+    fc2_grad_done()
     qkv_grad_done()
     small_grad_done()
     for c in outs:
@@ -1022,13 +1044,13 @@
         PFr1=vm((2, V, D), B), PFxs=vm((V, D), B), PFr2=vm((V, D), B),
         DX1=vm((V, D), F), DP=vm((NF, V, D), B), OT=vm((n, NF, R, VP), B), DO=vm((VP, C), B),
         DPRE=vm((VP, 3 * C), B), CO=vm((NF, V, D), B), DX=vm((NF, V, D), B),
-        X1B=vm((T, D), F), X1H=vm((T, D), F), GT=vm((NF, T, HF), B),
+        X1H=vm((T, D), F), GT=vm((NF, T, HF), B),
         PTr1=vm((2, T, D), B), PTxs=vm((T, D), B), PTr2=vm((T, D), B),
         CH=vm((T, D), B), DXH=vm((T, D), B), TO=vm((T, D), B),
         SG=vm((NF, 16, 128), F), SGo=vm((16, 128), F),
         E1=vm((NF, R, HF), B), F1=vm((NF, R, HF), B), EQ=vm((NF, R, 3 * C), B), FQ=vm((NF, R, 3 * C), B),
-        send_sems=pltpu.SemaphoreType.DMA((200,)), recv_sems=pltpu.SemaphoreType.DMA((200,)),
-        local_sems=pltpu.SemaphoreType.DMA((16,)), mask_v=vm((1, T), jnp.int32),
+        send_sems=pltpu.SemaphoreType.DMA((61,)), recv_sems=pltpu.SemaphoreType.DMA((109,)),
+        local_sems=pltpu.SemaphoreType.DMA((16,)), mask_v=vm((1, T), jnp.int32), LT=vm((D, VP), B),
     )
     arr = jax.ShapeDtypeStruct
     ins = dict(

time: 143 us -> 135 us (0.944)
  Pallas kernels: 141 us -> 133 us
    pallas_call x1, Pallas kernels: 138 us -> 130 us  [run_layer(): pl.pallas_call(functools.partial(layer_kernel, (n, D, FF, T, V), names),...]
where the time goes in v4:
time: 135 us
  Pallas kernels  133 us (99%)
  between operations  1.51 us (1%)
    pallas_call x1, Pallas kernels, run_layer(): pl.pallas_call(functools.partial(layer_kernel, (n, D, FF, T, V), names),...  130 us
    pallas_call x1, Pallas kernels, write_outputs(): pl.pallas_call(functools.partial(outputs_kernel, (n, R, C, HC), 8), out_s...  3.33 us

profile of v4, /device:TPU:0, one launch (start us, length us, event | category | flops | bytes accessed | tf_op | source)
XLA Modules:
  0.0 134.8 jit_solution(12636321726710924194)
XLA Ops:
  1.3 130.0 %layer.1 = (bf16[256,1024]{1,0:T(8,128)(2,1)}, bf16[256,1024]{1,0:T(8,128)(2,1)}, bf16[256,1024]{1,0:T(8,128)(2,1)}, bf16[4,32,768]{2,1,0:T(8,128)(2,1)}, f32[32...) custom-call(s32[1,6]{1,0:T(1,128)} %refs_0_.1, ...), custom_call_target="tpu_custom_call" | custom-call | tf_op jit(solution)/shard_map/layer/pallas_call | solution.py:1069
  131.3 3.3 %outputs.1 = (bf16[256,1024]{1,0:T(8,128)(2,1)}, bf16[256,1024]{1,0:T(8,128)(2,1)}, bf16[256,1024]{1,0:T(8,128)(2,1)}, f32[32,3072]{1,0:T(8,128)}, f32[32,1024]{...) custom-call(bf16[256,1024]{1,0:T(8,128)(2,1)} %get-tuple-element.38., ...), custom_call_target="tpu_custom_call" | custom-call | tf_op jit(solution)/shard_map/outputs/pallas_call | solution.py:1144

commit v5 on v4

--- a/solution.py
+++ b/solution.py
@@ -96,18 +96,32 @@
 
 class Sems:
     def __init__(self, send, recv):
-        self.send, self.recv, self.sends, self.recvs = send, recv, 0, 0
+        self.send, self.recv = send, recv
+        self.sends = self.recvs = self.clock = 0
+        self.idle_sends, self.idle_recvs, self.waited = [], [], []
 
     def take_send(self):
+        if self.idle_sends:
+            return self.idle_sends.pop()
         self.sends += 1
         return self.send.at[self.sends - 1]
+
+    def give_send(self, sem):
+        self.idle_sends.append(sem)
 
     def take_recv(self):
         self.recvs += 1
         return self.recv.at[self.recvs - 1]
 
-    def take(self):
-        return self.take_send(), self.take_recv()
+    def ring_sent(self):
+        rs = self.idle_recvs.pop() if self.idle_recvs else self.take_recv()
+        self.clock += 1
+        return rs, self.clock
+
+    def ring_landed(self, sem, sent):
+        self.idle_recvs += [old for at, old in self.waited if at < sent]
+        self.waited = [(at, old) for at, old in self.waited if at >= sent]
+        self.waited.append((self.clock, sem))
 
 
 def layer_kernel(dims, names, *refs):
@@ -142,8 +156,6 @@
 
     right, left = idx(pos + 1), idx(pos - 1)
 
-    pending = []
-
     def launch(src, dst, ss, rs, to):
         c = pltpu.make_async_remote_copy(
             src_ref=src, dst_ref=dst, send_sem=ss, recv_sem=rs, device_id=to, device_id_type=MESH
@@ -151,20 +163,19 @@
         c.start()
         return c
 
+    def sent(copies):
+        for c in copies:
+            c.wait_send()
+            sems.give_send(c.src_sem)
+
     def received(copies):
         for c in copies:
             c.wait_recv()
+        sent(copies)
 
     def remote(src, dst, to):
-        ss, rs = sems.take()
-        c = launch(src, dst, ss, rs, to)
-        pending.append(c)
-        return c, ss, rs
-
-    def drain(*copies):
-        for c in copies:
-            pending[:] = [d for d in pending if d is not c]
-            c.wait_send()
+        ss, rs = sems.take_send(), sems.take_recv()
+        return launch(src, dst, ss, rs, to), ss, rs
 
     def arrival(dst, ss, rs, to):
         return pltpu.make_async_remote_copy(
@@ -214,50 +225,54 @@
     pl.semaphore_wait(barrier, 5)
 
     def scatter(src, dst, three):
-        ss, rs = sems.take()
+        ss, rs = sems.take_send(), sems.take_recv()
         for fj, to in peers:
             launch(src(fj), dst(f), ss, rs, to)
-        got = arrival(three, ss, rs, to1)
-        pending.append(got)
-        return (got,)
+        return (arrival(three, ss, rs, to1),)
 
     class AllGather4:
         def __init__(self, slot):
             self.slot = slot
-            _, ss, rs = remote(slot(f), slot(f), to2)
+            self.done = False
+            c, ss, rs = remote(slot(f), slot(f), to2)
+            d, sd, rd = remote(slot(f), slot(f), to1)
             self.across = arrival(slot(f2), ss, rs, to2)
-            _, ss, rs = remote(slot(f), slot(f), to1)
-            self.beside = arrival(slot(f1), ss, rs, to1)
+            self.beside = arrival(slot(f1), sd, rd, to1)
+            self.copies = [c, d]
 
         def forward(self):
-            self.done = False
             self.across.wait_recv()
-            _, ss, rs = remote(self.slot(f2), self.slot(f2), to1)
+            c, ss, rs = remote(self.slot(f2), self.slot(f2), to1)
             self.passed = arrival(self.slot(f3), ss, rs, to1)
+            self.copies.append(c)
 
         def finish(self):
             if not self.done:
                 self.done = True
                 self.beside.wait_recv()
                 self.passed.wait_recv()
+                sent(self.copies)
 
     class ReduceScatter4:
         def __init__(self, part, r1, xs, r2):
             self.part, self.r1, self.xs, self.r2 = part, r1, xs, r2
-            self.ca, ss, rs = remote(part.at[f3], r1.at[1], to1)
+            c, ss, rs = remote(part.at[f3], r1.at[1], to1)
+            d, sd, rd = remote(part.at[f1], r1.at[0], to1)
             self.other = arrival(r1.at[1], ss, rs, to1)
-            self.cb, ss, rs = remote(part.at[f1], r1.at[0], to1)
-            self.own = arrival(r1.at[0], ss, rs, to1)
+            self.own = arrival(r1.at[0], sd, rd, to1)
+            self.copies = [c, d]
 
         def forward(self):
             self.other.wait_recv()
             self.xs[...] = (self.part[f2].astype(F32) + self.r1[1].astype(F32)).astype(BF)
-            _, ss, rs = remote(self.xs, self.r2, to2)
+            c, ss, rs = remote(self.xs, self.r2, to2)
             self.across = arrival(self.r2, ss, rs, to2)
+            self.copies.append(c)
 
         def finish(self):
             self.own.wait_recv()
             self.across.wait_recv()
+            sent(self.copies)
 
         def total(self):
             return self.part[f].astype(F32) + self.r1[0].astype(F32) + self.r2[...].astype(F32)
@@ -266,26 +281,26 @@
         def __init__(self, view, pair, rows):
             self.view, self.pair, self.rows = view, pair, rows
             self.before, self.flight = (), None
-            self.ss = sems.take_send()
 
         def landed(self):
             received(self.before)
             self.before = ()
             if self.flight is not None:
-                self.flight.wait_recv()
-                self.flight.wait_send()
+                received([self.flight])
+                sems.ring_landed(self.flight.dst_sem, self.at)
                 self.flight = None
 
         def step(self, r):
             self.landed()
             h = self.rows // 2
             spans = ((0, self.rows), (0, self.rows)) if r < last else ((0, h), (h, h))
-            rs = sems.take_recv()
+            ss = sems.take_send()
+            rs, self.at = sems.ring_sent()
             for way, (s, c) in zip((1, -1), spans):
                 piece = self.view(idx(pos - way * r), s, c)
-                launch(piece, piece, self.ss, rs, {"dp": right if way == 1 else left})
+                launch(piece, piece, ss, rs, {"dp": right if way == 1 else left})
             both = self.pair if r < last else self.view(0, 0, self.rows)
-            self.flight = arrival(both, self.ss, rs, {"dp": left})
+            self.flight = arrival(both, ss, rs, {"dp": left})
 
         def finish(self):
             self.landed()
@@ -308,12 +323,11 @@
             self.G, self.o, self.rows, self.st, self.rr, self.rl = grads, start, rows, st, rr, rl
             self.wire = wire
             self.flight = None
-            self.ss = sems.take_send()
 
         def landed(self):
             if self.flight is not None:
-                self.flight.wait_recv()
-                self.flight.wait_send()
+                received([self.flight])
+                sems.ring_landed(self.flight.dst_sem, self.at)
                 self.flight = None
 
         def step(self, r):
@@ -321,15 +335,16 @@
             o, rows = self.o, self.rows
             hh = rows // 2
             whole = pl.ds(o, rows)
-            rs = sems.take_recv()
+            ss = sems.take_send()
+            rs, self.at = sems.ring_sent()
             ways = ((1, self.rr, 0, {"dp": right}), (-1, self.rl, hh, {"dp": left}))
             if r == 0:
                 far = idx(pos + n // 2)
                 self.st[whole, :] = self.G[far, whole, :].astype(self.wire)
                 for _, buf, s, to in ways:
                     half = pl.ds(o + s, hh)
-                    launch(self.st.at[half, :], buf.at[0, half, :], self.ss, rs, to)
-                self.flight = arrival(self.st.at[whole, :], self.ss, rs, {"dp": left})
+                    launch(self.st.at[half, :], buf.at[0, half, :], ss, rs, to)
+                self.flight = arrival(self.st.at[whole, :], ss, rs, {"dp": left})
                 return
             for way, buf, s, to in ways:
                 c = idx(pos + way * (n // 2 - r))
@@ -341,8 +356,8 @@
                 else:
                     total = buf[r - 1, whole, :].astype(F32) + self.G[c, whole, :]
                     buf[r - 1, whole, :] = total.astype(self.wire)
-                launch(buf.at[r - 1, whole, :], buf.at[r, whole, :], self.ss, rs, to)
-            self.flight = arrival(self.rr.at[pl.ds(0, 2), whole, :], self.ss, rs, {"dp": left})
+                launch(buf.at[r - 1, whole, :], buf.at[r, whole, :], ss, rs, to)
+            self.flight = arrival(self.rr.at[pl.ds(0, 2), whole, :], ss, rs, {"dp": left})
 
         def finish(self):
             self.landed()
@@ -745,7 +760,6 @@
             VG[q, 13:16, :] = jnp.zeros((3, 128), F32)
 
     def first_grad():
-        drain(st.n2.ca, st.n2.cb)
         for k, cols in enumerate(blocks):
             part = dot(DPRE[...], AQ[2 * k : 2 * k + 2].reshape(256, 3 * C), NT).astype(BF)
             PN[:, :, cols] = part.reshape(NF, V, 256)
@@ -856,151 +870,149 @@
         store(g.SGo, g.sg_o, 6)
 
     start()
+    o_ring.step(0)
+    w2_ring[0].step(0)
     small_start()
+    layout()
     cast_fc1()
+    w2_ring[1].step(0)
     tokens_start()
+    o_ring.step(1)
     cot_start()
-    w2_ring[0].step(0)
-    o_ring.step(0)
-    layout()
     q_ring[0].step(0)
+    visible()
+    s_ring.step(0)
     q_ring[1].step(0)
-    s_ring.step(0)
-    visible()
     w1_ring[0].step(0)
-    o_ring.step(1)
+    o_ring.step(2)
     q_ring[0].step(1)
+    s_ring.step(1)
     q_ring[1].step(1)
-    s_ring.step(1)
+    w1_ring[1].step(0)
+    o_ring.step(3)
+    st.tok.forward()
+    q_ring[0].step(2)
+    s_ring.step(2)
+    q_ring[1].step(2)
     w1_ring[0].step(1)
-    o_ring.step(2)
-    q_ring[0].step(2)
-    st.tok.forward()
-    q_ring[1].step(2)
-    s_ring.step(2)
+    wo_start()
+    w1_ring[1].step(1)
+    s_ring.step(3)
+    q_ring[0].step(3)
+    st.cot.forward()
+    q_ring[1].step(3)
+    select_cot()
+    w2_ring[0].step(1)
     w1_ring[0].step(2)
-    o_ring.step(3)
-    q_ring[0].step(3)
-    q_ring[1].step(3)
-    s_ring.step(3)
-    st.cot.forward()
-    w1_ring[1].step(0)
-    w1_ring[0].step(3)
-    wo_start()
-    select_cot()
     small_vectors()
     first_norm()
-    w2_ring[1].step(0)
+    select_rows()
+    w1_ring[1].step(2)
     project_half(0)
-    w1_ring[1].step(1)
     project_half(1)
-    select_rows()
     context_attention()
+    w1_ring[0].step(3)
+    st.wo.forward()
+    attend_target(3, 0)
     w2_ring[1].step(1)
+    attend_target(0, 0)
+    w1_ring[1].step(3)
+    attend_target(3, 1)
+    w2_ring[0].step(2)
+    st.ov.forward()
     attend_target(2, 0)
-    w2_ring[0].step(1)
-    attend_target(1, 0)
-    w1_ring[1].step(2)
-    st.wo.forward()
-    attend_target(1, 1)
-    attend_target(0, 0)
-    st.ov.forward()
-    attend_target(0, 1)
-    w2_ring[0].step(2)
+    attend_target(2, 1)
+    oa_start(1)
     context_middle()
-    transpose_attended()
-    oa_start(0)
-    attend_target(2, 1)
-    w1_ring[1].step(3)
-    attend_target(3, 0)
     w2_ring[1].step(2)
-    attend_target(3, 1)
-    oa_start(1)
-    w2_ring[0].step(3)
     context_hidden()
     fc2_grad()
+    g2_ring[1].step(0)
+    attend_target(1, 0)
+    w2_ring[0].step(3)
+    attend_target(1, 1)
+    transpose_attended()
+    w2_ring[1].step(3)
     g2_ring[0].step(0)
-    g2_ring[1].step(0)
-    st.oa[0].forward()
-    w2_ring[1].step(3)
-    g2_ring[0].step(1)
+    attend_target(0, 1)
+    oa_start(0)
+    st.oa[1].forward()
     g2_ring[1].step(1)
-    st.oa[1].forward()
     hidden_grad()
-    second_grad()
     fc1_grad()
     g1_ring[0].step(0)
+    context_partial()
+    g2_ring[0].step(1)
+    second_grad()
     g1_ring[1].step(0)
-    context_partial()
+    st.pf.forward()
     st.n2.forward()
+    g1_ring[0].step(1)
+    st.oa[0].forward()
     target_middle(0)
+    g2_ring[0].step(2)
+    target_hidden(0)
+    context_result()
+    target_out(0)
+    g1_ring[1].step(1)
     target_middle(1)
-    g2_ring[0].step(2)
-    st.pf.forward()
-    g2_ring[1].step(2)
-    target_hidden(0)
+    target_hidden(1)
+    second_norm_back()
+    g1_ring[0].step(2)
     target_middle(2)
-    g1_ring[0].step(1)
     target_middle(3)
-    second_norm_back()
+    st.co.forward()
     target_hidden(2)
+    target_out(2)
+    g2_ring[0].step(3)
+    home_context()
+    g1_ring[1].step(2)
+    st.dp.forward()
     target_hidden(3)
-    context_result()
-    target_hidden(1)
-    g1_ring[1].step(1)
-    target_out(0)
     target_out(1)
-    g2_ring[1].step(3)
-    st.dp.forward()
-    target_out(2)
+    attended_grad()
+    attention_back()
+    g1_ring[0].step(3)
+    first_grad()
     target_out(3)
-    attended_grad()
-    g1_ring[0].step(2)
-    attention_back()
-    first_grad()
     qkv_grad()
+    gq_ring[1].step(0)
+    st.n1.forward()
     gq_ring[0].step(0)
-    gq_ring[1].step(0)
+    qkv_bias_grad()
     out_grad()
-    go_ring.step(0)
-    qkv_bias_grad()
-    st.n1.forward()
-    st.co.forward()
+    g1_ring[1].step(3)
     st.pt.forward()
-    g1_ring[1].step(2)
-    home_context()
-    g1_ring[0].step(3)
-    gq_ring[0].step(1)
+    gq_ring[1].step(1)
     first_norm_back()
     gs_ring.step(0)
-    gq_ring[1].step(1)
+    gq_ring[0].step(1)
+    fc1_grad_trade()
+    go_ring.step(0)
+    g2_ring[1].step(2)
+    gq_ring[1].step(2)
+    gs_ring.step(1)
+    gq_ring[0].step(2)
+    target_result()
     go_ring.step(1)
-    g1_ring[1].step(3)
-    gq_ring[0].step(2)
-    gs_ring.step(1)
-    gq_ring[1].step(2)
-    target_result()
+    gq_ring[1].step(3)
+    gs_ring.step(2)
+    st.dx.forward()
+    gq_ring[0].step(3)
+    home_grad()
+    fc1_grad_done()
     go_ring.step(2)
-    st.dx.forward()
-    fc1_grad_trade()
-    home_grad()
-    gq_ring[0].step(3)
-    gs_ring.step(2)
-    gq_ring[1].step(3)
-    fc1_grad_done()
+    gs_ring.step(3)
+    g2_ring[1].step(3)
+    qkv_grad_trade()
     go_ring.step(3)
-    gs_ring.step(3)
-    g2_ring[0].step(3)
-    qkv_grad_trade()
-    out_grad_done()
     small_grad_trade()
     fc2_grad_done()
     qkv_grad_done()
     small_grad_done()
+    out_grad_done()
     for c in outs:
         c.wait()
-    for c in pending:
-        c.wait_send()
 
 
 def run_layer(n, tokens, cot, lengths, mask, counts, vectors, wqkv, wo, w1, w2, V):
@@ -1049,7 +1061,7 @@
         CH=vm((T, D), B), DXH=vm((T, D), B), TO=vm((T, D), B),
         SG=vm((NF, 16, 128), F), SGo=vm((16, 128), F),
         E1=vm((NF, R, HF), B), F1=vm((NF, R, HF), B), EQ=vm((NF, R, 3 * C), B), FQ=vm((NF, R, 3 * C), B),
-        send_sems=pltpu.SemaphoreType.DMA((61,)), recv_sems=pltpu.SemaphoreType.DMA((109,)),
+        send_sems=pltpu.SemaphoreType.DMA((16,)), recv_sems=pltpu.SemaphoreType.DMA((59,)),
         local_sems=pltpu.SemaphoreType.DMA((16,)), mask_v=vm((1, T), jnp.int32), LT=vm((D, VP), B),
     )
     arr = jax.ShapeDtypeStruct
@@ -1089,7 +1101,7 @@
     bufs = refs[23:31]
     gq_w, g1_w, sem_in, sem_out = refs[31:]
     loads = []
-    for k, (src, dst) in enumerate(zip((gq, g1, sg, g2, tgt, ctx, dx, go), bufs)):
+    for k, (src, dst) in enumerate(zip((g2, tgt, ctx, dx, go, gq, g1, sg), bufs)):
         c = pltpu.make_async_copy(src, dst, sem_in.at[k])
         c.start()
         loads.append(c)
@@ -1100,23 +1112,23 @@
         c.start()
         stores.append(c)
 
+    for k, out in enumerate((g2_o, tgt_o, ctx_o, dx_o, go_o)):
+        loads[k].wait()
+        store(bufs[k], out)
     D = NF * C
-    loads[0].wait()
+    loads[5].wait()
     for j in range(NF):
         for t in range(3):
-            gq_w[:, D * t + C * j : D * t + C * j + C] = bufs[0][j, :, C * t : C * t + C].astype(F32)
+            gq_w[:, D * t + C * j : D * t + C * j + C] = bufs[5][j, :, C * t : C * t + C].astype(F32)
     store(gq_w, gq_o)
-    loads[1].wait()
+    loads[6].wait()
     for j in range(NF):
         for t in range(n):
             at = HC * (NF * t + j)
-            g1_w[:, at : at + HC] = bufs[1][j, :, HC * t : HC * t + HC].astype(F32)
+            g1_w[:, at : at + HC] = bufs[6][j, :, HC * t : HC * t + HC].astype(F32)
     store(g1_w, g1_o)
-    for k, out in enumerate((g2_o, tgt_o, ctx_o, dx_o, go_o)):
-        loads[3 + k].wait()
-        store(bufs[3 + k], out)
-    loads[2].wait()
-    small = bufs[2]
+    loads[7].wait()
+    small = bufs[7]
     for k in range(6):
         vec_o[k][...] = pltpu.roll(small[k : k + 1, :], lax.rem(128 - R * f, 128), 1)[:, :R]
     rows = jnp.concatenate([small[6 + t : 7 + t, :] for t in range(3)], axis=1)
@@ -1135,7 +1147,7 @@
     tgt = parts[0]
     arr = jax.ShapeDtypeStruct
     any_spec = pl.BlockSpec(memory_space=pl.ANY)
-    order = [parts[k] for k in (3, 5, 7, 6, 0, 1, 2, 4)]
+    order = [parts[k] for k in (6, 0, 1, 2, 4, 3, 5, 7)]
     big = [
         arr(tgt.shape, BF), arr(tgt.shape, BF), arr(tgt.shape, BF),
         arr((R, 3 * D), F32), arr((R, D), F32), arr((R, FF), F32), arr((HC, D), F32),

time: 135 us -> 133 us (0.985)
  Pallas kernels: 133 us -> 131 us
    pallas_call x1, Pallas kernels: 130 us -> 128 us  [run_layer(): pl.pallas_call(functools.partial(layer_kernel, (n, D, FF, T, V), names),...]
where the time goes in v5:
time: 133 us
  Pallas kernels  131 us (98%)
  between operations  1.51 us (1%)
    pallas_call x1, Pallas kernels, run_layer(): pl.pallas_call(functools.partial(layer_kernel, (n, D, FF, T, V), names),...  128 us
    pallas_call x1, Pallas kernels, write_outputs(): pl.pallas_call(functools.partial(outputs_kernel, (n, R, C, HC), 8), out_s...  3.39 us

profile of v5, /device:TPU:0, one launch (start us, length us, event | category | flops | bytes accessed | tf_op | source)
XLA Modules:
  0.0 132.7 jit_solution(967836806941113831)
XLA Ops:
  1.3 127.8 %layer.1 = (bf16[256,1024]{1,0:T(8,128)(2,1)}, bf16[256,1024]{1,0:T(8,128)(2,1)}, bf16[256,1024]{1,0:T(8,128)(2,1)}, bf16[4,32,768]{2,1,0:T(8,128)(2,1)}, f32[32...) custom-call(s32[1,6]{1,0:T(1,128)} %refs_0_.1, ...), custom_call_target="tpu_custom_call" | custom-call | tf_op jit(solution)/shard_map/layer/pallas_call | solution.py:1081
  129.1 3.4 %outputs.1 = (bf16[256,1024]{1,0:T(8,128)(2,1)}, bf16[256,1024]{1,0:T(8,128)(2,1)}, bf16[256,1024]{1,0:T(8,128)(2,1)}, f32[32,3072]{1,0:T(8,128)}, f32[32,1024]{...) custom-call(bf16[256,1024]{1,0:T(8,128)(2,1)} %get-tuple-element.38., ...), custom_call_target="tpu_custom_call" | custom-call | tf_op jit(solution)/shard_map/outputs/pallas_call | solution.py:1156
